TPU v7x, 32 devices: a whole 2x2x4 slice. The times are simulated.
32 devices in a mesh: section: 2 (over x), dp: 16 (over z, y, core).
Axes of the slice: x: 2, y: 2, z: 4, core: 2. Of those that a mesh axis runs over, the one named last changes fastest.
Arguments:
- images: bfloat16 [64, 196, 768], P('dp'), may hold values from -6 to 6
- cotangent: bfloat16 [64, 196, 768], P('dp'), may hold values from -6 to 6
- w_qkv: bfloat16 [2, 768, 2304], P('section', 'dp'), may hold values from -0.21875 to 0.21875
- w_up: bfloat16 [2, 768, 3072], P('section', 'dp'), may hold values from -0.21875 to 0.21875
- w_proj: bfloat16 [2, 768, 768], P('section', 'dp'), may hold values from -1.75 to 1.75
- w_down: bfloat16 [2, 3072, 768], P('section', 'dp'), may hold values from -0.109375 to 0.109375
- ln_gain: float32 [2, 768], P('section'), may hold values from 0.1 to 1.9
- q_gain: float32 [2, 768], P('section'), may hold values from 0.1 to 1.9
- k_gain: float32 [2, 768], P('section'), may hold values from 0.1 to 1.9
Outputs:
- outputs: bfloat16 [2, 64, 196, 768], P('section', 'dp')
- input_grads: bfloat16 [2, 64, 196, 768], P('section', 'dp')
- grad_qkv: float32 [2, 768, 2304], P('section', 'dp')
- grad_up: float32 [2, 768, 3072], P('section', 'dp')
- grad_proj: float32 [2, 768, 768], P('section', 'dp')
- grad_down: float32 [2, 3072, 768], P('section', 'dp')
- grad_ln: float32 [2, 768], P('section')
- grad_q: float32 [2, 768], P('section')
- grad_k: float32 [2, 768], P('section')
All inputs are finite; a program needn't handle non-finite values.
Results may differ from a plain program's by a relative error of at most 0.017.
Values may be sent and summed in bfloat16 or wider, within the bound.
No kernel may reach another device: no remote copies, remote signals or barrier semaphores. Data moves between devices by JAX's collectives and lax.ppermute only.
A program may use at most 320 MiB of HBM per device.

v0:
```python
from functools import partial

import jax
import jax.numpy as jnp
from jax import lax
from jax.sharding import PartitionSpec as P

HEADS = 12
HEAD = 64
M = 2


EPSILON = 1e-06


def from_behind(value, axis, steps):
    count = lax.axis_size(axis)
    first, last = (max(0, -steps), min(count, count - steps))
    return lax.ppermute(value, axis, [(source, source + steps) for source in range(first, last)])


def layer_norm(values, gain):
    centred = values - jnp.mean(values, axis=-1, keepdims=True)
    spread = jnp.mean(centred * centred, axis=-1, keepdims=True)
    return centred * lax.rsqrt(spread + EPSILON) * gain


def head_norm(values, gain):
    shaped = values.reshape(values.shape[:-1] + (HEADS, HEAD))
    centred = shaped - jnp.mean(shaped, axis=-1, keepdims=True)
    spread = jnp.mean(centred * centred, axis=-1, keepdims=True)
    return (centred * lax.rsqrt(spread + EPSILON)).reshape(values.shape) * gain


def outer_sum(left, right):
    return lax.dot_general(
        left, right, (((0,), (0,)), ((), ())), preferred_element_type=jnp.float32
    )


def times_transpose(left, right):
    return lax.dot_general(
        left, right, (((1,), (1,)), ((), ())), preferred_element_type=jnp.float32
    )


def forward_parts(inputs, weights, gains):
    w_qkv, w_up, w_proj, w_down = weights
    ln_gain, q_gain, k_gain = gains
    count = inputs.shape[0]
    width = inputs.shape[2]
    flat = inputs.astype(jnp.float32).reshape(count * inputs.shape[1], width)
    normed = layer_norm(flat, ln_gain).astype(jnp.bfloat16)
    qkv = jnp.dot(normed, w_qkv, preferred_element_type=jnp.float32)
    shape_four = (count, inputs.shape[1], HEADS, HEAD)
    query = head_norm(qkv[:, :width], q_gain).astype(jnp.bfloat16).reshape(shape_four)
    key = head_norm(qkv[:, width : 2 * width], k_gain).astype(jnp.bfloat16).reshape(shape_four)
    value = qkv[:, 2 * width :].astype(jnp.bfloat16).reshape(shape_four)
    scores = jnp.einsum(
        "bqhd,bkhd->bhqk", query, key, preferred_element_type=jnp.float32
    ) * HEAD ** (-0.5)
    probs = jax.nn.softmax(scores, axis=-1)
    probs_low = probs.astype(jnp.bfloat16)
    mixed = jnp.einsum("bhqk,bkhd->bqhd", probs_low, value, preferred_element_type=jnp.float32)
    mixed = mixed.reshape(flat.shape).astype(jnp.bfloat16)
    up_proj = jnp.dot(normed, w_up, preferred_element_type=jnp.float32)
    hidden = jax.nn.gelu(up_proj, approximate=True).astype(jnp.bfloat16)
    branch = jnp.dot(mixed, w_proj, preferred_element_type=jnp.float32) + jnp.dot(
        hidden, w_down, preferred_element_type=jnp.float32
    )
    kept = (flat, normed, qkv, query, key, value, probs, probs_low, mixed, up_proj, hidden)
    return (flat + branch, kept)


def backward_parts(inputs, grad_out, weights, gains):
    w_qkv, w_up, w_proj, w_down = weights
    ln_gain, q_gain, k_gain = gains
    unused, kept = forward_parts(inputs, weights, gains)
    flat, normed, qkv, query, key, value, probs, probs_low, mixed, up_proj, hidden = kept
    width = flat.shape[1]
    grad_rows = grad_out.reshape(flat.shape)
    grad_proj = outer_sum(mixed, grad_rows)
    grad_down = outer_sum(hidden, grad_rows)
    d_mixed = times_transpose(grad_rows, w_proj).astype(jnp.bfloat16).reshape(query.shape)
    d_hidden = times_transpose(grad_rows, w_down)
    unused_gelu, gelu_pull = jax.vjp(partial(jax.nn.gelu, approximate=True), up_proj)
    d_up = gelu_pull(d_hidden)[0].astype(jnp.bfloat16)
    d_probs = jnp.einsum("bqhd,bkhd->bhqk", d_mixed, value, preferred_element_type=jnp.float32)
    d_value = jnp.einsum("bhqk,bqhd->bkhd", probs_low, d_mixed, preferred_element_type=jnp.float32)
    d_scores = (probs * (d_probs - jnp.sum(probs * d_probs, axis=-1, keepdims=True))).astype(
        jnp.bfloat16
    )
    d_query = jnp.einsum(
        "bhqk,bkhd->bqhd", d_scores, key, preferred_element_type=jnp.float32
    ) * HEAD ** (-0.5)
    d_key = jnp.einsum(
        "bhqk,bqhd->bkhd", d_scores, query, preferred_element_type=jnp.float32
    ) * HEAD ** (-0.5)
    unused_query, query_pull = jax.vjp(head_norm, qkv[:, :width], q_gain)
    d_query_raw, grad_q = query_pull(d_query.reshape(flat.shape))
    unused_key, key_pull = jax.vjp(head_norm, qkv[:, width : 2 * width], k_gain)
    d_key_raw, grad_k = key_pull(d_key.reshape(flat.shape))
    d_qkv = jnp.concatenate([d_query_raw, d_key_raw, d_value.reshape(flat.shape)], axis=1).astype(
        jnp.bfloat16
    )
    grad_qkv = outer_sum(normed, d_qkv)
    grad_up = outer_sum(normed, d_up)
    d_normed = times_transpose(d_qkv, w_qkv) + times_transpose(d_up, w_up)
    unused_norm, norm_pull = jax.vjp(layer_norm, flat, ln_gain)
    d_flat, grad_ln = norm_pull(d_normed)
    d_inputs = (grad_rows.astype(jnp.float32) + d_flat).reshape(inputs.shape).astype(jnp.bfloat16)
    return (d_inputs, (grad_qkv, grad_up, grad_proj, grad_down), (grad_ln, grad_q, grad_k))


def on_device(images, cotangent, w_qkv, w_up, w_proj, w_down, ln_gain, q_gain, k_gain):
    first_section = lax.axis_index("section") == 0
    shards = (w_qkv, w_up, w_proj, w_down)
    gains = (ln_gain[0], q_gain[0], k_gain[0])

    def weights_now():
        return tuple(
            (
                piece[0]
                for piece in (
                    lax.all_gather(w_qkv, "dp", axis=1, tiled=True),
                    lax.all_gather(w_up, "dp", axis=1, tiled=True),
                    lax.all_gather(w_proj, "dp", axis=1, tiled=True),
                    lax.all_gather(w_down, "dp", axis=1, tiled=True),
                )
            )
        )

    group = images.shape[0] // M
    blank = jnp.zeros((group,) + images.shape[1:], jnp.bfloat16)
    received = blank
    kept_inputs = []
    kept_outputs = []
    for moment in range(M + 1):
        chosen = min(moment, M - 1)
        own = images[chosen * group : (chosen + 1) * group]
        inputs = jnp.where(first_section, own, received)
        output = forward_parts(inputs, weights_now(), gains)[0]
        output = output.reshape(inputs.shape).astype(jnp.bfloat16)
        kept_inputs.append(inputs)
        kept_outputs.append(output)
        if moment < M:
            received = from_behind(output, "section", 1)
    section_inputs = [
        jnp.where(first_section, kept_inputs[index], kept_inputs[index + 1]) for index in range(M)
    ]
    section_outputs = [
        jnp.where(first_section, kept_outputs[index], kept_outputs[index + 1]) for index in range(M)
    ]
    dp_count = lax.axis_size("dp")
    weight_totals = tuple(
        (jnp.zeros((piece.shape[1] * dp_count, piece.shape[2]), jnp.float32) for piece in shards)
    )
    gain_totals = tuple((jnp.zeros_like(gain) for gain in gains))
    arriving = blank
    grads_kept = []
    for moment in range(M + 1):
        later = min(moment, M - 1)
        earlier = max(moment - 1, 0)
        inputs = jnp.where(first_section, section_inputs[earlier], section_inputs[later])
        valid = jnp.where(first_section, moment >= 1, moment < M)
        incoming = jnp.where(
            first_section, arriving, cotangent[later * group : (later + 1) * group]
        )
        incoming = jnp.where(valid, incoming, blank)
        d_inputs, weight_terms, gain_terms = backward_parts(inputs, incoming, weights_now(), gains)
        weight_totals = tuple((total + term for total, term in zip(weight_totals, weight_terms)))
        gain_totals = tuple((total + term for total, term in zip(gain_totals, gain_terms)))
        grads_kept.append(d_inputs)
        if moment < M:
            arriving = from_behind(d_inputs, "section", -1)
    section_grads = [
        jnp.where(first_section, grads_kept[index + 1], grads_kept[index]) for index in range(M)
    ]
    summed = lax.psum_scatter(weight_totals, "dp", scatter_dimension=0, tiled=True)
    gain_sums = lax.psum(gain_totals, "dp")
    outputs = jnp.concatenate(section_outputs, axis=0)[None]
    input_grads = jnp.concatenate(section_grads, axis=0)[None]
    return (
        outputs,
        input_grads,
        summed[0][None],
        summed[1][None],
        summed[2][None],
        summed[3][None],
        gain_sums[0][None],
        gain_sums[1][None],
        gain_sums[2][None],
    )


def solution(mesh):
    placed = (
        P("dp", None, None),
        P("dp", None, None),
        P("section", "dp", None),
        P("section", "dp", None),
        P("section", "dp", None),
        P("section", "dp", None),
        P("section", None),
        P("section", None),
        P("section", None),
    )
    return jax.shard_map(
        on_device,
        mesh=mesh,
        in_specs=placed,
        out_specs=(
            P("section", "dp", None, None),
            P("section", "dp", None, None),
            P("section", "dp", None),
            P("section", "dp", None),
            P("section", "dp", None),
            P("section", "dp", None),
            P("section", None),
            P("section", None),
            P("section", None),
        ),
        check_vma=False,
    )
```

profile of v0, /device:TPU:0, one launch (start us, length us, event | category | flops | bytes accessed | tf_op | source)
XLA Modules:
  0.0 1140.5 jit_solution(12178413584066658649)
XLA Ops:
  10.0 3.5 fusion.296
  17.6 42.6 %all-gather.5.cloned.1.call-done = bf16[1,768,2304]{2,1,0:T(8,128)(2,1)} async-done(((bf16[1,48,2304]{2,1,0:T(8,128)(2,1)}), bf16[1,768,2304]{2,1,0:T(8,128)(2,1)}) %all-gather.5.cloned.1.call-update) | async-done | bytes 3538960 | tf_op jit(solution)/shard_map/all_gather | solution.py:125
  60.2 3.6 fusion.115
  77.5 3.6 multiply_convert_fusion.29
  88.1 3.8 fusion.298
  95.3 3.7 fusion.178
  101.1 13.8 %all-gather.9.cloned.1.call-done = bf16[1,768,3072]{2,1,0:T(8,128)(2,1)} async-done(((bf16[1,48,3072]{2,1,0:T(8,128)(2,1)}), bf16[1,768,3072]{2,1,0:T(8,128)(2,1)}) %all-gather.9.cloned.1.call-update) | async-done | bytes 4718608 | tf_op jit(solution)/shard_map/all_gather | solution.py:126
  114.9 6.7 fusion.34
  121.6 47.5 %all-gather.11.cloned.1.call-done = bf16[1,3072,768]{2,1,0:T(8,128)(2,1)} async-done(((bf16[1,192,768]{2,1,0:T(8,128)(2,1)}), bf16[1,3072,768]{2,1,0:T(8,128)(2,1)}) %all-gather.11.cloned.1.call-update) | async-done | bytes 4718608 | tf_op jit(solution)/shard_map/all_gather | solution.py:128
  169.2 6.1 fusion.61
  175.3 32.9 %all-gather.7.cloned.1.call-done = bf16[1,768,768]{2,1,0:T(8,128)(2,1)} async-done(((bf16[1,48,768]{2,1,0:T(8,128)(2,1)}), bf16[1,768,768]{2,1,0:T(8,128)(2,1)}) %all-gather.7.cloned.1.call-update) | async-done | bytes 1179664 | tf_op jit(solution)/shard_map/all_gather | solution.py:127
  214.9 13.1 %collective-permute-done = bf16[2,196,768]{2,0,1:T(2,128)(2,1)S(1)} collective-permute-done((bf16[2,196,768]{2,0,1:T(2,128)(2,1)S(1)}, bf16[2,196,768]{2,0,1:T(2,128)(2,1)S(1)}, u32[]{:S(2)}, u32[]{:S(2)}) %collective-permute-start) | collective-permute-done | bytes 602144 | tf_op jit(solution)/shard_map/ppermute | solution.py:19
  230.2 3.8 fusion.113
  247.9 4.6 multiply_convert_fusion.27
  260.4 3.6 fusion.299
  269.4 5.5 fusion.42
  274.9 4.5 fusion.59
  284.2 5.2 collective-permute-start.1
  310.2 3.8 fusion.109
  328.9 3.8 fusion.105
  350.8 7.0 multiply_convert_fusion.23
  370.3 5.6 fusion.301
  375.9 4.4 fusion.172
  385.0 4.1 reshape.1224
  410.3 3.5 reshape.1181
  420.4 3.9 fusion.101
  429.5 3.8 fusion.111
  459.8 3.7 copy.549
  471.2 3.6 copy.370
  491.4 6.3 multiply_reduce_fusion.35
  497.8 5.1 fusion.218
  506.7 4.7 fusion.12
  529.9 6.9 multiply_convert_fusion.25
  552.6 5.3 fusion.302
  557.8 4.1 fusion.303
  561.9 4.3 fusion.176
  587.1 3.5 copy.436
  603.5 6.6 fusion.69
  616.0 4.6 fusion.173
  630.8 3.5 reshape.1193
  642.0 3.7 reshape.1196
  676.7 6.4 multiply_reduce_fusion.34
  683.1 8.8 fusion.19
  703.9 5.2 fusion.217
  709.1 8.1 collective-permute-done.3
  723.5 4.6 fusion.174
  736.2 3.5 reshape.1208
  742.0 4.2 add_add_fusion.9
  757.8 3.6 copy.559
  788.1 6.4 multiply_reduce_fusion.33
  795.6 8.3 add_add_fusion.2
  805.0 4.6 fusion.65
  816.3 8.5 fusion.26
  824.8 7.7 add_add_fusion.1
  833.6 5.1 fusion.138
  838.7 9.1 fusion.139
  847.8 8.2 add_add_fusion
  869.5 4.3 fusion.300
  876.7 5.3 fusion.50
  882.1 4.9 fusion.57
  896.1 4.8 multiply_reduce_fusion.39
  904.6 31.2 %all-reduce = (f32[1,768]{1,0:T(1,128)}, f32[1,768]{1,0:T(1,128)}, f32[1,768]{1,0:T(1,128)}) all-reduce(f32[1,768]{1,0:T(1,128)S(1)} %broadcast_in_dim.232, f32[1,768]{1,0:T(1,128)S(1)} %broadcast_in_dim.233, f32[1,768]{1,0:T(1,128)S(1)} %broadcast_in_dim.234), channel_id=1, replica_groups=mesh['section'=2,'dp'=16] {'dp'}, use_global_device_ids=true, to_apply=%region_76.77 | all-reduce | flops 2304 | bytes 18432 | tf_op jit(solution)/shard_map/psum | solution.py:180
  935.8 81.2 %reduce-scatter.7.cloned.1.call-done = f32[48,3072]{1,0:T(8,128)} async-done(((f32[768,3072]{1,0:T(8,128)}), f32[48,3072]{1,0:T(8,128)}) %reduce-scatter.7.cloned.1.call-update) | async-done | bytes 589840 | tf_op jit(solution)/shard_map/reduce_scatter | solution.py:179
  1017.0 116.4 %reduce-scatter.11.cloned.1.call-done = f32[192,768]{1,0:T(8,128)} async-done(((f32[3072,768]{1,0:T(8,128)}), f32[192,768]{1,0:T(8,128)}) %reduce-scatter.11.cloned.1.call-update) | async-done | bytes 589840 | tf_op jit(solution)/shard_map/reduce_scatter | solution.py:179
  (880 shorter events, 458.6 us)
Async XLA Ops:
  7.2 53.0 %all-gather.5.cloned.1.call-start = ((), (), s32[]{:S(2)}) async-start(), calls=%async_computation.4 | async-start | bytes 3760128 | tf_op jit(solution)/shard_map/all_gather | solution.py:125
  7.9 5.6 copy-start.119
  7.9 107.0 %all-gather.9.cloned.1.call-start = ((), (), s32[]{:S(2)}) async-start(), calls=%async_computation.6 | async-start | bytes 5013504 | tf_op jit(solution)/shard_map/all_gather | solution.py:126
  8.7 160.5 %all-gather.11.cloned.1.call-start = ((), (), s32[]{:S(2)}) async-start(), calls=%async_computation.7 | async-start | bytes 5013504 | tf_op jit(solution)/shard_map/all_gather | solution.py:128
  9.4 198.8 %all-gather.7.cloned.1.call-start = ((), (), s32[]{:S(2)}) async-start(), calls=%async_computation.5 | async-start | bytes 1253376 | tf_op jit(solution)/shard_map/all_gather | solution.py:127
  10.0 925.8 %reduce-scatter.9.cloned.1.call-start = ((), (), s32[]{:S(2)}) async-start(), calls=%async_computation.10 | async-start | bytes 2506752 | tf_op jit(solution)/shard_map/reduce_scatter | solution.py:179
  14.4 213.7 %copy-start.70 = (bf16[2,196,768]{2,0,1:T(2,128)(2,1)}, bf16[2,196,768]{2,0,1:T(2,128)(2,1)S(1)}, u32[]{:S(2)}) copy-start(bf16[2,196,768]{2,0,1:T(2,128)(2,1)S(1)} %get-tuple-element.88) | copy-start | bytes 1806340
  17.5 46.3 %copy-start.140 = (bf16[392,768]{1,0:T(8,128)(2,1)}, bf16[392,768]{1,0:T(8,128)(2,1)S(1)}, u32[]{:S(2)}) copy-start(bf16[392,768]{1,0:T(8,128)(2,1)S(1)} %convert_element_type.275) | copy-start | bytes 1806340
  98.9 16.0 %copy-start.141 = (bf16[392,768]{1,0:T(8,128)(2,1)S(1)}, bf16[392,768]{1,0:T(8,128)(2,1)}, u32[]{:S(2)}) copy-start(bf16[392,768]{1,0:T(8,128)(2,1)} %copy-done.140) | copy-start | bytes 1806340
  121.6 86.6 %copy-start.83 = (f32[392,768]{1,0:T(8,128)S(1)}, f32[392,768]{1,0:T(8,128)}, u32[]{:S(2)}) copy-start(f32[392,768]{1,0:T(8,128)} %reshape.1152) | copy-start | bytes 3612676
  210.9 17.1 %copy-start.62 = (bf16[2,196,768]{2,1,0:T(8,128)(2,1)}, bf16[2,196,768]{2,1,0:T(8,128)(2,1)S(1)}, u32[]{:S(2)}) copy-start(bf16[2,196,768]{2,1,0:T(8,128)(2,1)S(1)} %convert_element_type.284) | copy-start | bytes 1806340
  211.4 16.6 %collective-permute-start = (bf16[2,196,768]{2,0,1:T(2,128)(2,1)S(1)}, bf16[2,196,768]{2,0,1:T(2,128)(2,1)S(1)}, u32[]{:S(2)}, u32[]{:S(2)}) collective-permute-start(bf16[2,196,768]{2,0,1:T(2,128)(2,1)S(1)} %copy.313), channel_id=1, source_target_pairs={{0,16},{1,17},{2,18},{3,19},{4,20},{5,21},{6,22},{7,23},{8,24},{9,... | collective-permute-start | bytes 1806344 | tf_op jit(solution)/shard_map/ppermute | solution.py:19
  214.9 182.8 %copy-start.151 = (f32[12,64]{1,0:T(8,128)}, f32[12,64]{1,0:T(8,128)S(1)}, u32[]{:S(2)}) copy-start(f32[12,64]{1,0:T(8,128)S(1)} %mul.1249) | copy-start | bytes 9220
  282.9 8.6 copy-start.64
  284.2 17.1 %collective-permute-start.1 = (bf16[2,196,768]{2,0,1:T(2,128)(2,1)}, bf16[2,196,768]{2,0,1:T(2,128)(2,1)}, u32[]{:S(2)}, u32[]{:S(2)}) collective-permute-start(bf16[2,196,768]{2,0,1:T(2,128)(2,1)} %copy.329), channel_id=1, source_target_pairs={{0,16},{1,17},{2,18},{3,19},{4,20},{5,21},{6,22},{7,23},{8,24},{9,... | collective-permute-start | bytes 1806344 | tf_op jit(solution)/shard_map/ppermute | solution.py:19
  289.5 124.4 %copy-start.153 = (f32[12,64]{1,0:T(8,128)}, f32[12,64]{1,0:T(8,128)S(1)}, u32[]{:S(2)}) copy-start(f32[12,64]{1,0:T(8,128)S(1)} %mul.1270) | copy-start | bytes 9220
  296.3 5.0 copy-start.71
  302.8 5.5 copy-start.15
  306.9 207.5 %copy-start.157 = (f32[392]{0:T(512)}, f32[392]{0:T(512)S(1)}, u32[]{:S(2)}) copy-start(f32[392]{0:T(512)S(1)} %div.388) | copy-start | bytes 4708
  370.3 5.6 copy-start.127
  417.2 10.6 slice-start.6
  420.4 7.4 slice-start.7
  459.8 54.6 %copy-start.159 = (f32[392]{0:T(512)}, f32[392]{0:T(512)S(1)}, u32[]{:S(2)}) copy-start(f32[392]{0:T(512)S(1)} %rsqrt.218) | copy-start | bytes 4708
  471.2 5.0 copy-start.19
  491.4 6.4 copy-start.35
  491.4 6.4 copy-start.111
  491.4 11.4 %copy-start.187 = (bf16[1,768,2304]{2,1,0:T(8,128)(2,1)S(1)}, bf16[1,768,2304]{2,1,0:T(8,128)(2,1)}, u32[]{:S(2)}) copy-start(bf16[1,768,2304]{2,1,0:T(8,128)(2,1)} %all-gather.5.cloned.1.call-done) | copy-start | bytes 10616836
  497.8 6.7 slice-start.10
  497.8 8.9 slice-start.14
  516.6 93.5 %collective-permute-start.2 = (bf16[2,196,768]{2,0,1:T(2,128)(2,1)}, bf16[2,196,768]{2,0,1:T(2,128)(2,1)}, u32[]{:S(2)}, u32[]{:S(2)}) collective-permute-start(bf16[2,196,768]{2,0,1:T(2,128)(2,1)} %copy.394), channel_id=1, source_target_pairs={{16,0},{17,1},{18,2},{19,3},{20,4},{21,5},{22,6},{23,7},{24,8},{25... | collective-permute-start | bytes 1806344 | tf_op jit(solution)/shard_map/ppermute | solution.py:19
  523.7 6.2 copy-start.29
  540.2 17.6 %copy-start.85 = (bf16[2,196,12,64]{1,3,2,0:T(8,128)(2,1)}, bf16[2,196,12,64]{1,3,2,0:T(8,128)(2,1)S(1)}, u32[]{:S(2)}) copy-start(bf16[2,196,12,64]{1,3,2,0:T(8,128)(2,1)S(1)} %copy.455) | copy-start | bytes 1806340
  552.6 5.3 copy-start.87
  603.5 6.6 copy-start.72
  614.1 6.6 slice-start.4
  676.7 6.4 copy-start.77
  676.7 16.9 %slice-start.12 = ((s8[4718592]{0:T(1024)(128)(4,1)}), s8[4194304]{0:T(1024)(128)(4,1)S(1)}, s32[]{:S(2)}) async-start(s8[4718592]{0:T(1024)(128)(4,1)} %bitcast.435), calls=%async_computation.24 | async-start | bytes 8388608
  683.1 8.8 copy-start.105
  683.1 8.8 copy-start.107
  683.1 8.8 copy-start.109
  683.1 8.8 copy-start.188
  683.1 10.5 slice-start.13
  700.3 17.0 %collective-permute-start.3 = (bf16[2,196,768]{2,0,1:T(2,128)(2,1)S(1)}, bf16[2,196,768]{2,0,1:T(2,128)(2,1)S(1)}, u32[]{:S(2)}, u32[]{:S(2)}) collective-permute-start(bf16[2,196,768]{2,0,1:T(2,128)(2,1)S(1)} %copy.445), channel_id=1, source_target_pairs={{16,0},{17,1},{18,2},{19,3},{20,4},{21,5},{22,6},{23,7},{24,8},{25... | collective-permute-start | bytes 1806344 | tf_op jit(solution)/shard_map/ppermute | solution.py:19
  703.9 13.3 %copy-start.73 = (bf16[2,196,768]{2,0,1:T(2,128)(2,1)S(1)}, bf16[2,196,768]{2,0,1:T(2,128)(2,1)}, u32[]{:S(2)}) copy-start(bf16[2,196,768]{2,0,1:T(2,128)(2,1)} %get-tuple-element.86) | copy-start | bytes 1806340
  709.1 8.4 copy-start.45
  719.0 9.0 slice-start.2
  746.2 189.6 %reduce-scatter.5.cloned.1.call-start = ((), (), s32[]{:S(2)}) async-start(), calls=%async_computation.8 | async-start | bytes 7520256 | tf_op jit(solution)/shard_map/reduce_scatter | solution.py:179
  785.0 10.5 slice-start
  788.1 7.4 slice-start.1
  788.1 7.4 copy-start
  788.1 7.4 copy-start.116
  803.9 5.6 copy-start.36
  804.0 5.6 copy-start.158
  804.0 5.6 copy-start.160
  804.0 213.1 %reduce-scatter.7.cloned.1.call-start = ((), (), s32[]{:S(2)}) async-start(), calls=%async_computation.9 | async-start | bytes 10027008 | tf_op jit(solution)/shard_map/reduce_scatter | solution.py:179
  809.6 6.7 copy-start.84
  816.3 8.5 copy-start.1
  832.5 6.2 copy-start.78
  832.5 300.9 %reduce-scatter.11.cloned.1.call-start = ((), (), s32[]{:S(2)}) async-start(), calls=%async_computation.11 | async-start | bytes 10027008 | tf_op jit(solution)/shard_map/reduce_scatter | solution.py:179
  833.6 14.2 %slice-start.8 = ((s8[4816896]{0:T(1024)(128)(4,1)}), s8[4194304]{0:T(1024)(128)(4,1)S(1)}, s32[]{:S(2)}) async-start(s8[4816896]{0:T(1024)(128)(4,1)} %bitcast.431), calls=%async_computation.20 | async-start | bytes 8388608
  838.7 9.1 slice-start.9
  882.1 4.9 copy-start.46
  882.1 4.9 copy-start.96
  896.1 4.8 copy-start.175
  (159 other events, 415.7 us)
Sparse Core Ops, SparseCore 0:
  10.3 49.8 all-gather.4
  62.5 52.3 all-gather.8
  117.2 51.9 all-gather.10
  171.3 36.8 all-gather.6
  746.3 61.0 reduce-scatter.8
  812.3 89.0 reduce-scatter.4
  906.1 110.8 reduce-scatter.6
  1022.3 111.1 reduce-scatter.10
where the time goes:
time: 1150 us; the launch traced here: 1140 us
  local copies, waits for them, and re-layouts  376 us (33%)
  waiting for transfers between devices  361 us (31%)
  matrix products  238 us (21%)
  other arithmetic  104 us (9%)
  blocking collectives  31.2 us (3%)
  between operations  17.6 us (2%)
  starting transfers between devices  12.5 us (1%)
    reduce_scatter x4, waiting for transfers between devices, on_device(): lax.psum_scatter(weight_totals, 'dp', scatter_dimension=0, tiled=True)  198 us
    dot_general x12, matrix products, outer_sum(): lax.dot_general(left, right, (((0,), (0,)), ((), ())), preferred_element_...  62.9 us
    all_gather x1, waiting for transfers between devices, weights_now(): lax.all_gather(w_down, 'dp', axis=1, tiled=True)  47.5 us
    all_gather x1, waiting for transfers between devices, weights_now(): lax.all_gather(w_qkv, 'dp', axis=1, tiled=True)  42.6 us
    dot_general x12, matrix products, times_transpose(): lax.dot_general(left, right, (((1,), (1,)), ((), ())), preferred_element_...  42.3 us
    reshape x12, local copies, waits for them, and re-layouts, head_norm(): shaped = values.reshape(values.shape[:-1] + (HEADS, HEAD))  36.1 us
    all_gather x1, waiting for transfers between devices, weights_now(): lax.all_gather(w_proj, 'dp', axis=1, tiled=True)  32.9 us
    psum x1, blocking collectives, on_device(): gain_sums = lax.psum(gain_totals, 'dp')  31.2 us
  transfers between devices with their start and end apart: 12, of which 9 were waited for; matrix products, arithmetic and copies ran while one was open for 28% of the time, Pallas kernels for 0%

commit v1 on v0

v1 whole, which is shorter than its diff:
```python
from functools import partial

import jax
import jax.numpy as jnp
from jax import lax
from jax.experimental import pallas as pl
from jax.experimental.pallas import tpu as pltpu
from jax.sharding import PartitionSpec as P

D = 768
HEADS = 12
HEAD = 64
HALF = D // 2
PAIRS = HALF // 128
EPSILON = 1e-06
TILE = 256
BF = jnp.bfloat16
F32 = jnp.float32
C0 = 0.7978845608028654
C1 = 0.044715


def dot(a, b):
    return lax.dot_general(a, b, (((1,), (0,)), ((), ())), preferred_element_type=F32)


def dot_nt(a, b):
    return lax.dot_general(a, b, (((1,), (1,)), ((), ())), preferred_element_type=F32)


def dot_tn(a, b):
    return lax.dot_general(a, b, (((0,), (0,)), ((), ())), preferred_element_type=F32)


def head_means(x):
    row = lax.broadcasted_iota(jnp.int32, (256, 256), 0) // HEAD
    col = lax.broadcasted_iota(jnp.int32, (256, 256), 1) // HEAD
    ones = jnp.where(row == col, 1.0 / HEAD, 0.0).astype(BF)
    high = x.astype(BF)
    rest = (x - high.astype(F32)).astype(BF)
    parts = []
    for at in range(0, x.shape[1], 256):
        parts.append(dot(high[:, at : at + 256], ones) + dot(rest[:, at : at + 256], ones))
    return jnp.concatenate(parts, axis=1)


def half_mask(rows, h):
    return lax.broadcasted_iota(jnp.int32, (rows, 128), 1) // HEAD == h


def params(steps):
    return pltpu.CompilerParams(
        dimension_semantics=("arbitrary",) * steps, vmem_limit_bytes=56 * 1024 * 1024
    )


def attention_forward_kernel(
    tokens, sec, x_ref, w_ref, ln_ref, gain_ref, normed_ref, qk_ref, v_ref, r_ref, pt_ref, mixed_ref, part_ref
):
    section = sec[0]
    x = x_ref[...].astype(F32)
    rows = x.shape[0]
    pad = rows // 2
    centred = x - jnp.mean(x, axis=-1, keepdims=True)
    spread = jnp.mean(centred * centred, axis=-1, keepdims=True)
    normed = (centred * lax.rsqrt(spread + EPSILON) * ln_ref[...]).astype(BF)
    normed_ref[...] = normed
    qkv = dot(normed, w_ref[:, D:])
    qk = qkv[:, :D]
    centred = qk - head_means(qk)
    rstd = lax.rsqrt(head_means(centred * centred) + EPSILON)
    qk_ref[...] = (centred * rstd * gain_ref[...]).astype(BF)
    r_ref[...] = rstd.astype(BF)
    v_ref[...] = qkv[:, D:].astype(BF)
    valid = lax.broadcasted_iota(jnp.int32, (pad, pad), 0) < tokens
    for image in range(2):
        at = slice(image * pad, (image + 1) * pad)
        for pair in range(PAIRS):
            query = qk_ref[at, pair * 128 : (pair + 1) * 128]
            key = qk_ref[at, HALF + pair * 128 : HALF + (pair + 1) * 128]
            value = v_ref[at, pair * 128 : (pair + 1) * 128]
            mixed = jnp.zeros((pad, 128), F32)
            for h in range(2):
                mask = half_mask(pad, h)
                scores = dot_nt(jnp.where(mask, key, 0), query) * HEAD ** (-0.5)
                scores = jnp.where(valid, scores, -1e30)
                top = jnp.max(scores, axis=0, keepdims=True)
                weights = jnp.exp(scores - top)
                probs = weights * (1.0 / jnp.sum(weights, axis=0, keepdims=True))
                probs = probs.astype(BF)
                pt_ref[image, 2 * pair + h] = probs
                mixed += dot_tn(probs, jnp.where(mask, value, 0))
            mixed_ref[at, pair * 128 : (pair + 1) * 128] = mixed.astype(BF)
    proj = w_ref[pl.ds(pl.multiple_of(section * HALF, HALF), HALF), :D]
    part_ref[...] = dot(mixed_ref[...], proj).astype(BF)


def attention_forward(tokens, section, x, weights, ln_gain, qk_gain):
    rows = x.shape[0]
    images = rows // pad_of(tokens)
    pad = pad_of(tokens)
    step = 2 * pad
    row = lambda width: pl.BlockSpec((step, width), lambda i, s: (i, 0))
    full = lambda shape: pl.BlockSpec(shape, lambda i, s: (0, 0), pipeline_mode=pl.Buffered(1))
    return pl.pallas_call(
        partial(attention_forward_kernel, tokens),
        grid_spec=pltpu.PrefetchScalarGridSpec(
            num_scalar_prefetch=1,
            grid=(images // 2,),
            in_specs=[row(D), full((D, D + 3 * HALF)), full((1, D)), full((1, D))],
            out_specs=[
                row(D),
                row(D),
                row(HALF),
                row(D),
                pl.BlockSpec((2, 2 * PAIRS, pad, pad), lambda i, s: (i, 0, 0, 0)),
                row(HALF),
                row(D),
            ],
        ),
        out_shape=[
            jax.ShapeDtypeStruct((rows, D), BF),
            jax.ShapeDtypeStruct((rows, D), BF),
            jax.ShapeDtypeStruct((rows, HALF), BF),
            jax.ShapeDtypeStruct((rows, D), BF),
            jax.ShapeDtypeStruct((images, 2 * PAIRS, pad, pad), BF),
            jax.ShapeDtypeStruct((rows, HALF), BF),
            jax.ShapeDtypeStruct((rows, D), BF),
        ],
        compiler_params=params(1),
        cost_estimate=pl.CostEstimate(
            flops=2 * rows * D * (3 * HALF + HALF) + 8 * images * 6 * pad * pad * 64,
            bytes_accessed=rows * D * 12 + D * 1920 * 2,
            transcendentals=images * 6 * pad * pad,
        ),
        name="attention_forward",
    )(section, x, weights, ln_gain, qk_gain)


def feed_forward_kernel(steps, normed_ref, up_ref, down_ref, part_ref, hidden_ref, slope_ref, out_ref, acc_ref):
    step = pl.program_id(0)
    up = dot(normed_ref[...], up_ref[...])
    square = up * up
    tanh = jnp.tanh(C0 * up * (1.0 + C1 * square))
    hidden = (0.5 * up * (1.0 + tanh)).astype(BF)
    slope = 0.5 * (1.0 + tanh) + (0.5 * C0) * up * (1.0 - tanh * tanh) * (1.0 + (3.0 * C1) * square)
    hidden_ref[...] = hidden
    slope_ref[...] = slope.astype(BF)
    term = dot(hidden, down_ref[...])

    @pl.when(step == 0)
    def _():
        acc_ref[...] = part_ref[...].astype(F32) + term

    @pl.when(step > 0)
    def _():
        acc_ref[...] += term

    @pl.when(step == steps - 1)
    def _():
        out_ref[...] = acc_ref[...].astype(BF)


def up_spec():
    return pl.BlockSpec((D, TILE), lambda j: (0, j))


def down_spec(units):
    across = D // TILE
    return pl.BlockSpec((TILE, D), lambda j: (j % across, units // D + j // across))


def feed_forward(normed, weights, part):
    rows = normed.shape[0]
    units = weights.shape[1] // 2
    steps = units // TILE
    whole = pl.BlockSpec((rows, D), lambda j: (0, 0))
    tile = pl.BlockSpec((rows, TILE), lambda j: (0, j))
    return pl.pallas_call(
        partial(feed_forward_kernel, steps),
        grid=(steps,),
        in_specs=[whole, up_spec(), down_spec(units), whole],
        out_specs=[tile, tile, whole],
        out_shape=[
            jax.ShapeDtypeStruct((rows, units), BF),
            jax.ShapeDtypeStruct((rows, units), BF),
            jax.ShapeDtypeStruct((rows, D), BF),
        ],
        scratch_shapes=[pltpu.VMEM((rows, D), F32)],
        compiler_params=params(1),
        cost_estimate=pl.CostEstimate(
            flops=4 * rows * D * units,
            bytes_accessed=rows * D * 6 + rows * units * 4 + D * units * 4,
            transcendentals=rows * units,
        ),
        name="feed_forward",
    )(normed, weights, weights, part)


def feed_backward_kernel(steps, g_ref, normed_ref, up_ref, down_ref, hidden_ref, slope_ref, grad_ref, out_ref, acc_ref):
    step = pl.program_id(0)
    grad = g_ref[...]
    across = D // TILE
    d_up = (slope_ref[...].astype(F32) * dot_nt(grad, down_ref[...])).astype(BF)
    row = pl.multiple_of((step % across) * TILE, TILE)
    column = pl.multiple_of(steps * TILE + (step // across) * D, TILE)
    grad_ref[pl.ds(row, TILE), pl.ds(column, D)] = dot_tn(hidden_ref[...], grad).astype(BF)
    grad_ref[:, pl.ds(pl.multiple_of(step * TILE, TILE), TILE)] = dot_tn(normed_ref[...], d_up).astype(BF)
    term = dot_nt(d_up, up_ref[...])

    @pl.when(step == 0)
    def _():
        acc_ref[...] = term

    @pl.when(step > 0)
    def _():
        acc_ref[...] += term

    @pl.when(step == steps - 1)
    def _():
        out_ref[...] = acc_ref[...].astype(BF)


def feed_backward(grad, normed, weights, hidden, slope):
    rows = normed.shape[0]
    units = weights.shape[1] // 2
    steps = units // TILE
    whole = pl.BlockSpec((rows, D), lambda j: (0, 0))
    tile = pl.BlockSpec((rows, TILE), lambda j: (0, j))
    return pl.pallas_call(
        partial(feed_backward_kernel, steps),
        grid=(steps,),
        in_specs=[whole, whole, up_spec(), down_spec(units), tile, tile],
        out_specs=[pl.BlockSpec((D, 2 * units), lambda j: (0, 0)), whole],
        out_shape=[
            jax.ShapeDtypeStruct((D, 2 * units), BF),
            jax.ShapeDtypeStruct((rows, D), BF),
        ],
        scratch_shapes=[pltpu.VMEM((rows, D), F32)],
        compiler_params=params(1),
        cost_estimate=pl.CostEstimate(
            flops=8 * rows * D * units,
            bytes_accessed=rows * D * 6 + rows * units * 4 + D * units * 8,
            transcendentals=0,
        ),
        name="feed_backward",
    )(grad, normed, weights, weights, hidden, slope)


def attention_backward_kernel(
    steps,
    sec,
    g_ref,
    w_ref,
    gain_ref,
    inverse_ref,
    normed_ref,
    qk_ref,
    v_ref,
    r_ref,
    pt_ref,
    mixed_ref,
    ff_ref,
    grad_ref,
    out_ref,
    sums_ref,
    qkv_acc,
    proj_acc,
    d_qk,
    d_qkv,
):
    step = pl.program_id(0)
    section = sec[0]
    rows = g_ref.shape[0]
    pad = rows // 2

    @pl.when(step == 0)
    def _():
        sums_ref[...] = jnp.zeros_like(sums_ref)

    grad = g_ref[...]
    here = pl.ds(pl.multiple_of(section * HALF, HALF), HALF)
    d_mixed = dot_nt(grad, w_ref[here, :D]).astype(BF)
    proj_term = dot_tn(mixed_ref[...], grad)
    for image in range(2):
        at = slice(image * pad, (image + 1) * pad)
        for pair in range(PAIRS):
            lanes = slice(pair * 128, (pair + 1) * 128)
            key_lanes = slice(HALF + pair * 128, HALF + (pair + 1) * 128)
            query = qk_ref[at, lanes]
            key = qk_ref[at, key_lanes]
            value = v_ref[at, lanes]
            d_mix = d_mixed[at, lanes]
            d_query = jnp.zeros((pad, 128), F32)
            d_key = jnp.zeros((pad, 128), F32)
            d_value = jnp.zeros((pad, 128), F32)
            for h in range(2):
                mask = half_mask(pad, h)
                d_mix_head = jnp.where(mask, d_mix, 0)
                probs_low = pt_ref[image, 2 * pair + h]
                probs = probs_low.astype(F32)
                d_probs = dot_nt(value, d_mix_head)
                weighted = jnp.sum(probs * d_probs, axis=0, keepdims=True)
                d_scores = (probs * (d_probs - weighted)).astype(BF)
                d_value += dot(probs_low, d_mix_head)
                d_key += dot(d_scores, jnp.where(mask, query, 0))
                d_query += dot_tn(d_scores, jnp.where(mask, key, 0))
            d_qk[at, lanes] = d_query * HEAD ** (-0.5)
            d_qk[at, key_lanes] = d_key * HEAD ** (-0.5)
            d_qkv[at, D + pair * 128 : D + (pair + 1) * 128] = d_value.astype(BF)
    d_normed_heads = d_qk[...]
    shaped = qk_ref[...].astype(F32) * inverse_ref[...]
    sums_ref[1:2, :] += jnp.sum(d_normed_heads * shaped, axis=0, keepdims=True)
    scaled = d_normed_heads * gain_ref[...]
    d_qkv[:, :D] = (
        r_ref[...].astype(F32) * (scaled - head_means(scaled) - shaped * head_means(scaled * shaped))
    ).astype(BF)
    normed = normed_ref[...]
    qkv_term = dot_tn(normed, d_qkv[...])
    d_normed = dot_nt(d_qkv[...], w_ref[:, D:]) + ff_ref[...].astype(F32)
    out_ref[...] = d_normed.astype(BF)
    sums_ref[0:1, :] += jnp.sum(d_normed * normed.astype(F32), axis=0, keepdims=True)

    @pl.when(step == 0)
    def _():
        qkv_acc[...] = qkv_term
        proj_acc[...] = proj_term

    @pl.when(step > 0)
    def _():
        qkv_acc[...] += qkv_term
        proj_acc[...] += proj_term

    @pl.when(step == steps - 1)
    def _():
        there = pl.ds(pl.multiple_of((1 - section) * HALF, HALF), HALF)
        grad_ref[here, :D] = proj_acc[...].astype(BF)
        grad_ref[there, :D] = jnp.zeros((HALF, D), BF)
        grad_ref[:, D:] = qkv_acc[...].astype(BF)


def attention_backward(tokens, section, grad, weights, qk_gain, normed, qk, v, r, pt, mixed, ff):
    rows = normed.shape[0]
    pad = pad_of(tokens)
    images = rows // pad
    step = 2 * pad
    steps = images // 2
    width = weights.shape[1]
    row = lambda columns: pl.BlockSpec((step, columns), lambda i, s: (i, 0))
    full = lambda shape: pl.BlockSpec(shape, lambda i, s: (0, 0), pipeline_mode=pl.Buffered(1))
    return pl.pallas_call(
        partial(attention_backward_kernel, steps),
        grid_spec=pltpu.PrefetchScalarGridSpec(
            num_scalar_prefetch=1,
            grid=(steps,),
            in_specs=[
                row(D),
                full((D, width)),
                full((1, D)),
                full((1, D)),
                row(D),
                row(D),
                row(HALF),
                row(D),
                pl.BlockSpec((2, 2 * PAIRS, pad, pad), lambda i, s: (i, 0, 0, 0)),
                row(HALF),
                row(D),
            ],
            out_specs=[
                pl.BlockSpec((D, width), lambda i, s: (0, 0)),
                row(D),
                pl.BlockSpec((8, D), lambda i, s: (0, 0)),
            ],
            scratch_shapes=[
                pltpu.VMEM((D, 3 * HALF), F32),
                pltpu.VMEM((HALF, D), F32),
                pltpu.VMEM((step, D), F32),
                pltpu.VMEM((step, 3 * HALF), BF),
            ],
        ),
        out_shape=[
            jax.ShapeDtypeStruct((D, width), BF),
            jax.ShapeDtypeStruct((rows, D), BF),
            jax.ShapeDtypeStruct((8, D), F32),
        ],
        compiler_params=params(1),
        cost_estimate=pl.CostEstimate(
            flops=4 * rows * D * 4 * HALF + 16 * images * 6 * pad * pad * 64,
            bytes_accessed=rows * D * 16 + D * width * 4,
            transcendentals=0,
        ),
        name="attention_backward",
    )(section, grad, weights, qk_gain, 1.0 / qk_gain, normed, qk, v, r, pt, mixed, ff)


def norm_backward_kernel(g_ref, x_ref, mine_ref, theirs_ref, ln_ref, out_ref):
    x = x_ref[...].astype(F32)
    centred = x - jnp.mean(x, axis=-1, keepdims=True)
    rstd = lax.rsqrt(jnp.mean(centred * centred, axis=-1, keepdims=True) + EPSILON)
    shaped = centred * rstd
    scaled = (mine_ref[...].astype(F32) + theirs_ref[...].astype(F32)) * ln_ref[...]
    d_x = rstd * (
        scaled
        - jnp.mean(scaled, axis=-1, keepdims=True)
        - shaped * jnp.mean(scaled * shaped, axis=-1, keepdims=True)
    )
    out_ref[...] = (g_ref[...].astype(F32) + d_x).astype(BF)


def norm_backward(grad, x, mine, theirs, ln_gain):
    rows = x.shape[0]
    block = pl.BlockSpec((rows // 4, D), lambda i: (i, 0))
    return pl.pallas_call(
        norm_backward_kernel,
        grid=(4,),
        in_specs=[block] * 4 + [pl.BlockSpec((1, D), lambda i: (0, 0))],
        out_specs=block,
        out_shape=jax.ShapeDtypeStruct((rows, D), BF),
        compiler_params=params(1),
        cost_estimate=pl.CostEstimate(flops=12 * rows * D, bytes_accessed=rows * D * 10, transcendentals=0),
        name="norm_backward",
    )(grad, x, mine, theirs, ln_gain)


def pad_of(tokens):
    return -(-tokens // 16) * 16


def relative(value, step):
    count = lax.axis_size("dp")
    return lax.ppermute(value, "dp", [(source, source ^ step) for source in range(count)])


def gather_rows(shard):
    count = lax.axis_size("dp")
    me = lax.axis_index("dp")
    quads = [shard] + [relative(shard, 4 * far) for far in range(1, count // 4)]
    pieces = {4 * far: piece for far, piece in enumerate(quads)}
    pieces.update({4 * far + 2: relative(piece, 2) for far, piece in enumerate(quads)})
    pieces.update({step + 1: relative(piece, 1) for step, piece in list(pieces.items())})
    whole = jnp.zeros((count,) + shard.shape, shard.dtype)
    for step, piece in pieces.items():
        whole = lax.dynamic_update_slice(whole, piece[None], (me ^ step, 0, 0))
    return whole.reshape(count * shard.shape[0], shard.shape[1])


def add_low(left, right):
    return (left.astype(F32) + right.astype(F32)).astype(BF)


def scatter_rows(terms):
    count = lax.axis_size("dp")
    me = lax.axis_index("dp")
    core, near, far = me % 2, (me // 2) % 2, me // 4
    rows, width = terms.shape
    shaped = terms.reshape(count // 4, 2, 2, rows // count, width)
    pick = lambda value, at, axis: lax.dynamic_index_in_dim(value, at, axis, keepdims=False)
    total = add_low(pick(shaped, core, 2), relative(pick(shaped, 1 - core, 2), 1))
    total = add_low(pick(total, near, 1), relative(pick(total, 1 - near, 1), 2))
    result = pick(total, far, 0).astype(F32)
    for step in range(1, count // 4):
        result = result + relative(pick(total, far ^ step, 0), 4 * step).astype(F32)
    return result


def on_device(images, cotangent, w_qkv, w_up, w_proj, w_down, ln_gain, q_gain, k_gain):
    count = lax.axis_size("dp")
    section = lax.axis_index("section")
    first = section == 0
    scalar = section.astype(jnp.int32).reshape(1)
    number, tokens, _ = images.shape
    pad = pad_of(tokens)
    rows = w_qkv.shape[1]
    group = w_down.shape[1] // 4
    units = w_up.shape[2] // 2

    def swap(value):
        return lax.ppermute(value, "section", [(0, 1), (1, 0)])

    def give(value, source):
        return lax.ppermute(value, "section", [(source, 1 - source)])

    def half_of(half):
        parts = [w_proj[0]]
        for pair in range(3):
            at = pair * D + half * HALF
            parts.append(w_qkv[0, :, at : at + HALF])
        ups = w_up[0].reshape(rows, count, 4, group)
        for part in (2 * half, 2 * half + 1):
            parts.append(ups[:, :, part].reshape(rows, count * group))
        for part in (2 * half, 2 * half + 1):
            parts.append(w_down[0, part * group : (part + 1) * group])
        return jnp.concatenate(parts, axis=1)

    halves = (half_of(0), half_of(1))
    mine = jnp.where(first, halves[0], halves[1])
    other = swap(jnp.where(first, halves[1], halves[0]))
    shards = (jnp.where(first, mine, other), jnp.where(first, other, mine))
    split = D + 3 * HALF

    gains = []
    for gain in (ln_gain, q_gain, k_gain):
        theirs = swap(gain[0])
        gains.append((jnp.where(first, gain[0], theirs), jnp.where(first, theirs, gain[0])))
    at_half = lambda gain: lax.dynamic_slice_in_dim(gain, section * HALF, HALF, 0)
    ln_gains = [gain[None] for gain in gains[0]]
    qk_gains = [
        jnp.concatenate([at_half(gains[1][block]), at_half(gains[2][block])])[None] for block in range(2)
    ]

    def padded(value):
        return jnp.pad(value, ((0, 0), (0, pad - tokens), (0, 0))).reshape(number * pad, D)

    def trimmed(value):
        return value.reshape(number, pad, D)[:, :tokens]

    attention_weights, feed_weights, inputs, kept = [], [], [padded(images)], []
    parts = None
    for block in range(2):
        gathered = gather_rows(shards[block])
        attention_weights.append(gathered[:, :split])
        feed_weights.append(gathered[:, split:])
        saved = attention_forward(
            tokens, scalar, inputs[block], attention_weights[block], ln_gains[block], qk_gains[block]
        )
        hidden, slope, part = feed_forward(saved[0], feed_weights[block], saved[6])
        kept.append(tuple(saved[:6]) + (hidden, slope))
        theirs = swap(part) if block == 0 else give(part, 0)
        inputs.append(
            (inputs[block].astype(F32) + part.astype(F32) + theirs.astype(F32)).astype(BF)
        )
    outputs = trimmed(jnp.where(first, inputs[1], inputs[2]))

    grad = padded(cotangent)
    grads = [None, None]
    summed = [None, None]
    sums = [None, None]
    for block in (1, 0):
        normed, qk, v, r, pt, mixed, hidden, slope = kept[block]
        feed_grads, feed_part = feed_backward(grad, normed, feed_weights[block], hidden, slope)
        attention_grads, part, sums[block] = attention_backward(
            tokens, scalar, grad, attention_weights[block], qk_gains[block], normed, qk, v, r, pt, mixed, feed_part
        )
        theirs = swap(part) if block == 1 else give(part, 1)
        grad = norm_backward(grad, inputs[block], part, theirs, ln_gains[block])
        grads[block] = grad
        summed[block] = jnp.concatenate([scatter_rows(attention_grads), scatter_rows(feed_grads)], axis=1)
    input_grads = trimmed(jnp.where(first, grads[0], grads[1]))

    own = jnp.where(first, summed[0], summed[1])
    theirs = swap(jnp.where(first, summed[1], summed[0]).astype(BF)).astype(F32)
    low_half = jnp.where(first, own, theirs)
    high_half = jnp.where(first, theirs, own)
    grad_proj = own[:, :D] + theirs[:, :D]
    pieces = []
    for pair in range(3):
        at = slice(D + pair * HALF, D + (pair + 1) * HALF)
        pieces += [low_half[:, at], high_half[:, at]]
    grad_qkv = jnp.concatenate(pieces, axis=1)
    ups, downs = [], []
    for source in (low_half, high_half):
        for part in range(2):
            at = split + part * D
            ups.append(source[:, at : at + D].reshape(rows, count, 1, group))
            at = split + units + part * D
            downs.append(source[:, at : at + D])
    grad_up = jnp.concatenate(ups, axis=2).reshape(rows, 2 * units)
    grad_down = jnp.concatenate(downs, axis=0)

    gain_rows = []
    for block in range(2):
        zero = jnp.zeros((D,), F32)
        place = lambda value: lax.dynamic_update_slice_in_dim(zero, value, section * HALF, 0)
        gain_rows += [
            sums[block][0] / gains[0][block],
            place(sums[block][1, :HALF]),
            place(sums[block][1, HALF:]),
        ]
    totals = lax.psum(jnp.stack(gain_rows), ("section", "dp"))
    totals = jnp.where(first, totals[:3], totals[3:])
    return (
        outputs[None],
        input_grads[None],
        grad_qkv[None],
        grad_up[None],
        grad_proj[None],
        grad_down[None],
        totals[0:1],
        totals[1:2],
        totals[2:3],
    )


def solution(mesh):
    placed = (
        P("dp", None, None),
        P("dp", None, None),
        P("section", "dp", None),
        P("section", "dp", None),
        P("section", "dp", None),
        P("section", "dp", None),
        P("section", None),
        P("section", None),
        P("section", None),
    )
    return jax.shard_map(
        on_device,
        mesh=mesh,
        in_specs=placed,
        out_specs=(
            P("section", "dp", None, None),
            P("section", "dp", None, None),
            P("section", "dp", None),
            P("section", "dp", None),
            P("section", "dp", None),
            P("section", "dp", None),
            P("section", None),
            P("section", None),
            P("section", None),
        ),
        check_vma=False,
    )
```

time: 1150 us -> 619 us (0.54)
  local copies, waits for them, and re-layouts: 376 us -> 75.8 us
  matrix products: 238 us -> 0 us
  Pallas kernels: 0 us -> 144 us
  waiting for transfers between devices: 361 us -> 261 us
  other arithmetic: 104 us -> 21.2 us
  starting transfers between devices: 12.5 us -> 54.9 us
  blocking collectives: 31.2 us -> 50.3 us
  between operations: 17.6 us -> 2.18 us
    ppermute x4 -> x59, waiting for transfers between devices: 24.2 us -> 261 us  [the longest x50 214 us: relative(): lax.ppermute(value, 'dp', [(source, source ^ step) for source in range(co...]
    dot_general x63 -> x0, matrix products: 223 us -> none  [the longest x12 62.9 us: outer_sum(): lax.dot_general(left, right, (((0,), (0,)), ((), ())), preferred_element_...]
    reduce_scatter x4 -> x0, waiting for transfers between devices: 198 us -> none  [on_device(): lax.psum_scatter(weight_totals, 'dp', scatter_dimension=0, tiled=True)]
    reshape x78 -> x4, local copies, waits for them, and re-layouts: 183 us -> 1.64 us  [on_device(): ups.append(source[:, at:at + D].reshape(rows, count, 1, group))]
    pallas_call x0 -> x10, Pallas kernels: none -> 144 us  [the longest x2 39.7 us: feed_forward(): pl.pallas_call(partial(feed_forward_kernel, steps), grid=(steps,), in_spe...]
    all_gather x4 -> x0, waiting for transfers between devices: 137 us -> none  [the longest x1 47.5 us: weights_now(): lax.all_gather(w_down, 'dp', axis=1, tiled=True)]
    reduce_sum x54 -> x0, other arithmetic: 52.7 us -> none  [the longest x9 30.6 us: head_norm(): return (centred * lax.rsqrt(spread + EPSILON)).reshape(values.shape) * gain]
    ppermute x4 -> x59, starting transfers between devices: 11.3 us -> 54.9 us  [the longest x50 42.9 us: relative(): lax.ppermute(value, 'dp', [(source, source ^ step) for source in range(co...]
  transfers between devices with their start and end apart: 12 -> 59, of which waited for: 9 -> 25; matrix products, arithmetic and copies ran while one was open for 28% -> 11% of each run, Pallas kernels for 0% -> 18%
where the time goes in v1:
time: 619 us; the launch traced here: 609 us
  waiting for transfers between devices  261 us (42%)
  Pallas kernels  144 us (23%)
  local copies, waits for them, and re-layouts  75.8 us (12%)
  starting transfers between devices  54.9 us (9%)
  blocking collectives  50.3 us (8%)
  other arithmetic  21.2 us (3%)
    ppermute x50, waiting for transfers between devices, relative(): lax.ppermute(value, 'dp', [(source, source ^ step) for source in range(co...  214 us
    psum x1, blocking collectives, on_device(): totals = lax.psum(jnp.stack(gain_rows), ('section', 'dp'))  50.3 us
    ppermute x7, waiting for transfers between devices, swap(): return lax.ppermute(value, 'section', [(0, 1), (1, 0)])  46.8 us
    ppermute x50, starting transfers between devices, relative(): lax.ppermute(value, 'dp', [(source, source ^ step) for source in range(co...  42.9 us
    pallas_call x2, Pallas kernels, feed_forward(): pl.pallas_call(partial(feed_forward_kernel, steps), grid=(steps,), in_spe...  39.7 us
    pallas_call x2, Pallas kernels, attention_backward(): pl.pallas_call(partial(attention_backward_kernel, steps), grid_spec=pltpu...  37.2 us
    pallas_call x2, Pallas kernels, feed_backward(): pl.pallas_call(partial(feed_backward_kernel, steps), grid=(steps,), in_sp...  33.9 us
    pallas_call x2, Pallas kernels, attention_forward(): pl.pallas_call(partial(attention_forward_kernel, tokens), grid_spec=pltpu...  22.4 us
  transfers between devices with their start and end apart: 59, of which 25 were waited for; matrix products, arithmetic and copies ran while one was open for 11% of the time, Pallas kernels for 18%

profile of v1, /device:TPU:0, one launch (start us, length us, event | category | flops | bytes accessed | tf_op | source)
XLA Modules:
  0.0 609.1 jit_solution(6739321875989403035)
XLA Ops:
  3.9 1.8 reshape_squeeze.16
  5.8 4.6 slice_reduce_fusion.2
  13.0 3.0 collective-permute-start
  16.1 2.1 collective-permute-start.18
  21.0 2.5 pad.7.clone
  24.6 2.5 collective-permute-done.16
  32.1 1.9 collective-permute-start.1
  33.9 2.6 collective-permute-start.2
  36.5 1.7 collective-permute-start.4
  39.0 14.3 %collective-permute-done.1 = bf16[48,4992]{1,0:T(8,128)(2,1)S(1)} collective-permute-done((bf16[48,4992]{1,0:T(8,128)(2,1)S(1)}, bf16[48,4992]{1,0:T(8,128)(2,1)S(1)}, u32[]{:S(2)}, u32[]{:S(2)}) %collective-permute-start.1) | collective-permute-done | bytes 479264 | tf_op jit(solution)/shard_map/ppermute | solution.py:431
  53.4 22.7 %collective-permute-done.20 = bf16[48,4992]{1,0:T(8,128)(2,1)S(1)} collective-permute-done((bf16[48,4992]{1,0:T(8,128)(2,1)S(1)}, bf16[48,4992]{1,0:T(8,128)(2,1)S(1)}, u32[]{:S(2)}, u32[]{:S(2)}) %collective-permute-start.20) | collective-permute-done | bytes 479264 | tf_op jit(solution)/shard_map/ppermute | solution.py:431
  76.0 1.7 collective-permute-start.21
  79.3 30.5 %collective-permute-done.21 = bf16[48,4992]{1,0:T(8,128)(2,1)S(1)} collective-permute-done((bf16[48,4992]{1,0:T(8,128)(2,1)S(1)}, bf16[48,4992]{1,0:T(8,128)(2,1)S(1)}, u32[]{:S(2)}, u32[]{:S(2)}) %collective-permute-start.21) | collective-permute-done | bytes 479264 | tf_op jit(solution)/shard_map/ppermute | solution.py:431
  113.7 9.9 %collective-permute-done.23 = bf16[48,4992]{1,0:T(8,128)(2,1)S(1)} collective-permute-done((bf16[48,4992]{1,0:T(8,128)(2,1)S(1)}, bf16[48,4992]{1,0:T(8,128)(2,1)S(1)}, u32[]{:S(2)}, u32[]{:S(2)}) %collective-permute-start.23) | collective-permute-done | bytes 479264 | tf_op jit(solution)/shard_map/ppermute | solution.py:431
  125.2 8.7 %collective-permute-done.5 = bf16[48,4992]{1,0:T(8,128)(2,1)S(1)} collective-permute-done((bf16[48,4992]{1,0:T(8,128)(2,1)S(1)}, bf16[48,4992]{1,0:T(8,128)(2,1)S(1)}, u32[]{:S(2)}, u32[]{:S(2)}) %collective-permute-start.5) | collective-permute-done | bytes 479264 | tf_op jit(solution)/shard_map/ppermute | solution.py:431
  135.5 26.6 %collective-permute-done.24 = bf16[48,4992]{1,0:T(8,128)(2,1)S(1)} collective-permute-done((bf16[48,4992]{1,0:T(8,128)(2,1)S(1)}, bf16[48,4992]{1,0:T(8,128)(2,1)S(1)}, u32[]{:S(2)}, u32[]{:S(2)}) %collective-permute-start.24) | collective-permute-done | bytes 479264 | tf_op jit(solution)/shard_map/ppermute | solution.py:431
  162.6 13.1 %collective-permute-done.25 = bf16[48,4992]{1,0:T(8,128)(2,1)} collective-permute-done((bf16[48,4992]{1,0:T(8,128)(2,1)S(1)}, bf16[48,4992]{1,0:T(8,128)(2,1)}, u32[]{:S(2)}, u32[]{:S(2)}) %collective-permute-start.25) | collective-permute-done | bytes 479264 | tf_op jit(solution)/shard_map/ppermute | solution.py:431
  177.2 13.1 %collective-permute-done.26 = bf16[48,4992]{1,0:T(8,128)(2,1)} collective-permute-done((bf16[48,4992]{1,0:T(8,128)(2,1)S(1)}, bf16[48,4992]{1,0:T(8,128)(2,1)}, u32[]{:S(2)}, u32[]{:S(2)}) %collective-permute-start.26) | collective-permute-done | bytes 479264 | tf_op jit(solution)/shard_map/ppermute | solution.py:431
  198.2 2.0 collective-permute-done.15
  200.3 3.1 copy-done
  203.3 1.8 slice.192.w_ref
  205.1 11.2 %attention_forward.2 = (bf16[832,768]{1,0:T(8,128)(2,1)}, bf16[832,768]{1,0:T(8,128)(2,1)}, bf16[832,384]{1,0:T(8,128)(2,1)}, bf16[832,768]{1,0:T(8,128)(2,1)}, ...) custom-call(s32[1]{0:T(128)} %bitcast.1.sec, bf16[832,768]{1,0:T(8,128)(2,1)} %bitcast.202, ...), custom_call_target="tpu_custom_call" | custom-call | flops 2494562304 | bytes 10616832 | tf_op jit(solution)/shard_map/attention_forward/pallas_call | solution.py:105
  216.3 4.9 slice.193.up_ref.down_ref
  221.2 15.4 %feed_forward.2 = (bf16[832,1536]{1,0:T(8,128)(2,1)}, bf16[832,1536]{1,0:T(8,128)(2,1)}, bf16[832,768]{1,0:T(8,128)(2,1)}) custom-call(bf16[832,768]{1,0:T(8,128)(2,1)} %get-tuple-element.39.normed_ref, bf16[768,3072]{1,0:T(8,128)(2,1)} %slice.193.up_ref.down_ref, bf16[768,3072]{1,0:T(8,128)(2,1)} %slice.193.up_ref.down_ref, ...), custom_call_target="tpu_custom_call" | custom-call | flops 3925868544 | bytes 13664256 | tf_op jit(solution)/shard_map/feed_forward/pallas_call | solution.py:179
  239.9 1.9 slice.194.w_ref
  241.8 2.8 slice.195.up_ref.down_ref
  244.6 22.5 %collective-permute-done.19 = bf16[832,768]{1,0:T(8,128)(2,1)S(1)} collective-permute-done((bf16[832,768]{1,0:T(8,128)(2,1)}, bf16[832,768]{1,0:T(8,128)(2,1)S(1)}, u32[]{:S(2)}, u32[]{:S(2)}) %collective-permute-start.19) | collective-permute-done | bytes 1277984 | tf_op jit(solution)/shard_map/ppermute | solution.py:478
  267.1 1.7 add_convert_fusion.1.x_ref
  268.8 11.2 %attention_forward.3 = (bf16[832,768]{1,0:T(8,128)(2,1)}, bf16[832,768]{1,0:T(8,128)(2,1)}, bf16[832,384]{1,0:T(8,128)(2,1)}, bf16[832,768]{1,0:T(8,128)(2,1)}, ...) custom-call(s32[1]{0:T(128)} %bitcast.1.sec, ...), custom_call_target="tpu_custom_call" | custom-call | flops 2494562304 | bytes 10616832 | tf_op jit(solution)/shard_map/attention_forward/pallas_call | solution.py:105
  280.0 24.3 %feed_forward.3 = (bf16[832,1536]{1,0:T(8,128)(2,1)}, bf16[832,1536]{1,0:T(8,128)(2,1)}, bf16[832,768]{1,0:T(8,128)(2,1)}) custom-call(bf16[832,768]{1,0:T(8,128)(2,1)} %get-tuple-element.42.normed_ref, bf16[768,3072]{1,0:T(8,128)(2,1)} %slice.195.up_ref.down_ref, bf16[768,3072]{1,0:T(8,128)(2,1)} %slice.195.up_ref.down_ref, ...), custom_call_target="tpu_custom_call" | custom-call | flops 3925868544 | bytes 13664256 | tf_op jit(solution)/shard_map/feed_forward/pallas_call | solution.py:179
  304.3 2.3 collective-permute-start.35
  306.6 16.8 %feed_backward.2 = (bf16[768,3072]{1,0:T(8,128)(2,1)}, bf16[832,768]{1,0:T(8,128)(2,1)}) custom-call(bf16[832,768]{1,0:T(8,128)(2,1)} %bitcast.204, bf16[832,768]{1,0:T(8,128)(2,1)} %get-tuple-element.42.normed_ref, bf16[768,3072]{1,0:T(8,128)(2,1)} %slice.195.up_ref.down_ref, bf16[768,3072]{1,0:T(8,128)(2,1)} %slice.195.up_ref.down_ref, ...), custom_call_target="tpu_custom_call" | custom-call | flops 7851737088 | bytes 18382848 | tf_op jit(solution)/shard_map/feed_backward/pallas_call | solution.py:230
  323.4 18.7 %attention_backward.2 = (bf16[768,1920]{1,0:T(8,128)(2,1)}, bf16[832,768]{1,0:T(8,128)(2,1)}, f32[8,768]{1,0:T(8,128)}) custom-call(s32[1]{0:T(128)} %bitcast.1.sec, bf16[832,768]{1,0:T(8,128)(2,1)} %bitcast.205, bf16[768,1920]{1,0:T(8,128)(2,1)} %slice.194.w_ref, f32[1,768]{1,0:T(1,128)} %broadcast_in_dim.158.gain_ref, ...), custom_call_target="tpu_custom_call" | custom-call | flops 4989124608 | bytes 16121856 | tf_op jit(solution)/shard_map/attention_backward/pallas_call | solution.py:351
  342.2 1.8 constant_dynamic-slice_fusion.1
  350.4 21.5 %collective-permute-done.36.theirs_ref = bf16[832,768]{1,0:T(8,128)(2,1)S(1)} collective-permute-done((bf16[832,768]{1,0:T(8,128)(2,1)}, bf16[832,768]{1,0:T(8,128)(2,1)S(1)}, u32[]{:S(2)}, u32[]{:S(2)}) %collective-permute-start.36) | collective-permute-done | bytes 1277984 | tf_op jit(solution)/shard_map/ppermute | solution.py:478
  373.0 5.1 norm_backward.2.g_ref
  378.1 17.1 %feed_backward.3 = (bf16[768,3072]{1,0:T(8,128)(2,1)}, bf16[832,768]{1,0:T(8,128)(2,1)}) custom-call(bf16[832,768]{1,0:T(8,128)(2,1)} %norm_backward.2.g_ref, bf16[832,768]{1,0:T(8,128)(2,1)} %get-tuple-element.39.normed_ref, bf16[768,3072]{1,0:T(8,128)(2,1)} %slice.193.up_ref.down_ref, bf16[768,3072]{1,0:T(8,128)(2,1)} %slice.193.up_ref.down_ref, ...), custom_call_target="tpu_custom_call" | custom-call | flops 7851737088 | bytes 18382848 | tf_op jit(solution)/shard_map/feed_backward/pallas_call | solution.py:230
  398.9 1.6 copy.66
  400.5 18.5 %attention_backward.3 = (bf16[768,1920]{1,0:T(8,128)(2,1)}, bf16[832,768]{1,0:T(8,128)(2,1)}, f32[8,768]{1,0:T(8,128)}) custom-call(s32[1]{0:T(128)} %bitcast.1.sec, bf16[832,768]{1,0:T(8,128)(2,1)} %norm_backward.2.g_ref, bf16[768,1920]{1,0:T(8,128)(2,1)} %slice.192.w_ref, f32[1,768]{1,0:T(1,128)} %broadcast_in_dim.140.gain_ref, ...), custom_call_target="tpu_custom_call" | custom-call | flops 4989124608 | bytes 16121856 | tf_op jit(solution)/shard_map/attention_backward/pallas_call | solution.py:351
  419.1 3.2 constant_dynamic-slice_fusion.7
  424.0 2.8 fusion.2
  426.8 2.0 dynamic-slice_bitcast_fusion.2
  432.1 50.3 %psum.7 = f32[6,768]{1,0:T(8,128)S(1)} all-reduce(f32[6,768]{1,0:T(8,128)S(1)} %stack.18), channel_id=1, replica_groups=mesh['section'=2,'dp'=16] {'section','dp'}, use_global_device_ids=true, to_apply=%region_0.1 | all-reduce | flops 4608 | bytes 36864 | tf_op jit(solution)/shard_map/psum | solution.py:579
  486.0 2.4 collective-permute-start.50
  488.4 2.7 fusion
  491.2 1.7 fusion.3
  493.0 2.4 collective-permute-start.39
  496.7 4.7 collective-permute-done.51
  502.9 9.8 %collective-permute-done.39 = bf16[4,48,1920]{2,1,0:T(8,128)(2,1)S(1)} collective-permute-done((bf16[4,48,1920]{2,1,0:T(8,128)(2,1)S(1)}, bf16[4,48,1920]{2,1,0:T(8,128)(2,1)S(1)}, u32[]{:S(2)}, u32[]{:S(2)}) %collective-permute-start.39) | collective-permute-done | bytes 737312 | tf_op jit(solution)/shard_map/ppermute | solution.py:431
  514.6 2.8 collective-permute-start.40
  517.5 2.6 fusion.1
  520.1 15.1 %collective-permute-done.54 = bf16[4,48,3072]{2,1,0:T(8,128)(2,1)S(1)} collective-permute-done((bf16[4,48,3072]{2,1,0:T(8,128)(2,1)S(1)}, bf16[4,48,3072]{2,1,0:T(8,128)(2,1)S(1)}, u32[]{:S(2)}, u32[]{:S(2)}) %collective-permute-start.54) | collective-permute-done | bytes 1179680 | tf_op jit(solution)/shard_map/ppermute | solution.py:431
  535.2 2.0 collective-permute-start.44
  537.8 1.6 collective-permute-start.57
  539.4 2.8 collective-permute-start.55
  542.3 17.9 %collective-permute-done.44 = bf16[4,48,3072]{2,1,0:T(8,128)(2,1)S(1)} collective-permute-done((bf16[4,48,3072]{2,1,0:T(8,128)(2,1)S(1)}, bf16[4,48,3072]{2,1,0:T(8,128)(2,1)S(1)}, u32[]{:S(2)}, u32[]{:S(2)}) %collective-permute-start.44) | collective-permute-done | bytes 1179680 | tf_op jit(solution)/shard_map/ppermute | solution.py:431
  560.7 1.6 collective-permute-start.47
  562.5 7.4 %collective-permute-done.56 = bf16[48,3072]{1,0:T(8,128)(2,1)S(1)} collective-permute-done((bf16[48,3072]{1,0:T(8,128)(2,1)S(1)}, bf16[48,3072]{1,0:T(8,128)(2,1)S(1)}, u32[]{:S(2)}, u32[]{:S(2)}) %collective-permute-start.56) | collective-permute-done | bytes 294944 | tf_op jit(solution)/shard_map/ppermute | solution.py:431
  570.1 2.4 collective-permute-done.47
  572.5 13.5 %collective-permute-done.46 = bf16[48,3072]{1,0:T(8,128)(2,1)S(1)} collective-permute-done((bf16[48,3072]{1,0:T(8,128)(2,1)S(1)}, bf16[48,3072]{1,0:T(8,128)(2,1)S(1)}, u32[]{:S(2)}, u32[]{:S(2)}) %collective-permute-start.46) | collective-permute-done | bytes 294944 | tf_op jit(solution)/shard_map/ppermute | solution.py:431
  586.3 3.1 collective-permute-start.58
  589.9 5.2 norm_backward.3
  603.5 2.6 broadcast_in_dim_reshape.3
  606.9 1.8 maximum_bitcast_fusion
  (270 shorter events, 72.8 us)
Async XLA Ops:
  12.9 18.7 %copy-start.5 = (bf16[48,4992]{1,0:T(8,128)(2,1)}, bf16[48,4992]{1,0:T(8,128)(2,1)S(1)}, u32[]{:S(2)}) copy-start(bf16[48,4992]{1,0:T(8,128)(2,1)S(1)} %get-tuple-element.108) | copy-start | bytes 1437700
  13.0 18.1 %collective-permute-start = (bf16[48,4992]{1,0:T(8,128)(2,1)S(1)}, bf16[48,4992]{1,0:T(8,128)(2,1)S(1)}, u32[]{:S(2)}, u32[]{:S(2)}) collective-permute-start(bf16[48,4992]{1,0:T(8,128)(2,1)S(1)} %broadcast_select_fusion.3), channel_id=1, source_target_pairs={{0,16},{16,0},{1,17},{17,1},{2,18},{18,2},{3,19},{19,3},{4,20},{20... | collective-permute-start | bytes 1437704 | tf_op jit(solution)/shard_map/ppermute | solution.py:478
  16.0 11.1 %collective-permute-start.16 = (f32[768]{0:T(1024)S(1)}, f32[768]{0:T(1024)S(1)}, u32[]{:S(2)}, u32[]{:S(2)}) collective-permute-start(f32[768]{0:T(1024)S(1)} %reduce), channel_id=1, source_target_pairs={{0,16},{16,0},{1,17},{17,1},{2,18},{18,2},{3,19},{19,3},{4,20},{20... | collective-permute-start | bytes 9224 | tf_op jit(solution)/shard_map/ppermute | solution.py:478
  16.1 11.0 %collective-permute-start.18 = (f32[768]{0:T(1024)S(1)}, f32[768]{0:T(1024)S(1)}, u32[]{:S(2)}, u32[]{:S(2)}) collective-permute-start(f32[768]{0:T(1024)S(1)} %reduce.2), channel_id=1, source_target_pairs={{0,16},{16,0},{1,17},{17,1},{2,18},{18,2},{3,19},{19,3},{4,20},{20... | collective-permute-start | bytes 9224 | tf_op jit(solution)/shard_map/ppermute | solution.py:478
  18.2 9.0 %collective-permute-start.17 = (f32[768]{0:T(1024)S(1)}, f32[768]{0:T(1024)S(1)}, u32[]{:S(2)}, u32[]{:S(2)}) collective-permute-start(f32[768]{0:T(1024)S(1)} %reduce.1), channel_id=1, source_target_pairs={{0,16},{16,0},{1,17},{17,1},{2,18},{18,2},{3,19},{19,3},{4,20},{20... | collective-permute-start | bytes 9224 | tf_op jit(solution)/shard_map/ppermute | solution.py:478
  32.1 21.3 %collective-permute-start.1 = (bf16[48,4992]{1,0:T(8,128)(2,1)S(1)}, bf16[48,4992]{1,0:T(8,128)(2,1)S(1)}, u32[]{:S(2)}, u32[]{:S(2)}) collective-permute-start(bf16[48,4992]{1,0:T(8,128)(2,1)S(1)} %get-tuple-element.78), channel_id=1, source_target_pairs={{0,4},{1,5},{2,6},{3,7},{4,0},{5,1},{6,2},{7,3},{8,12},{9,13},{10,... | collective-permute-start | bytes 1437704 | tf_op jit(solution)/shard_map/ppermute | solution.py:431
  33.9 43.8 %collective-permute-start.2 = (bf16[48,4992]{1,0:T(8,128)(2,1)S(1)}, bf16[48,4992]{1,0:T(8,128)(2,1)S(1)}, u32[]{:S(2)}, u32[]{:S(2)}) collective-permute-start(bf16[48,4992]{1,0:T(8,128)(2,1)S(1)} %get-tuple-element.78), channel_id=1, source_target_pairs={{0,8},{1,9},{2,10},{3,11},{4,12},{5,13},{6,14},{7,15},{8,0},{9,1},... | collective-permute-start | bytes 1437704 | tf_op jit(solution)/shard_map/ppermute | solution.py:431
  36.5 74.8 %collective-permute-start.3 = (bf16[48,4992]{1,0:T(8,128)(2,1)S(1)}, bf16[48,4992]{1,0:T(8,128)(2,1)S(1)}, u32[]{:S(2)}, u32[]{:S(2)}) collective-permute-start(bf16[48,4992]{1,0:T(8,128)(2,1)S(1)} %get-tuple-element.78), channel_id=1, source_target_pairs={{0,12},{1,13},{2,14},{3,15},{4,8},{5,9},{6,10},{7,11},{8,4},{9,5},... | collective-permute-start | bytes 1437704 | tf_op jit(solution)/shard_map/ppermute | solution.py:431
  36.5 75.6 %collective-permute-start.4 = (bf16[48,4992]{1,0:T(8,128)(2,1)S(1)}, bf16[48,4992]{1,0:T(8,128)(2,1)S(1)}, u32[]{:S(2)}, u32[]{:S(2)}) collective-permute-start(bf16[48,4992]{1,0:T(8,128)(2,1)S(1)} %get-tuple-element.78), channel_id=1, source_target_pairs={{0,2},{1,3},{2,0},{3,1},{4,6},{5,7},{6,4},{7,5},{8,10},{9,11},{10,... | collective-permute-start | bytes 1437704 | tf_op jit(solution)/shard_map/ppermute | solution.py:431
  38.3 153.2 %collective-permute-start.8 = (bf16[48,4992]{1,0:T(8,128)(2,1)S(1)}, bf16[48,4992]{1,0:T(8,128)(2,1)S(1)}, u32[]{:S(2)}, u32[]{:S(2)}) collective-permute-start(bf16[48,4992]{1,0:T(8,128)(2,1)S(1)} %get-tuple-element.78), channel_id=1, source_target_pairs={{0,1},{1,0},{2,3},{3,2},{4,5},{5,4},{6,7},{7,6},{8,9},{9,8},{10,11... | collective-permute-start | bytes 1437704 | tf_op jit(solution)/shard_map/ppermute | solution.py:431
  53.3 22.7 %collective-permute-start.20 = (bf16[48,4992]{1,0:T(8,128)(2,1)S(1)}, bf16[48,4992]{1,0:T(8,128)(2,1)S(1)}, u32[]{:S(2)}, u32[]{:S(2)}) collective-permute-start(bf16[48,4992]{1,0:T(8,128)(2,1)S(1)} %get-tuple-element.76), channel_id=1, source_target_pairs={{0,4},{1,5},{2,6},{3,7},{4,0},{5,1},{6,2},{7,3},{8,12},{9,13},{10,... | collective-permute-start | bytes 1437704 | tf_op jit(solution)/shard_map/ppermute | solution.py:431
  76.0 33.8 %collective-permute-start.21 = (bf16[48,4992]{1,0:T(8,128)(2,1)S(1)}, bf16[48,4992]{1,0:T(8,128)(2,1)S(1)}, u32[]{:S(2)}, u32[]{:S(2)}) collective-permute-start(bf16[48,4992]{1,0:T(8,128)(2,1)S(1)} %get-tuple-element.76), channel_id=1, source_target_pairs={{0,8},{1,9},{2,10},{3,11},{4,12},{5,13},{6,14},{7,15},{8,0},{9,1},... | collective-permute-start | bytes 1437704 | tf_op jit(solution)/shard_map/ppermute | solution.py:431
  77.7 33.7 %collective-permute-start.22 = (bf16[48,4992]{1,0:T(8,128)(2,1)S(1)}, bf16[48,4992]{1,0:T(8,128)(2,1)S(1)}, u32[]{:S(2)}, u32[]{:S(2)}) collective-permute-start(bf16[48,4992]{1,0:T(8,128)(2,1)S(1)} %get-tuple-element.76), channel_id=1, source_target_pairs={{0,12},{1,13},{2,14},{3,15},{4,8},{5,9},{6,10},{7,11},{8,4},{9,5},... | collective-permute-start | bytes 1437704 | tf_op jit(solution)/shard_map/ppermute | solution.py:431
  109.8 13.9 %collective-permute-start.23 = (bf16[48,4992]{1,0:T(8,128)(2,1)S(1)}, bf16[48,4992]{1,0:T(8,128)(2,1)S(1)}, u32[]{:S(2)}, u32[]{:S(2)}) collective-permute-start(bf16[48,4992]{1,0:T(8,128)(2,1)S(1)} %get-tuple-element.76), channel_id=1, source_target_pairs={{0,2},{1,3},{2,0},{3,1},{4,6},{5,7},{6,4},{7,5},{8,10},{9,11},{10,... | collective-permute-start | bytes 1437704 | tf_op jit(solution)/shard_map/ppermute | solution.py:431
  111.3 80.7 %collective-permute-start.27 = (bf16[48,4992]{1,0:T(8,128)(2,1)S(1)}, bf16[48,4992]{1,0:T(8,128)(2,1)S(1)}, u32[]{:S(2)}, u32[]{:S(2)}) collective-permute-start(bf16[48,4992]{1,0:T(8,128)(2,1)S(1)} %get-tuple-element.76), channel_id=1, source_target_pairs={{0,1},{1,0},{2,3},{3,2},{4,5},{5,4},{6,7},{7,6},{8,9},{9,8},{10,11... | collective-permute-start | bytes 1437704 | tf_op jit(solution)/shard_map/ppermute | solution.py:431
  111.5 22.5 %collective-permute-start.5 = (bf16[48,4992]{1,0:T(8,128)(2,1)S(1)}, bf16[48,4992]{1,0:T(8,128)(2,1)S(1)}, u32[]{:S(2)}, u32[]{:S(2)}) collective-permute-start(bf16[48,4992]{1,0:T(8,128)(2,1)S(1)} %collective-permute-done.1), channel_id=1, source_target_pairs={{0,2},{1,3},{2,0},{3,1},{4,6},{5,7},{6,4},{7,5},{8,10},{9,11},{10,... | collective-permute-start | bytes 1437704 | tf_op jit(solution)/shard_map/ppermute | solution.py:431
  112.1 50.1 %collective-permute-start.6 = (bf16[48,4992]{1,0:T(8,128)(2,1)S(1)}, bf16[48,4992]{1,0:T(8,128)(2,1)S(1)}, u32[]{:S(2)}, u32[]{:S(2)}) collective-permute-start(bf16[48,4992]{1,0:T(8,128)(2,1)S(1)} %collective-permute-done.2), channel_id=1, source_target_pairs={{0,2},{1,3},{2,0},{3,1},{4,6},{5,7},{6,4},{7,5},{8,10},{9,11},{10,... | collective-permute-start | bytes 1437704 | tf_op jit(solution)/shard_map/ppermute | solution.py:431
  123.7 53.1 %collective-permute-start.7 = (bf16[48,4992]{1,0:T(8,128)(2,1)S(1)}, bf16[48,4992]{1,0:T(8,128)(2,1)S(1)}, u32[]{:S(2)}, u32[]{:S(2)}) collective-permute-start(bf16[48,4992]{1,0:T(8,128)(2,1)S(1)} %collective-permute-done.3), channel_id=1, source_target_pairs={{0,2},{1,3},{2,0},{3,1},{4,6},{5,7},{6,4},{7,5},{8,10},{9,11},{10,... | collective-permute-start | bytes 1437704 | tf_op jit(solution)/shard_map/ppermute | solution.py:431
  133.9 28.2 %collective-permute-start.24 = (bf16[48,4992]{1,0:T(8,128)(2,1)S(1)}, bf16[48,4992]{1,0:T(8,128)(2,1)S(1)}, u32[]{:S(2)}, u32[]{:S(2)}) collective-permute-start(bf16[48,4992]{1,0:T(8,128)(2,1)S(1)} %collective-permute-done.20), channel_id=1, source_target_pairs={{0,2},{1,3},{2,0},{3,1},{4,6},{5,7},{6,4},{7,5},{8,10},{9,11},{10,... | collective-permute-start | bytes 1437704 | tf_op jit(solution)/shard_map/ppermute | solution.py:431
  162.2 30.1 %collective-permute-start.9 = (bf16[48,4992]{1,0:T(8,128)(2,1)S(1)}, bf16[48,4992]{1,0:T(8,128)(2,1)S(1)}, u32[]{:S(2)}, u32[]{:S(2)}) collective-permute-start(bf16[48,4992]{1,0:T(8,128)(2,1)S(1)} %collective-permute-done.1), channel_id=1, source_target_pairs={{0,1},{1,0},{2,3},{3,2},{4,5},{5,4},{6,7},{7,6},{8,9},{9,8},{10,11... | collective-permute-start | bytes 1437704 | tf_op jit(solution)/shard_map/ppermute | solution.py:431
  162.2 13.5 %collective-permute-start.25 = (bf16[48,4992]{1,0:T(8,128)(2,1)S(1)}, bf16[48,4992]{1,0:T(8,128)(2,1)}, u32[]{:S(2)}, u32[]{:S(2)}) collective-permute-start(bf16[48,4992]{1,0:T(8,128)(2,1)S(1)} %collective-permute-done.21), channel_id=1, source_target_pairs={{0,2},{1,3},{2,0},{3,1},{4,6},{5,7},{6,4},{7,5},{8,10},{9,11},{10,... | collective-permute-start | bytes 1437704 | tf_op jit(solution)/shard_map/ppermute | solution.py:431
  175.7 19.1 %collective-permute-start.10 = (bf16[48,4992]{1,0:T(8,128)(2,1)S(1)}, bf16[48,4992]{1,0:T(8,128)(2,1)S(1)}, u32[]{:S(2)}, u32[]{:S(2)}) collective-permute-start(bf16[48,4992]{1,0:T(8,128)(2,1)S(1)} %collective-permute-done.2), channel_id=1, source_target_pairs={{0,1},{1,0},{2,3},{3,2},{4,5},{5,4},{6,7},{7,6},{8,9},{9,8},{10,11... | collective-permute-start | bytes 1437704 | tf_op jit(solution)/shard_map/ppermute | solution.py:431
  176.8 13.5 %collective-permute-start.26 = (bf16[48,4992]{1,0:T(8,128)(2,1)S(1)}, bf16[48,4992]{1,0:T(8,128)(2,1)}, u32[]{:S(2)}, u32[]{:S(2)}) collective-permute-start(bf16[48,4992]{1,0:T(8,128)(2,1)S(1)} %collective-permute-done.22), channel_id=1, source_target_pairs={{0,2},{1,3},{2,0},{3,1},{4,6},{5,7},{6,4},{7,5},{8,10},{9,11},{10,... | collective-permute-start | bytes 1437704 | tf_op jit(solution)/shard_map/ppermute | solution.py:431
  190.4 5.2 collective-permute-start.11
  191.5 5.0 collective-permute-start.12
  192.1 2.1 collective-permute-start.28
  192.2 2.9 collective-permute-start.29
  194.2 1.8 collective-permute-start.30
  194.9 1.9 collective-permute-start.31
  195.1 2.3 collective-permute-start.13
  195.6 2.5 collective-permute-start.14
  196.0 4.2 collective-permute-start.15
  196.5 40.2 %collective-permute-start.32 = (bf16[48,4992]{1,0:T(8,128)(2,1)S(1)}, bf16[48,4992]{1,0:T(8,128)(2,1)}, u32[]{:S(2)}, u32[]{:S(2)}) collective-permute-start(bf16[48,4992]{1,0:T(8,128)(2,1)S(1)} %collective-permute-done.24), channel_id=1, source_target_pairs={{0,1},{1,0},{2,3},{3,2},{4,5},{5,4},{6,7},{7,6},{8,9},{9,8},{10,11... | collective-permute-start | bytes 1437704 | tf_op jit(solution)/shard_map/ppermute | solution.py:431
  196.8 40.9 %collective-permute-start.33 = (bf16[48,4992]{1,0:T(8,128)(2,1)}, bf16[48,4992]{1,0:T(8,128)(2,1)}, u32[]{:S(2)}, u32[]{:S(2)}) collective-permute-start(bf16[48,4992]{1,0:T(8,128)(2,1)} %collective-permute-done.25), channel_id=1, source_target_pairs={{0,1},{1,0},{2,3},{3,2},{4,5},{5,4},{6,7},{7,6},{8,9},{9,8},{10,11... | collective-permute-start | bytes 1437704 | tf_op jit(solution)/shard_map/ppermute | solution.py:431
  197.5 41.3 %collective-permute-start.34 = (bf16[48,4992]{1,0:T(8,128)(2,1)}, bf16[48,4992]{1,0:T(8,128)(2,1)}, u32[]{:S(2)}, u32[]{:S(2)}) collective-permute-start(bf16[48,4992]{1,0:T(8,128)(2,1)} %collective-permute-done.26), channel_id=1, source_target_pairs={{0,1},{1,0},{2,3},{3,2},{4,5},{5,4},{6,7},{7,6},{8,9},{9,8},{10,11... | collective-permute-start | bytes 1437704 | tf_op jit(solution)/shard_map/ppermute | solution.py:431
  236.5 30.6 %collective-permute-start.19 = (bf16[832,768]{1,0:T(8,128)(2,1)}, bf16[832,768]{1,0:T(8,128)(2,1)S(1)}, u32[]{:S(2)}, u32[]{:S(2)}) collective-permute-start(bf16[832,768]{1,0:T(8,128)(2,1)} %get-tuple-element.41), channel_id=1, source_target_pairs={{0,16},{16,0},{1,17},{17,1},{2,18},{18,2},{3,19},{19,3},{4,20},{20... | collective-permute-start | bytes 3833864 | tf_op jit(solution)/shard_map/ppermute | solution.py:478
  241.7 25.4 %copy-start.1 = (bf16[4,208,768]{2,1,0:T(8,128)(2,1)S(1)}, bf16[4,208,768]{2,1,0:T(8,128)(2,1)}, u32[]{:S(2)}) copy-start(bf16[4,208,768]{2,1,0:T(8,128)(2,1)} %pad.7.clone) | copy-start | bytes 3833860
  241.8 25.4 %copy-start.14 = (bf16[832,768]{1,0:T(8,128)(2,1)S(1)}, bf16[832,768]{1,0:T(8,128)(2,1)}, u32[]{:S(2)}) copy-start(bf16[832,768]{1,0:T(8,128)(2,1)} %get-tuple-element.41) | copy-start | bytes 3833860
  304.3 90.9 %collective-permute-start.35 = (bf16[832,768]{1,0:T(8,128)(2,1)}, bf16[832,768]{1,0:T(8,128)(2,1)S(1)}, u32[]{:S(2)}, u32[]{:S(2)}) collective-permute-start(bf16[832,768]{1,0:T(8,128)(2,1)} %get-tuple-element.44), channel_id=1, source_target_pairs={{0,16},{1,17},{2,18},{3,19},{4,20},{5,21},{6,22},{7,23},{8,24},{9,... | collective-permute-start | bytes 3833864 | tf_op jit(solution)/shard_map/ppermute | solution.py:481
  323.4 18.8 %slice-start = ((s8[4718592]{0:T(1024)(128)(4,1)}), s8[4194304]{0:T(1024)(128)(4,1)S(1)}, s32[]{:S(2)}) async-start(s8[4718592]{0:T(1024)(128)(4,1)} %bitcast.209), calls=%async_computation | async-start | bytes 8388608
  323.4 18.8 %slice-start.1 = ((s8[4718592]{0:T(1024)(128)(4,1)}), s8[524288]{0:T(1024)(128)(4,1)S(1)}, s32[]{:S(2)}) async-start(s8[4718592]{0:T(1024)(128)(4,1)} %bitcast.209), calls=%async_computation.1 | async-start | bytes 1048576
  342.1 29.8 %collective-permute-start.36 = (bf16[832,768]{1,0:T(8,128)(2,1)}, bf16[832,768]{1,0:T(8,128)(2,1)S(1)}, u32[]{:S(2)}, u32[]{:S(2)}) collective-permute-start(bf16[832,768]{1,0:T(8,128)(2,1)} %get-tuple-element.53.mine_ref), channel_id=1, source_target_pairs={{0,16},{16,0},{1,17},{17,1},{2,18},{18,2},{3,19},{19,3},{4,20},{20... | collective-permute-start | bytes 3833864 | tf_op jit(solution)/shard_map/ppermute | solution.py:478
  345.5 140.5 %collective-permute-start.53 = (bf16[4,2,48,3072]{3,2,0,1:T(8,128)(2,1)}, bf16[4,2,48,3072]{3,2,0,1:T(8,128)(2,1)}, u32[]{:S(2)}, u32[]{:S(2)}) collective-permute-start(bf16[4,2,48,3072]{3,2,0,1:T(8,128)(2,1)} %bitcast.192), channel_id=1, source_target_pairs={{0,1},{1,0},{2,3},{3,2},{4,5},{5,4},{6,7},{7,6},{8,9},{9,8},{10,11... | collective-permute-start | bytes 7077896 | tf_op jit(solution)/shard_map/ppermute | solution.py:431
  348.1 75.9 %collective-permute-start.48 = (bf16[4,2,48,1920]{3,2,0,1:T(8,128)(2,1)}, bf16[4,2,48,1920]{3,2,0,1:T(8,128)(2,1)}, u32[]{:S(2)}, u32[]{:S(2)}) collective-permute-start(bf16[4,2,48,1920]{3,2,0,1:T(8,128)(2,1)} %bitcast.194), channel_id=1, source_target_pairs={{0,1},{1,0},{2,3},{3,2},{4,5},{5,4},{6,7},{7,6},{8,9},{9,8},{10,11... | collective-permute-start | bytes 4423688 | tf_op jit(solution)/shard_map/ppermute | solution.py:431
  400.5 114.1 %collective-permute-start.43 = (bf16[4,2,48,3072]{3,2,0,1:T(8,128)(2,1)}, bf16[4,2,48,3072]{3,2,0,1:T(8,128)(2,1)}, u32[]{:S(2)}, u32[]{:S(2)}) collective-permute-start(bf16[4,2,48,3072]{3,2,0,1:T(8,128)(2,1)} %bitcast.193), channel_id=1, source_target_pairs={{0,1},{1,0},{2,3},{3,2},{4,5},{5,4},{6,7},{7,6},{8,9},{9,8},{10,11... | collective-permute-start | bytes 7077896 | tf_op jit(solution)/shard_map/ppermute | solution.py:431
  423.5 67.7 %collective-permute-start.38 = (bf16[4,2,48,1920]{3,2,0,1:T(8,128)(2,1)}, bf16[4,2,48,1920]{3,2,0,1:T(8,128)(2,1)}, u32[]{:S(2)}, u32[]{:S(2)}) collective-permute-start(bf16[4,2,48,1920]{3,2,0,1:T(8,128)(2,1)} %bitcast.195), channel_id=1, source_target_pairs={{0,1},{1,0},{2,3},{3,2},{4,5},{5,4},{6,7},{7,6},{8,9},{9,8},{10,11... | collective-permute-start | bytes 4423688 | tf_op jit(solution)/shard_map/ppermute | solution.py:431
  428.9 53.6 %collective-permute-start.49 = (bf16[4,48,1920]{2,1,0:T(8,128)(2,1)}, bf16[4,48,1920]{2,1,0:T(8,128)(2,1)S(1)}, u32[]{:S(2)}, u32[]{:S(2)}) collective-permute-start(bf16[4,48,1920]{2,1,0:T(8,128)(2,1)} %dynamic-slice_bitcast_fusion.2), channel_id=1, source_target_pairs={{0,2},{1,3},{2,0},{3,1},{4,6},{5,7},{6,4},{7,5},{8,10},{9,11},{10,... | collective-permute-start | bytes 2211848 | tf_op jit(solution)/shard_map/ppermute | solution.py:431
  483.9 11.5 %collective-permute-start.52 = (bf16[48,1920]{1,0:T(8,128)(2,1)S(1)}, bf16[48,1920]{1,0:T(8,128)(2,1)S(1)}, u32[]{:S(2)}, u32[]{:S(2)}) collective-permute-start(bf16[48,1920]{1,0:T(8,128)(2,1)S(1)} %get-tuple-element.105), channel_id=1, source_target_pairs={{0,12},{1,13},{2,14},{3,15},{4,8},{5,9},{6,10},{7,11},{8,4},{9,5},... | collective-permute-start | bytes 552968 | tf_op jit(solution)/shard_map/ppermute | solution.py:431
  485.6 15.9 %collective-permute-start.51 = (bf16[48,1920]{1,0:T(8,128)(2,1)S(1)}, bf16[48,1920]{1,0:T(8,128)(2,1)S(1)}, u32[]{:S(2)}, u32[]{:S(2)}) collective-permute-start(bf16[48,1920]{1,0:T(8,128)(2,1)S(1)} %get-tuple-element.106), channel_id=1, source_target_pairs={{0,8},{1,9},{2,10},{3,11},{4,12},{5,13},{6,14},{7,15},{8,0},{9,1},... | collective-permute-start | bytes 552968 | tf_op jit(solution)/shard_map/ppermute | solution.py:431
  486.0 16.8 %collective-permute-start.50 = (bf16[48,1920]{1,0:T(8,128)(2,1)S(1)}, bf16[48,1920]{1,0:T(8,128)(2,1)S(1)}, u32[]{:S(2)}, u32[]{:S(2)}) collective-permute-start(bf16[48,1920]{1,0:T(8,128)(2,1)S(1)} %get-tuple-element.104), channel_id=1, source_target_pairs={{0,4},{1,5},{2,6},{3,7},{4,0},{5,1},{6,2},{7,3},{8,12},{9,13},{10,... | collective-permute-start | bytes 552968 | tf_op jit(solution)/shard_map/ppermute | solution.py:431
  493.0 19.8 %collective-permute-start.39 = (bf16[4,48,1920]{2,1,0:T(8,128)(2,1)S(1)}, bf16[4,48,1920]{2,1,0:T(8,128)(2,1)S(1)}, u32[]{:S(2)}, u32[]{:S(2)}) collective-permute-start(bf16[4,48,1920]{2,1,0:T(8,128)(2,1)S(1)} %dynamic-slice_bitcast_fusion.3), channel_id=1, source_target_pairs={{0,2},{1,3},{2,0},{3,1},{4,6},{5,7},{6,4},{7,5},{8,10},{9,11},{10,... | collective-permute-start | bytes 2211848 | tf_op jit(solution)/shard_map/ppermute | solution.py:431
  495.4 94.5 %collective-permute-start.37 = (bf16[832,768]{1,0:T(8,128)(2,1)S(1)}, bf16[832,768]{1,0:T(8,128)(2,1)}, u32[]{:S(2)}, u32[]{:S(2)}) collective-permute-start(bf16[832,768]{1,0:T(8,128)(2,1)S(1)} %copy-done.12), channel_id=1, source_target_pairs={{16,0},{17,1},{18,2},{19,3},{20,4},{21,5},{22,6},{23,7},{24,8},{25... | collective-permute-start | bytes 3833864 | tf_op jit(solution)/shard_map/ppermute | solution.py:481
  501.5 33.8 %collective-permute-start.54 = (bf16[4,48,3072]{2,1,0:T(8,128)(2,1)S(1)}, bf16[4,48,3072]{2,1,0:T(8,128)(2,1)S(1)}, u32[]{:S(2)}, u32[]{:S(2)}) collective-permute-start(bf16[4,48,3072]{2,1,0:T(8,128)(2,1)S(1)} %dynamic-slice_bitcast_fusion), channel_id=1, source_target_pairs={{0,2},{1,3},{2,0},{3,1},{4,6},{5,7},{6,4},{7,5},{8,10},{9,11},{10,... | collective-permute-start | bytes 3538952 | tf_op jit(solution)/shard_map/ppermute | solution.py:431
  513.0 24.8 %collective-permute-start.42 = (bf16[48,1920]{1,0:T(8,128)(2,1)S(1)}, bf16[48,1920]{1,0:T(8,128)(2,1)S(1)}, u32[]{:S(2)}, u32[]{:S(2)}) collective-permute-start(bf16[48,1920]{1,0:T(8,128)(2,1)S(1)} %get-tuple-element.102), channel_id=1, source_target_pairs={{0,12},{1,13},{2,14},{3,15},{4,8},{5,9},{6,10},{7,11},{8,4},{9,5},... | collective-permute-start | bytes 552968 | tf_op jit(solution)/shard_map/ppermute | solution.py:431
  514.6 24.8 %collective-permute-start.41 = (bf16[48,1920]{1,0:T(8,128)(2,1)S(1)}, bf16[48,1920]{1,0:T(8,128)(2,1)S(1)}, u32[]{:S(2)}, u32[]{:S(2)}) collective-permute-start(bf16[48,1920]{1,0:T(8,128)(2,1)S(1)} %get-tuple-element.103), channel_id=1, source_target_pairs={{0,8},{1,9},{2,10},{3,11},{4,12},{5,13},{6,14},{7,15},{8,0},{9,1},... | collective-permute-start | bytes 552968 | tf_op jit(solution)/shard_map/ppermute | solution.py:431
  514.6 24.8 %collective-permute-start.40 = (bf16[48,1920]{1,0:T(8,128)(2,1)S(1)}, bf16[48,1920]{1,0:T(8,128)(2,1)S(1)}, u32[]{:S(2)}, u32[]{:S(2)}) collective-permute-start(bf16[48,1920]{1,0:T(8,128)(2,1)S(1)} %get-tuple-element.101), channel_id=1, source_target_pairs={{0,4},{1,5},{2,6},{3,7},{4,0},{5,1},{6,2},{7,3},{8,12},{9,13},{10,... | collective-permute-start | bytes 552968 | tf_op jit(solution)/shard_map/ppermute | solution.py:431
  535.2 25.0 %collective-permute-start.44 = (bf16[4,48,3072]{2,1,0:T(8,128)(2,1)S(1)}, bf16[4,48,3072]{2,1,0:T(8,128)(2,1)S(1)}, u32[]{:S(2)}, u32[]{:S(2)}) collective-permute-start(bf16[4,48,3072]{2,1,0:T(8,128)(2,1)S(1)} %dynamic-slice_bitcast_fusion.1), channel_id=1, source_target_pairs={{0,2},{1,3},{2,0},{3,1},{4,6},{5,7},{6,4},{7,5},{8,10},{9,11},{10,... | collective-permute-start | bytes 3538952 | tf_op jit(solution)/shard_map/ppermute | solution.py:431
  537.8 24.6 %collective-permute-start.57 = (bf16[48,3072]{1,0:T(8,128)(2,1)S(1)}, bf16[48,3072]{1,0:T(8,128)(2,1)S(1)}, u32[]{:S(2)}, u32[]{:S(2)}) collective-permute-start(bf16[48,3072]{1,0:T(8,128)(2,1)S(1)} %get-tuple-element.91), channel_id=1, source_target_pairs={{0,12},{1,13},{2,14},{3,15},{4,8},{5,9},{6,10},{7,11},{8,4},{9,5},... | collective-permute-start | bytes 884744 | tf_op jit(solution)/shard_map/ppermute | solution.py:431
  539.4 30.6 %collective-permute-start.56 = (bf16[48,3072]{1,0:T(8,128)(2,1)S(1)}, bf16[48,3072]{1,0:T(8,128)(2,1)S(1)}, u32[]{:S(2)}, u32[]{:S(2)}) collective-permute-start(bf16[48,3072]{1,0:T(8,128)(2,1)S(1)} %get-tuple-element.92), channel_id=1, source_target_pairs={{0,8},{1,9},{2,10},{3,11},{4,12},{5,13},{6,14},{7,15},{8,0},{9,1},... | collective-permute-start | bytes 884744 | tf_op jit(solution)/shard_map/ppermute | solution.py:431
  539.4 30.6 %collective-permute-start.55 = (bf16[48,3072]{1,0:T(8,128)(2,1)S(1)}, bf16[48,3072]{1,0:T(8,128)(2,1)S(1)}, u32[]{:S(2)}, u32[]{:S(2)}) collective-permute-start(bf16[48,3072]{1,0:T(8,128)(2,1)S(1)} %get-tuple-element.90), channel_id=1, source_target_pairs={{0,4},{1,5},{2,6},{3,7},{4,0},{5,1},{6,2},{7,3},{8,12},{9,13},{10,... | collective-permute-start | bytes 884744 | tf_op jit(solution)/shard_map/ppermute | solution.py:431
  560.7 11.8 %collective-permute-start.47 = (bf16[48,3072]{1,0:T(8,128)(2,1)S(1)}, bf16[48,3072]{1,0:T(8,128)(2,1)S(1)}, u32[]{:S(2)}, u32[]{:S(2)}) collective-permute-start(bf16[48,3072]{1,0:T(8,128)(2,1)S(1)} %get-tuple-element.88), channel_id=1, source_target_pairs={{0,12},{1,13},{2,14},{3,15},{4,8},{5,9},{6,10},{7,11},{8,4},{9,5},... | collective-permute-start | bytes 884744 | tf_op jit(solution)/shard_map/ppermute | solution.py:431
  562.3 23.7 %collective-permute-start.46 = (bf16[48,3072]{1,0:T(8,128)(2,1)S(1)}, bf16[48,3072]{1,0:T(8,128)(2,1)S(1)}, u32[]{:S(2)}, u32[]{:S(2)}) collective-permute-start(bf16[48,3072]{1,0:T(8,128)(2,1)S(1)} %get-tuple-element.89), channel_id=1, source_target_pairs={{0,8},{1,9},{2,10},{3,11},{4,12},{5,13},{6,14},{7,15},{8,0},{9,1},... | collective-permute-start | bytes 884744 | tf_op jit(solution)/shard_map/ppermute | solution.py:431
  570.0 16.1 %collective-permute-start.45 = (bf16[48,3072]{1,0:T(8,128)(2,1)S(1)}, bf16[48,3072]{1,0:T(8,128)(2,1)S(1)}, u32[]{:S(2)}, u32[]{:S(2)}) collective-permute-start(bf16[48,3072]{1,0:T(8,128)(2,1)S(1)} %get-tuple-element.87), channel_id=1, source_target_pairs={{0,4},{1,5},{2,6},{3,7},{4,0},{5,1},{6,2},{7,3},{8,12},{9,13},{10,... | collective-permute-start | bytes 884744 | tf_op jit(solution)/shard_map/ppermute | solution.py:431
  586.3 12.1 %collective-permute-start.58 = (bf16[48,4992]{1,0:T(8,128)(2,1)S(1)}, bf16[48,4992]{1,0:T(8,128)(2,1)S(1)}, u32[]{:S(2)}, u32[]{:S(2)}) collective-permute-start(bf16[48,4992]{1,0:T(8,128)(2,1)S(1)} %select_convert_fusion), channel_id=1, source_target_pairs={{0,16},{16,0},{1,17},{17,1},{2,18},{18,2},{3,19},{19,3},{4,20},{20... | collective-permute-start | bytes 1437704 | tf_op jit(solution)/shard_map/ppermute | solution.py:478
  (19 other events, 125.3 us)

commit v2 on v1

--- a/solution.py
+++ b/solution.py
@@ -16,6 +16,8 @@
 TILE = 256
 BF = jnp.bfloat16
 F32 = jnp.float32
+SPLIT = D + 3 * HALF
+ANYWHERE = pl.BlockSpec(memory_space=pl.ANY)
 C0 = 0.7978845608028654
 C1 = 0.044715
 
@@ -50,14 +52,42 @@
 
 def params(steps):
     return pltpu.CompilerParams(
-        dimension_semantics=("arbitrary",) * steps, vmem_limit_bytes=56 * 1024 * 1024
+        dimension_semantics=("arbitrary",) * steps, vmem_limit_bytes=20 * 1024 * 1024
     )
 
 
-def attention_forward_kernel(
-    tokens, sec, x_ref, w_ref, ln_ref, gain_ref, normed_ref, qk_ref, v_ref, r_ref, pt_ref, mixed_ref, part_ref
-):
-    section = sec[0]
+def copies(place, pieces, columns, dest_ref, sems):
+    made = []
+    for step, piece in enumerate(pieces):
+        rows = piece.shape[0]
+        at = pl.ds(pl.multiple_of((place[1] ^ step) * rows, rows), rows)
+        made.append(pltpu.make_async_copy(piece.at[:, columns], dest_ref.at[at, :], sems.at[step]))
+    return made
+
+
+def attention_forward_kernel(tokens, count, place, *refs):
+    pieces = refs[:count]
+    (
+        x_ref,
+        ln_ref,
+        gain_ref,
+        normed_ref,
+        qk_ref,
+        v_ref,
+        r_ref,
+        pt_ref,
+        mixed_ref,
+        part_ref,
+        w_ref,
+        sems,
+    ) = refs[count:]
+    section = place[0]
+
+    @pl.when(pl.program_id(0) == 0)
+    def _():
+        for copy in copies(place, pieces, slice(0, SPLIT), w_ref, sems):
+            copy.start()
+
     x = x_ref[...].astype(F32)
     rows = x.shape[0]
     pad = rows // 2
@@ -65,6 +95,12 @@
     spread = jnp.mean(centred * centred, axis=-1, keepdims=True)
     normed = (centred * lax.rsqrt(spread + EPSILON) * ln_ref[...]).astype(BF)
     normed_ref[...] = normed
+
+    @pl.when(pl.program_id(0) == 0)
+    def _():
+        for copy in copies(place, pieces, slice(0, SPLIT), w_ref, sems):
+            copy.wait()
+
     qkv = dot(normed, w_ref[:, D:])
     qk = qkv[:, :D]
     centred = qk - head_means(qk)
@@ -95,7 +131,7 @@
     part_ref[...] = dot(mixed_ref[...], proj).astype(BF)
 
 
-def attention_forward(tokens, section, x, weights, ln_gain, qk_gain):
+def attention_forward(tokens, place, x, pieces, ln_gain, qk_gain):
     rows = x.shape[0]
     images = rows // pad_of(tokens)
     pad = pad_of(tokens)
@@ -103,11 +139,11 @@
     row = lambda width: pl.BlockSpec((step, width), lambda i, s: (i, 0))
     full = lambda shape: pl.BlockSpec(shape, lambda i, s: (0, 0), pipeline_mode=pl.Buffered(1))
     return pl.pallas_call(
-        partial(attention_forward_kernel, tokens),
+        partial(attention_forward_kernel, tokens, len(pieces)),
         grid_spec=pltpu.PrefetchScalarGridSpec(
             num_scalar_prefetch=1,
             grid=(images // 2,),
-            in_specs=[row(D), full((D, D + 3 * HALF)), full((1, D)), full((1, D))],
+            in_specs=[ANYWHERE] * len(pieces) + [row(D), full((1, D)), full((1, D))],
             out_specs=[
                 row(D),
                 row(D),
@@ -116,6 +152,10 @@
                 pl.BlockSpec((2, 2 * PAIRS, pad, pad), lambda i, s: (i, 0, 0, 0)),
                 row(HALF),
                 row(D),
+            ],
+            scratch_shapes=[
+                pltpu.VMEM((D, SPLIT), BF),
+                pltpu.SemaphoreType.DMA((len(pieces),)),
             ],
         ),
         out_shape=[
@@ -134,19 +174,47 @@
             transcendentals=images * 6 * pad * pad,
         ),
         name="attention_forward",
-    )(section, x, weights, ln_gain, qk_gain)
-
-
-def feed_forward_kernel(steps, normed_ref, up_ref, down_ref, part_ref, hidden_ref, slope_ref, out_ref, acc_ref):
+    )(place, *pieces, x, ln_gain, qk_gain)
+
+
+def feed_copies(place, pieces, units, up_ref, down_ref, sems):
+    base = pieces[0].shape[1] - 2 * units
+    ups = copies(place, pieces, slice(base, base + units), up_ref, sems.at[0])
+    downs = []
+    for part in range(units // D):
+        columns = slice(base + units + part * D, base + units + (part + 1) * D)
+        downs += copies(place, pieces, columns, down_ref.at[part], sems.at[1 + part])
+    return ups, downs
+
+
+def feed_tiles(step):
+    across = D // TILE
+    columns = pl.ds(pl.multiple_of(step * TILE, TILE), TILE)
+    return columns, step // across, pl.ds(pl.multiple_of((step % across) * TILE, TILE), TILE)
+
+
+def feed_forward_kernel(steps, count, place, *refs):
+    pieces = refs[:count]
+    normed_ref, part_ref, hidden_ref, slope_ref, out_ref, acc_ref, up_ref, down_ref, sems = refs[count:]
     step = pl.program_id(0)
-    up = dot(normed_ref[...], up_ref[...])
+    columns, part, rows = feed_tiles(step)
+
+    @pl.when(step == 0)
+    def _():
+        ups, downs = feed_copies(place, pieces, steps * TILE, up_ref, down_ref, sems)
+        for copy in ups + downs:
+            copy.start()
+        for copy in ups + downs:
+            copy.wait()
+
+    up = dot(normed_ref[...], up_ref[:, columns])
     square = up * up
     tanh = jnp.tanh(C0 * up * (1.0 + C1 * square))
     hidden = (0.5 * up * (1.0 + tanh)).astype(BF)
     slope = 0.5 * (1.0 + tanh) + (0.5 * C0) * up * (1.0 - tanh * tanh) * (1.0 + (3.0 * C1) * square)
     hidden_ref[...] = hidden
     slope_ref[...] = slope.astype(BF)
-    term = dot(hidden, down_ref[...])
+    term = dot(hidden, down_ref[part, rows, :])
 
     @pl.when(step == 0)
     def _():
@@ -161,32 +229,34 @@
         out_ref[...] = acc_ref[...].astype(BF)
 
 
-def up_spec():
-    return pl.BlockSpec((D, TILE), lambda j: (0, j))
-
-
-def down_spec(units):
-    across = D // TILE
-    return pl.BlockSpec((TILE, D), lambda j: (j % across, units // D + j // across))
-
-
-def feed_forward(normed, weights, part):
+def feed_scratch(rows, units, count):
+    return [
+        pltpu.VMEM((rows, D), F32),
+        pltpu.VMEM((D, units), BF),
+        pltpu.VMEM((units // D, D, D), BF),
+        pltpu.SemaphoreType.DMA((1 + units // D, count)),
+    ]
+
+
+def feed_forward(place, units, normed, pieces, part):
     rows = normed.shape[0]
-    units = weights.shape[1] // 2
     steps = units // TILE
-    whole = pl.BlockSpec((rows, D), lambda j: (0, 0))
-    tile = pl.BlockSpec((rows, TILE), lambda j: (0, j))
+    whole = pl.BlockSpec((rows, D), lambda j, s: (0, 0))
+    tile = pl.BlockSpec((rows, TILE), lambda j, s: (0, j))
     return pl.pallas_call(
-        partial(feed_forward_kernel, steps),
-        grid=(steps,),
-        in_specs=[whole, up_spec(), down_spec(units), whole],
-        out_specs=[tile, tile, whole],
+        partial(feed_forward_kernel, steps, len(pieces)),
+        grid_spec=pltpu.PrefetchScalarGridSpec(
+            num_scalar_prefetch=1,
+            grid=(steps,),
+            in_specs=[ANYWHERE] * len(pieces) + [whole, whole],
+            out_specs=[tile, tile, whole],
+            scratch_shapes=feed_scratch(rows, units, len(pieces)),
+        ),
         out_shape=[
             jax.ShapeDtypeStruct((rows, units), BF),
             jax.ShapeDtypeStruct((rows, units), BF),
             jax.ShapeDtypeStruct((rows, D), BF),
         ],
-        scratch_shapes=[pltpu.VMEM((rows, D), F32)],
         compiler_params=params(1),
         cost_estimate=pl.CostEstimate(
             flops=4 * rows * D * units,
@@ -194,19 +264,29 @@
             transcendentals=rows * units,
         ),
         name="feed_forward",
-    )(normed, weights, weights, part)
-
-
-def feed_backward_kernel(steps, g_ref, normed_ref, up_ref, down_ref, hidden_ref, slope_ref, grad_ref, out_ref, acc_ref):
+    )(place, *pieces, normed, part)
+
+
+def feed_backward_kernel(steps, count, place, *refs):
+    pieces = refs[:count]
+    g_ref, normed_ref, hidden_ref, slope_ref, grad_ref, out_ref, acc_ref, up_ref, down_ref, sems = refs[count:]
     step = pl.program_id(0)
+    columns, part, rows = feed_tiles(step)
+
+    @pl.when(step == 0)
+    def _():
+        ups, downs = feed_copies(place, pieces, steps * TILE, up_ref, down_ref, sems)
+        for copy in downs + ups:
+            copy.start()
+        for copy in downs + ups:
+            copy.wait()
+
     grad = g_ref[...]
-    across = D // TILE
-    d_up = (slope_ref[...].astype(F32) * dot_nt(grad, down_ref[...])).astype(BF)
-    row = pl.multiple_of((step % across) * TILE, TILE)
-    column = pl.multiple_of(steps * TILE + (step // across) * D, TILE)
-    grad_ref[pl.ds(row, TILE), pl.ds(column, D)] = dot_tn(hidden_ref[...], grad).astype(BF)
-    grad_ref[:, pl.ds(pl.multiple_of(step * TILE, TILE), TILE)] = dot_tn(normed_ref[...], d_up).astype(BF)
-    term = dot_nt(d_up, up_ref[...])
+    d_up = (slope_ref[...].astype(F32) * dot_nt(grad, down_ref[part, rows, :])).astype(BF)
+    there = pl.ds(pl.multiple_of(steps * TILE + part * D, D), D)
+    grad_ref[rows, there] = dot_tn(hidden_ref[...], grad).astype(BF)
+    grad_ref[:, columns] = dot_tn(normed_ref[...], d_up).astype(BF)
+    term = dot_nt(d_up, up_ref[:, columns])
 
     @pl.when(step == 0)
     def _():
@@ -221,22 +301,24 @@
         out_ref[...] = acc_ref[...].astype(BF)
 
 
-def feed_backward(grad, normed, weights, hidden, slope):
+def feed_backward(place, units, grad, normed, pieces, hidden, slope):
     rows = normed.shape[0]
-    units = weights.shape[1] // 2
     steps = units // TILE
-    whole = pl.BlockSpec((rows, D), lambda j: (0, 0))
-    tile = pl.BlockSpec((rows, TILE), lambda j: (0, j))
+    whole = pl.BlockSpec((rows, D), lambda j, s: (0, 0))
+    tile = pl.BlockSpec((rows, TILE), lambda j, s: (0, j))
     return pl.pallas_call(
-        partial(feed_backward_kernel, steps),
-        grid=(steps,),
-        in_specs=[whole, whole, up_spec(), down_spec(units), tile, tile],
-        out_specs=[pl.BlockSpec((D, 2 * units), lambda j: (0, 0)), whole],
+        partial(feed_backward_kernel, steps, len(pieces)),
+        grid_spec=pltpu.PrefetchScalarGridSpec(
+            num_scalar_prefetch=1,
+            grid=(steps,),
+            in_specs=[ANYWHERE] * len(pieces) + [whole, whole, tile, tile],
+            out_specs=[pl.BlockSpec((D, 2 * units), lambda j, s: (0, 0)), whole],
+            scratch_shapes=feed_scratch(rows, units, len(pieces)),
+        ),
         out_shape=[
             jax.ShapeDtypeStruct((D, 2 * units), BF),
             jax.ShapeDtypeStruct((rows, D), BF),
         ],
-        scratch_shapes=[pltpu.VMEM((rows, D), F32)],
         compiler_params=params(1),
         cost_estimate=pl.CostEstimate(
             flops=8 * rows * D * units,
@@ -244,39 +326,44 @@
             transcendentals=0,
         ),
         name="feed_backward",
-    )(grad, normed, weights, weights, hidden, slope)
-
-
-def attention_backward_kernel(
-    steps,
-    sec,
-    g_ref,
-    w_ref,
-    gain_ref,
-    inverse_ref,
-    normed_ref,
-    qk_ref,
-    v_ref,
-    r_ref,
-    pt_ref,
-    mixed_ref,
-    ff_ref,
-    grad_ref,
-    out_ref,
-    sums_ref,
-    qkv_acc,
-    proj_acc,
-    d_qk,
-    d_qkv,
-):
+    )(place, *pieces, grad, normed, hidden, slope)
+
+
+def attention_backward_kernel(steps, count, place, *refs):
+    pieces = refs[:count]
+    (
+        g_ref,
+        gain_ref,
+        inverse_ref,
+        normed_ref,
+        qk_ref,
+        v_ref,
+        r_ref,
+        pt_ref,
+        mixed_ref,
+        ff_ref,
+        grad_ref,
+        out_ref,
+        sums_ref,
+        qkv_acc,
+        proj_acc,
+        d_qk,
+        d_qkv,
+        w_ref,
+        sems,
+    ) = refs[count:]
     step = pl.program_id(0)
-    section = sec[0]
+    section = place[0]
     rows = g_ref.shape[0]
     pad = rows // 2
 
     @pl.when(step == 0)
     def _():
+        for copy in copies(place, pieces, slice(0, SPLIT), w_ref, sems):
+            copy.start()
         sums_ref[...] = jnp.zeros_like(sums_ref)
+        for copy in copies(place, pieces, slice(0, SPLIT), w_ref, sems):
+            copy.wait()
 
     grad = g_ref[...]
     here = pl.ds(pl.multiple_of(section * HALF, HALF), HALF)
@@ -339,23 +426,23 @@
         grad_ref[:, D:] = qkv_acc[...].astype(BF)
 
 
-def attention_backward(tokens, section, grad, weights, qk_gain, normed, qk, v, r, pt, mixed, ff):
+def attention_backward(tokens, place, grad, pieces, qk_gain, normed, qk, v, r, pt, mixed, ff):
     rows = normed.shape[0]
     pad = pad_of(tokens)
     images = rows // pad
     step = 2 * pad
     steps = images // 2
-    width = weights.shape[1]
+    width = SPLIT
     row = lambda columns: pl.BlockSpec((step, columns), lambda i, s: (i, 0))
     full = lambda shape: pl.BlockSpec(shape, lambda i, s: (0, 0), pipeline_mode=pl.Buffered(1))
     return pl.pallas_call(
-        partial(attention_backward_kernel, steps),
+        partial(attention_backward_kernel, steps, len(pieces)),
         grid_spec=pltpu.PrefetchScalarGridSpec(
             num_scalar_prefetch=1,
             grid=(steps,),
-            in_specs=[
-                row(D),
-                full((D, width)),
+            in_specs=[ANYWHERE] * len(pieces)
+            + [
+                row(D),
                 full((1, D)),
                 full((1, D)),
                 row(D),
@@ -376,6 +463,8 @@
                 pltpu.VMEM((HALF, D), F32),
                 pltpu.VMEM((step, D), F32),
                 pltpu.VMEM((step, 3 * HALF), BF),
+                pltpu.VMEM((D, SPLIT), BF),
+                pltpu.SemaphoreType.DMA((len(pieces),)),
             ],
         ),
         out_shape=[
@@ -390,7 +479,7 @@
             transcendentals=0,
         ),
         name="attention_backward",
-    )(section, grad, weights, qk_gain, 1.0 / qk_gain, normed, qk, v, r, pt, mixed, ff)
+    )(place, *pieces, grad, qk_gain, 1.0 / qk_gain, normed, qk, v, r, pt, mixed, ff)
 
 
 def norm_backward_kernel(g_ref, x_ref, mine_ref, theirs_ref, ln_ref, out_ref):
@@ -431,35 +520,69 @@
     return lax.ppermute(value, "dp", [(source, source ^ step) for source in range(count)])
 
 
-def gather_rows(shard):
+def after(value, *others):
+    return lax.optimization_barrier((value,) + others)[0]
+
+
+def gather_far(shard):
     count = lax.axis_size("dp")
+    return [shard] + [relative(shard, 4 * far) for far in range(1, count // 4)]
+
+
+def gather_near(quads):
+    nears = [relative(piece, 2) for piece in quads]
+    pieces = []
+    for left, right in zip(quads, nears):
+        pieces += [left, relative(left, 1), right, relative(right, 1)]
+    rows, width = pieces[0].shape
+    if rows % 16 == 0:
+        return pieces
     me = lax.axis_index("dp")
-    quads = [shard] + [relative(shard, 4 * far) for far in range(1, count // 4)]
-    pieces = {4 * far: piece for far, piece in enumerate(quads)}
-    pieces.update({4 * far + 2: relative(piece, 2) for far, piece in enumerate(quads)})
-    pieces.update({step + 1: relative(piece, 1) for step, piece in list(pieces.items())})
-    whole = jnp.zeros((count,) + shard.shape, shard.dtype)
-    for step, piece in pieces.items():
+    whole = jnp.zeros((len(pieces), rows, width), BF)
+    for step, piece in enumerate(pieces):
         whole = lax.dynamic_update_slice(whole, piece[None], (me ^ step, 0, 0))
-    return whole.reshape(count * shard.shape[0], shard.shape[1])
+    return [whole.reshape(len(pieces) * rows, width)]
 
 
 def add_low(left, right):
     return (left.astype(F32) + right.astype(F32)).astype(BF)
 
 
-def scatter_rows(terms):
+def pick(value, at, axis):
+    return lax.dynamic_index_in_dim(value, at, axis, keepdims=False)
+
+
+def coordinates():
+    me = lax.axis_index("dp")
+    return me % 2, (me // 2) % 2, me // 4
+
+
+def scatter_core(terms):
     count = lax.axis_size("dp")
-    me = lax.axis_index("dp")
-    core, near, far = me % 2, (me // 2) % 2, me // 4
+    core, _, _ = coordinates()
     rows, width = terms.shape
     shaped = terms.reshape(count // 4, 2, 2, rows // count, width)
-    pick = lambda value, at, axis: lax.dynamic_index_in_dim(value, at, axis, keepdims=False)
-    total = add_low(pick(shaped, core, 2), relative(pick(shaped, 1 - core, 2), 1))
-    total = add_low(pick(total, near, 1), relative(pick(total, 1 - near, 1), 2))
-    result = pick(total, far, 0).astype(F32)
+    return pick(shaped, core, 2), pick(shaped, 1 - core, 2)
+
+
+def scatter_near(total):
+    _, near, _ = coordinates()
+    return pick(total, near, 1), pick(total, 1 - near, 1)
+
+
+def scatter_far(total):
+    count = lax.axis_size("dp")
+    _, _, far = coordinates()
+    terms = [pick(total, far, 0)]
     for step in range(1, count // 4):
-        result = result + relative(pick(total, far ^ step, 0), 4 * step).astype(F32)
+        terms.append(relative(pick(total, far ^ step, 0), 4 * step))
+    return terms
+
+
+def add_all(terms):
+    result = terms[0].astype(F32)
+    for term in terms[1:]:
+        result = result + term.astype(F32)
     return result
 
 
@@ -467,7 +590,7 @@
     count = lax.axis_size("dp")
     section = lax.axis_index("section")
     first = section == 0
-    scalar = section.astype(jnp.int32).reshape(1)
+    me = lax.axis_index("dp")
     number, tokens, _ = images.shape
     pad = pad_of(tokens)
     rows = w_qkv.shape[1]
@@ -480,32 +603,43 @@
     def give(value, source):
         return lax.ppermute(value, "section", [(source, 1 - source)])
 
-    def half_of(half):
+    place = jnp.stack([section, 0 * me]).astype(jnp.int32)
+
+    def attention_half(half):
         parts = [w_proj[0]]
         for pair in range(3):
             at = pair * D + half * HALF
             parts.append(w_qkv[0, :, at : at + HALF])
+        return jnp.concatenate(parts, axis=1)
+
+    def feed_half(half):
         ups = w_up[0].reshape(rows, count, 4, group)
+        parts = []
         for part in (2 * half, 2 * half + 1):
             parts.append(ups[:, :, part].reshape(rows, count * group))
         for part in (2 * half, 2 * half + 1):
             parts.append(w_down[0, part * group : (part + 1) * group])
         return jnp.concatenate(parts, axis=1)
 
-    halves = (half_of(0), half_of(1))
-    mine = jnp.where(first, halves[0], halves[1])
-    other = swap(jnp.where(first, halves[1], halves[0]))
-    shards = (jnp.where(first, mine, other), jnp.where(first, other, mine))
-    split = D + 3 * HALF
-
-    gains = []
-    for gain in (ln_gain, q_gain, k_gain):
-        theirs = swap(gain[0])
-        gains.append((jnp.where(first, gain[0], theirs), jnp.where(first, theirs, gain[0])))
+    shards = [[None, None], [None, None]]
+    held = None
+    for kind, half_of in enumerate((attention_half, feed_half)):
+        halves = (half_of(0), half_of(1))
+        mine = jnp.where(first, halves[0], halves[1])
+        theirs = jnp.where(first, halves[1], halves[0])
+        other = swap(theirs if held is None else after(theirs, held))
+        held = other
+        shards[0][kind] = jnp.where(first, mine, other)
+        shards[1][kind] = jnp.where(first, other, mine)
+
+    own_gains = jnp.concatenate([ln_gain, q_gain, k_gain], axis=0)
+    their_gains = swap(after(own_gains, *shards[0]))
+    gains = (jnp.where(first, own_gains, their_gains), jnp.where(first, their_gains, own_gains))
+
     at_half = lambda gain: lax.dynamic_slice_in_dim(gain, section * HALF, HALF, 0)
-    ln_gains = [gain[None] for gain in gains[0]]
+    ln_gains = [gains[block][:1] for block in range(2)]
     qk_gains = [
-        jnp.concatenate([at_half(gains[1][block]), at_half(gains[2][block])])[None] for block in range(2)
+        jnp.concatenate([at_half(gains[block][1]), at_half(gains[block][2])])[None] for block in range(2)
     ]
 
     def padded(value):
@@ -514,38 +648,78 @@
     def trimmed(value):
         return value.reshape(number, pad, D)[:, :tokens]
 
-    attention_weights, feed_weights, inputs, kept = [], [], [padded(images)], []
-    parts = None
+    weights = []
     for block in range(2):
-        gathered = gather_rows(shards[block])
-        attention_weights.append(gathered[:, :split])
-        feed_weights.append(gathered[:, split:])
+        shard = jnp.concatenate(shards[block], axis=1)
+        if block == 1:
+            shard = after(shard, weights[0][0])
+        weights.append([lax.all_gather(shard, "dp", axis=0, tiled=True)])
+
+    inputs, kept, parts = [padded(images)], [], []
+    for block in range(2):
         saved = attention_forward(
-            tokens, scalar, inputs[block], attention_weights[block], ln_gains[block], qk_gains[block]
+            tokens, place, inputs[block], weights[block], ln_gains[block], qk_gains[block]
         )
-        hidden, slope, part = feed_forward(saved[0], feed_weights[block], saved[6])
+        hidden, slope, part = feed_forward(place, units, saved[0], weights[block], saved[6])
         kept.append(tuple(saved[:6]) + (hidden, slope))
-        theirs = swap(part) if block == 0 else give(part, 0)
-        inputs.append(
-            (inputs[block].astype(F32) + part.astype(F32) + theirs.astype(F32)).astype(BF)
+        parts.append(part)
+        if block == 0:
+            inputs.append((inputs[0].astype(F32) + part.astype(F32) + swap(part).astype(F32)).astype(BF))
+
+    def feed_step(block, grad):
+        normed, hidden, slope = kept[block][0], kept[block][6], kept[block][7]
+        return feed_backward(place, units, grad, normed, weights[block], hidden, slope)
+
+    def attention_step(block, grad, feed_part):
+        return attention_backward(
+            tokens, place, grad, weights[block], qk_gains[block], *kept[block][:6], feed_part
         )
-    outputs = trimmed(jnp.where(first, inputs[1], inputs[2]))
+
+    def core_stage(terms):
+        mine, sent = scatter_core(terms)
+        return mine, relative(sent, 1)
+
+    def near_stage(mine, arrived):
+        mine, sent = scatter_near(add_low(mine, arrived))
+        return mine, sent, relative(sent, 2)
 
     grad = padded(cotangent)
-    grads = [None, None]
-    summed = [None, None]
-    sums = [None, None]
-    for block in (1, 0):
-        normed, qk, v, r, pt, mixed, hidden, slope = kept[block]
-        feed_grads, feed_part = feed_backward(grad, normed, feed_weights[block], hidden, slope)
-        attention_grads, part, sums[block] = attention_backward(
-            tokens, scalar, grad, attention_weights[block], qk_gains[block], normed, qk, v, r, pt, mixed, feed_part
-        )
-        theirs = swap(part) if block == 1 else give(part, 1)
-        grad = norm_backward(grad, inputs[block], part, theirs, ln_gains[block])
-        grads[block] = grad
-        summed[block] = jnp.concatenate([scatter_rows(attention_grads), scatter_rows(feed_grads)], axis=1)
-    input_grads = trimmed(jnp.where(first, grads[0], grads[1]))
+    feed_grads, feed_part = feed_step(1, grad)
+    attention_grads, part, sums_1 = attention_step(1, grad, feed_part)
+    theirs = swap(part)
+    terms = jnp.concatenate([attention_grads, feed_grads], axis=1)
+    second_sum = lax.psum_scatter(terms, "dp", scatter_dimension=0, tiled=True).astype(F32)
+    middle_grad = norm_backward(grad, inputs[1], part, theirs, ln_gains[1])
+    feed_grads, feed_part = feed_step(0, middle_grad)
+
+    feed_near = near_stage(*core_stage(feed_grads))
+    attention_grads, part, sums_0 = attention_step(0, after(middle_grad, feed_near[1]), feed_part)
+    feed_far = add_low(feed_near[0], feed_near[2])
+    feed_terms = scatter_far(feed_far)
+
+    gain_rows = []
+    for block, sums in enumerate((sums_0, sums_1)):
+        zero = jnp.zeros((D,), F32)
+        put = lambda value: lax.dynamic_update_slice_in_dim(zero, value, section * HALF, 0)
+        gain_rows += [sums[0] / gains[block][0], put(sums[1, :HALF]), put(sums[1, HALF:])]
+    totals = jnp.stack(gain_rows)
+
+    kept_rows, arrived = core_stage(after(attention_grads, feed_far))
+    totals = totals + relative(after(totals, feed_far), 1)
+    kept_rows, sent_rows, arrived = near_stage(after(kept_rows, totals), arrived)
+    totals = totals + relative(after(totals, sent_rows), 2)
+    attention_far = add_low(after(kept_rows, totals), arrived)
+    attention_terms = scatter_far(attention_far)
+    after_far = after(totals, attention_far)
+    totals = add_all([totals] + [relative(after_far, 4 * far) for far in range(1, count // 4)])
+    feed_sum = add_all([after(feed_terms[0], attention_far)] + feed_terms[1:])
+    attention_sum = add_all([after(attention_terms[0], feed_sum, totals)] + attention_terms[1:])
+    theirs = give(after(part, sent_rows), 1)
+    summed = [jnp.concatenate([attention_sum, feed_sum], axis=1), second_sum]
+    first_grad = norm_backward(middle_grad, inputs[0], part, theirs, ln_gains[0])
+    input_grads = trimmed(jnp.where(first, first_grad, middle_grad))
+    last = (inputs[1].astype(F32) + parts[1].astype(F32)) + give(parts[1], 0).astype(F32)
+    outputs = trimmed(jnp.where(first, inputs[1], last.astype(BF)))
 
     own = jnp.where(first, summed[0], summed[1])
     theirs = swap(jnp.where(first, summed[1], summed[0]).astype(BF)).astype(F32)
@@ -560,23 +734,14 @@
     ups, downs = [], []
     for source in (low_half, high_half):
         for part in range(2):
-            at = split + part * D
+            at = SPLIT + part * D
             ups.append(source[:, at : at + D].reshape(rows, count, 1, group))
-            at = split + units + part * D
+            at = SPLIT + units + part * D
             downs.append(source[:, at : at + D])
     grad_up = jnp.concatenate(ups, axis=2).reshape(rows, 2 * units)
     grad_down = jnp.concatenate(downs, axis=0)
 
-    gain_rows = []
-    for block in range(2):
-        zero = jnp.zeros((D,), F32)
-        place = lambda value: lax.dynamic_update_slice_in_dim(zero, value, section * HALF, 0)
-        gain_rows += [
-            sums[block][0] / gains[0][block],
-            place(sums[block][1, :HALF]),
-            place(sums[block][1, HALF:]),
-        ]
-    totals = lax.psum(jnp.stack(gain_rows), ("section", "dp"))
+    totals = totals + swap(after(totals, own))
     totals = jnp.where(first, totals[:3], totals[3:])
     return (
         outputs[None],

time: 619 us -> 439 us (0.71)
  waiting for transfers between devices: 261 us -> 183 us
  blocking collectives: 50.3 us -> 0 us
  Pallas kernels: 144 us -> 107 us
  starting transfers between devices: 54.9 us -> 33.4 us
  between operations: 2.18 us -> 15.1 us
  local copies, waits for them, and re-layouts: 75.8 us -> 68.1 us
    ppermute x50 -> x15, waiting for transfers between devices: 214 us -> 43.8 us  [relative(): lax.ppermute(value, 'dp', [(source, source ^ step) for source in range(co...]
    all_gather x0 -> x2, waiting for transfers between devices: none -> 78.7 us  [on_device(): weights.append([lax.all_gather(shard, 'dp', axis=0, tiled=True)])]
    psum x1 -> x0, blocking collectives: 50.3 us -> none  [on_device(): totals = lax.psum(jnp.stack(gain_rows), ('section', 'dp'))]
    pallas_call x8, Pallas kernels: 133 us -> 99.3 us  [the longest x2 28.8 us: attention_backward(): pl.pallas_call(partial(attention_backward_kernel, steps, len(pieces)), gr...]
    ppermute x50 -> x15, starting transfers between devices: 42.9 us -> 19 us  [relative(): lax.ppermute(value, 'dp', [(source, source ^ step) for source in range(co...]
    unnamed x68 -> x105, local copies, waits for them, and re-layouts: 17.8 us -> 41.3 us
    ppermute x7, waiting for transfers between devices: 46.8 us -> 60.8 us  [swap(): return lax.ppermute(value, 'section', [(0, 1), (1, 0)])]
    slice x7 -> x3, local copies, waits for them, and re-layouts: 17.4 us -> 4.55 us  [the longest x1 4.54 us: feed_half(): parts.append(ups[:, :, part].reshape(rows, count * group))]
  transfers between devices with their start and end apart: 59 -> 27, of which waited for: 25 -> 16; matrix products, arithmetic and copies ran while one was open for 11% -> 11% of each run, Pallas kernels for 18% -> 13%
where the time goes in v2:
time: 439 us; the launch traced here: 433 us
  waiting for transfers between devices  183 us (42%)
  Pallas kernels  107 us (24%)
  local copies, waits for them, and re-layouts  68.1 us (16%)
  starting transfers between devices  33.4 us (8%)
  other arithmetic  25.5 us (6%)
  between operations  15.1 us (3%)
    all_gather x2, waiting for transfers between devices, on_device(): weights.append([lax.all_gather(shard, 'dp', axis=0, tiled=True)])  78.7 us
    ppermute x7, waiting for transfers between devices, swap(): return lax.ppermute(value, 'section', [(0, 1), (1, 0)])  60.8 us
    ppermute x15, waiting for transfers between devices, relative(): lax.ppermute(value, 'dp', [(source, source ^ step) for source in range(co...  43.8 us
    unnamed x105, local copies, waits for them, and re-layouts  41.3 us
    pallas_call x2, Pallas kernels, attention_backward(): pl.pallas_call(partial(attention_backward_kernel, steps, len(pieces)), gr...  28.8 us
    pallas_call x2, Pallas kernels, feed_forward(): pl.pallas_call(partial(feed_forward_kernel, steps, len(pieces)), grid_spe...  26.6 us
    pallas_call x2, Pallas kernels, feed_backward(): pl.pallas_call(partial(feed_backward_kernel, steps, len(pieces)), grid_sp...  26.2 us
    ppermute x15, starting transfers between devices, relative(): lax.ppermute(value, 'dp', [(source, source ^ step) for source in range(co...  19 us
  transfers between devices with their start and end apart: 27, of which 16 were waited for; matrix products, arithmetic and copies ran while one was open for 11% of the time, Pallas kernels for 13%

profile of v2, /device:TPU:0, one launch (start us, length us, event | category | flops | bytes accessed | tf_op | source)
XLA Modules:
  0.0 433.0 jit_solution(17266959168921505191)
XLA Ops:
  9.1 3.0 collective-permute-start
  13.9 4.5 %slice_reduce_fusion.3 = (bf16[48,16,48]{2,1,0:T(8,128)(2,1)S(1)}, bf16[48,16,48]{2,1,0:T(8,128)(2,1)S(1)}, bf16[48,16,48]{2,1,0:T(8,128)(2,1)S(1)}, bf16[48,16,48]{2,1,0:T(8,128)(2,1)S(1)}) fusion(bf16[48,16,4,48]{3,2,1,0:T(4,128)(2,1)S(1)} %reshape_squeeze.16), kind=kLoop, calls=%fused_computation.33 | loop fusion | bytes 589824 | tf_op jit(solution)/shard_map/slice | solution.py:619
  19.6 8.4 %collective-permute-done.1 = bf16[48,3072]{1,0:T(8,128)(2,1)S(1)} collective-permute-done((bf16[48,3072]{1,0:T(8,128)(2,1)S(1)}, bf16[48,3072]{1,0:T(8,128)(2,1)S(1)}, u32[]{:S(2)}, u32[]{:S(2)}) %collective-permute-start.1) | collective-permute-done | bytes 294944 | tf_op jit(solution)/shard_map/ppermute | solution.py:601
  29.9 70.0 %all-gather.3.cloned.1.call-done.refs_0_ = bf16[768,4992]{1,0:T(8,128)(2,1)} async-done(((bf16[48,4992]{1,0:T(8,128)(2,1)}), bf16[768,4992]{1,0:T(8,128)(2,1)}) %all-gather.3.cloned.1.call-update) | async-done | bytes 7667728 | tf_op jit(solution)/shard_map/all_gather | solution.py:656
  100.4 1.5 collective-permute-start.2
  102.3 1.9 collective-permute-done.2
  104.3 3.2 copy-done.10
  107.5 8.8 %attention_forward.2 = (bf16[832,768]{1,0:T(8,128)(2,1)S(1)}, bf16[832,768]{1,0:T(8,128)(2,1)S(1)}, bf16[832,384]{1,0:T(8,128)(2,1)S(1)}, bf16[832,768]{1,0:T(8,...) custom-call(s32[2]{0:T(128)S(1)} %pad_add_fusion.place, ...), custom_call_target="tpu_custom_call" | custom-call | flops 2494562304 | bytes 10616832 | tf_op jit(solution)/shard_map/attention_forward/pallas_call | solution.py:141
  118.2 13.2 %feed_forward.2 = (bf16[832,1536]{1,0:T(8,128)(2,1)S(1)}, bf16[832,1536]{1,0:T(8,128)(2,1)S(1)}, bf16[832,768]{1,0:T(8,128)(2,1)S(1)}) custom-call(s32[2]{0:T(128)S(1)} %pad_add_fusion.place, bf16[768,4992]{1,0:T(8,128)(2,1)S(1)} %copy-done.11, bf16[832,768]{1,0:T(8,128)(2,1)S(1)} %get-tuple-element.55.refs_1_.refs_2_.refs_4_, ...), custom_call_target="tpu_custom_call" | custom-call | flops 3925868544 | bytes 13664256 | tf_op jit(solution)/shard_map/feed_forward/pallas_call | solution.py:246
  131.5 1.4 copy-done.31
  132.9 1.5 collective-permute-start.3
  135.8 26.2 %collective-permute-done.3 = bf16[832,768]{1,0:T(8,128)(2,1)S(1)} collective-permute-done((bf16[832,768]{1,0:T(8,128)(2,1)S(1)}, bf16[832,768]{1,0:T(8,128)(2,1)S(1)}, u32[]{:S(2)}, u32[]{:S(2)}) %collective-permute-start.3) | collective-permute-done | bytes 1277984 | tf_op jit(solution)/shard_map/ppermute | solution.py:601
  162.6 8.7 %all-gather.5.cloned.1.call-done.refs_0_ = bf16[768,4992]{1,0:T(8,128)(2,1)} async-done(((bf16[48,4992]{1,0:T(8,128)(2,1)}), bf16[768,4992]{1,0:T(8,128)(2,1)}) %all-gather.5.cloned.1.call-update) | async-done | bytes 7667728 | tf_op jit(solution)/shard_map/all_gather | solution.py:656
  171.3 3.2 copy-done.14
  174.5 8.9 %attention_forward.3 = (bf16[832,768]{1,0:T(8,128)(2,1)S(1)}, bf16[832,768]{1,0:T(8,128)(2,1)S(1)}, bf16[832,384]{1,0:T(8,128)(2,1)S(1)}, bf16[832,768]{1,0:T(8,...) custom-call(s32[2]{0:T(128)S(1)} %pad_add_fusion.place, ...), custom_call_target="tpu_custom_call" | custom-call | flops 2494562304 | bytes 10616832 | tf_op jit(solution)/shard_map/attention_forward/pallas_call | solution.py:141
  183.4 13.4 %feed_forward.3 = (bf16[832,1536]{1,0:T(8,128)(2,1)S(1)}, bf16[832,1536]{1,0:T(8,128)(2,1)S(1)}, bf16[832,768]{1,0:T(8,128)(2,1)S(1)}) custom-call(s32[2]{0:T(128)S(1)} %pad_add_fusion.place, bf16[768,4992]{1,0:T(8,128)(2,1)S(1)} %copy-done.15, bf16[832,768]{1,0:T(8,128)(2,1)S(1)} %get-tuple-element.59.refs_1_.refs_2_.refs_4_, ...), custom_call_target="tpu_custom_call" | custom-call | flops 3925868544 | bytes 13664256 | tf_op jit(solution)/shard_map/feed_forward/pallas_call | solution.py:246
  197.9 13.0 %feed_backward.2 = (bf16[768,3072]{1,0:T(8,128)(2,1)S(1)}, bf16[832,768]{1,0:T(8,128)(2,1)S(1)}) custom-call(s32[2]{0:T(128)S(1)} %pad_add_fusion.place, bf16[768,4992]{1,0:T(8,128)(2,1)S(1)} %copy-done.15, bf16[832,768]{1,0:T(8,128)(2,1)S(1)} %bitcast.76, bf16[832,768]{1,0:T(8,128)(2,1)S(1)} %get-tuple-element.59.refs_1_.refs_2_.refs_4_, ...), custom_call_target="tpu_custom_call" | custom-call | flops 7851737088 | bytes 18382848 | tf_op jit(solution)/shard_map/feed_backward/pallas_call | solution.py:309
  210.9 2.1 copy-done.6
  213.0 14.3 %attention_backward.2 = (bf16[768,1920]{1,0:T(8,128)(2,1)S(1)}, bf16[832,768]{1,0:T(8,128)(2,1)}, f32[8,768]{1,0:T(8,128)S(1)}) custom-call(s32[2]{0:T(128)S(1)} %pad_add_fusion.place, bf16[768,4992]{1,0:T(8,128)(2,1)S(1)} %copy-done.15, bf16[832,768]{1,0:T(8,128)(2,1)S(1)} %bitcast.77, f32[1,768]{1,0:T(1,128)S(1)} %broadcast_in_dim.22.refs_3_.refs_2_, ...), custom_call_target="tpu_custom_call" | custom-call | flops 4989124608 | bytes 16121856 | tf_op jit(solution)/shard_map/attention_backward/pallas_call | solution.py:438
  227.4 1.6 copy-done.7
  229.0 1.5 collective-permute-start.5
  230.5 6.9 %pad_maximum_fusion = bf16[768,4992]{1,0:T(8,128)(2,1)} fusion(bf16[768,3072]{1,0:T(8,128)(2,1)} %copy-done.6, bf16[768,1920]{1,0:T(8,128)(2,1)} %copy-done.7), kind=kLoop, calls=%fused_computation | loop fusion | flops 15335424 | bytes 15335424 | tf_op jit(solution)/shard_map/concatenate | solution.py:690
  237.4 22.2 %collective-permute-done.5.theirs_ref = bf16[832,768]{1,0:T(8,128)(2,1)} collective-permute-done((bf16[832,768]{1,0:T(8,128)(2,1)}, bf16[832,768]{1,0:T(8,128)(2,1)}, u32[]{:S(2)}, u32[]{:S(2)}) %collective-permute-start.5) | collective-permute-done | bytes 1277984 | tf_op jit(solution)/shard_map/ppermute | solution.py:601
  259.5 1.3 copy-done.4
  260.9 4.4 %norm_backward.2.refs_1_.g_ref = bf16[832,768]{1,0:T(8,128)(2,1)S(1)} custom-call(bf16[832,768]{1,0:T(8,128)(2,1)S(1)} %bitcast.78, bf16[832,768]{1,0:T(8,128)(2,1)S(1)} %add_convert_fusion.2.refs_1_.x_ref, bf16[832,768]{1,0:T(8,128)(2,1)} %get-tuple-element.70.mine_ref, bf16[832,768]{1,0:T(8,128)(2,1)} %collective-permute-done.5.theirs_ref, ...), custom_call_target="tpu_custom_call" | custom-call | flops 7667712 | bytes 6389760 | tf_op jit(solution)/shard_map/norm_backward/pallas_call | solution.py:502
  265.3 4.0 copy-done.12
  269.3 13.2 %feed_backward.3 = (bf16[768,3072]{1,0:T(8,128)(2,1)S(1)}, bf16[832,768]{1,0:T(8,128)(2,1)S(1)}) custom-call(s32[2]{0:T(128)S(1)} %pad_add_fusion.place, bf16[768,4992]{1,0:T(8,128)(2,1)S(1)} %copy-done.12, bf16[832,768]{1,0:T(8,128)(2,1)S(1)} %norm_backward.2.refs_1_.g_ref, bf16[832,768]{1,0:T(8,128)(2,1)S(1)} %copy-done.19, ...), custom_call_target="tpu_custom_call" | custom-call | flops 7851737088 | bytes 18382848 | tf_op jit(solution)/shard_map/feed_backward/pallas_call | solution.py:309
  283.7 1.8 dynamic-slice_bitcast_fusion
  286.5 4.9 %collective-permute-done.6 = bf16[4,2,48,3072]{3,2,1,0:T(8,128)(2,1)} collective-permute-done((bf16[4,2,48,3072]{3,2,1,0:T(8,128)(2,1)}, bf16[4,2,48,3072]{3,2,1,0:T(8,128)(2,1)}, u32[]{:S(2)}, u32[]{:S(2)}) %collective-permute-start.6) | collective-permute-done | bytes 2359328 | tf_op jit(solution)/shard_map/ppermute | solution.py:520
  291.4 3.3 fusion
  294.8 1.4 copy-done.33
  298.4 1.3 copy-done.1
  299.7 3.2 copy-done.13
  303.0 1.7 copy-done.17
  304.7 1.3 copy-done.20
  306.0 1.3 copy-done.22
  307.3 1.3 copy-done.24
  309.7 1.3 copy-done.28
  311.0 14.4 %attention_backward.3 = (bf16[768,1920]{1,0:T(8,128)(2,1)S(1)}, bf16[832,768]{1,0:T(8,128)(2,1)}, f32[8,768]{1,0:T(8,128)S(1)}) custom-call(s32[2]{0:T(128)S(1)} %pad_add_fusion.place, bf16[768,4992]{1,0:T(8,128)(2,1)S(1)} %copy-done.13, bf16[832,768]{1,0:T(8,128)(2,1)S(1)} %copy-done.1, f32[1,768]{1,0:T(1,128)S(1)} %broadcast_in_dim.21.refs_3_.refs_2_, ...), custom_call_target="tpu_custom_call" | custom-call | flops 4989124608 | bytes 16121856 | tf_op jit(solution)/shard_map/attention_backward/pallas_call | solution.py:438
  325.5 5.3 %collective-permute-done.7 = bf16[4,48,3072]{2,1,0:T(8,128)(2,1)} collective-permute-done((bf16[4,48,3072]{2,1,0:T(8,128)(2,1)}, bf16[4,48,3072]{2,1,0:T(8,128)(2,1)}, u32[]{:S(2)}, u32[]{:S(2)}) %collective-permute-start.7) | collective-permute-done | bytes 1179680 | tf_op jit(solution)/shard_map/ppermute | solution.py:520
  330.8 2.7 fusion.1
  333.5 1.9 dynamic-slice_bitcast_fusion.2
  336.1 2.6 collective-permute-done.8
  339.0 2.2 add_convert_fusion
  343.3 4.7 %collective-permute-start.4 = (bf16[832,768]{1,0:T(8,128)(2,1)}, bf16[832,768]{1,0:T(8,128)(2,1)}, u32[]{:S(2)}, u32[]{:S(2)}) collective-permute-start(bf16[832,768]{1,0:T(8,128)(2,1)} %copy-done.8), channel_id=1, source_target_pairs={{0,16},{1,17},{2,18},{3,19},{4,20},{5,21},{6,22},{7,23},{8,24},{9,... | collective-permute-start | bytes 3833864 | tf_op jit(solution)/shard_map/ppermute | solution.py:604
  349.1 1.3 dynamic-slice_bitcast_fusion.9
  350.4 2.1 collective-permute-start.15
  353.2 8.2 %collective-permute-done.11 = f32[6,768]{1,0:T(8,128)S(1)} collective-permute-done((f32[6,768]{1,0:T(8,128)S(1)}, f32[6,768]{1,0:T(8,128)S(1)}, u32[]{:S(2)}, u32[]{:S(2)}) %collective-permute-start.11) | collective-permute-done | bytes 18464 | tf_op jit(solution)/shard_map/ppermute | solution.py:520
  361.4 1.5 collective-permute-start.13
  364.2 1.3 add_convert_fusion.3
  365.5 2.2 collective-permute-start.18
  367.8 11.4 %collective-permute-done.14 = bf16[48,3072]{1,0:T(8,128)(2,1)S(1)} collective-permute-done((bf16[48,3072]{1,0:T(8,128)(2,1)S(1)}, bf16[48,3072]{1,0:T(8,128)(2,1)S(1)}, u32[]{:S(2)}, u32[]{:S(2)}) %collective-permute-start.14) | collective-permute-done | bytes 294944 | tf_op jit(solution)/shard_map/ppermute | solution.py:520
  379.1 2.7 collective-permute-start.16
  382.1 1.7 collective-permute-start.21
  384.1 3.9 collective-permute-start.19
  388.1 3.5 collective-permute-done.21
  391.6 7.4 %collective-permute-done.20 = bf16[48,1920]{1,0:T(8,128)(2,1)S(1)} collective-permute-done((bf16[48,1920]{1,0:T(8,128)(2,1)S(1)}, bf16[48,1920]{1,0:T(8,128)(2,1)S(1)}, u32[]{:S(2)}, u32[]{:S(2)}) %collective-permute-start.20) | collective-permute-done | bytes 184352 | tf_op jit(solution)/shard_map/ppermute | solution.py:520
  400.6 1.9 fusion.2
  402.6 1.5 copy.38
  404.1 3.8 norm_backward.3
  408.1 1.5 copy.37
  409.6 2.1 collective-permute-done.22
  419.2 2.2 copy.26
  421.3 4.0 broadcast_in_dim_reshape.3
  (188 shorter events, 34.6 us)
Async XLA Ops:
  7.2 5.9 %copy-start.43 = (bf16[1,48,3072]{2,1,0:T(8,128)(2,1)S(1)}, bf16[1,48,3072]{2,1,0:T(8,128)(2,1)}, u32[]{:S(2)}) copy-start(bf16[1,48,3072]{2,1,0:T(8,128)(2,1)} %param.12) | copy-start | bytes 884740
  7.2 92.6 %all-gather.3.cloned.1.call-start = ((), (), s32[]{:S(2)}) async-start(), calls=%async_computation.1 | async-start | bytes 8146944 | tf_op jit(solution)/shard_map/all_gather | solution.py:656
  9.1 10.3 %collective-permute-start = (bf16[48,1920]{1,0:T(8,128)(2,1)S(1)}, bf16[48,1920]{1,0:T(8,128)(2,1)S(1)}, u32[]{:S(2)}, u32[]{:S(2)}) collective-permute-start(bf16[48,1920]{1,0:T(8,128)(2,1)S(1)} %broadcast_select_fusion.7), channel_id=1, source_target_pairs={{0,16},{16,0},{1,17},{17,1},{2,18},{18,2},{3,19},{19,3},{4,20},{20... | collective-permute-start | bytes 552968 | tf_op jit(solution)/shard_map/ppermute | solution.py:601
  19.4 8.5 %collective-permute-start.1 = (bf16[48,3072]{1,0:T(8,128)(2,1)S(1)}, bf16[48,3072]{1,0:T(8,128)(2,1)S(1)}, u32[]{:S(2)}, u32[]{:S(2)}) collective-permute-start(bf16[48,3072]{1,0:T(8,128)(2,1)S(1)} %broadcast_select_fusion.3), channel_id=1, source_target_pairs={{0,16},{16,0},{1,17},{17,1},{2,18},{18,2},{3,19},{19,3},{4,20},{20... | collective-permute-start | bytes 884744 | tf_op jit(solution)/shard_map/ppermute | solution.py:601
  28.1 72.2 %copy-start.45 = (f32[1,768]{1,0:T(1,128)S(1)}, f32[1,768]{1,0:T(1,128)}, u32[]{:S(2)}) copy-start(f32[1,768]{1,0:T(1,128)} %param.17) | copy-start | bytes 9220
  28.1 72.2 %copy-start.46 = (f32[1,768]{1,0:T(1,128)S(1)}, f32[1,768]{1,0:T(1,128)}, u32[]{:S(2)}) copy-start(f32[1,768]{1,0:T(1,128)} %param.16) | copy-start | bytes 9220
  28.2 72.2 %copy-start.47 = (f32[1,768]{1,0:T(1,128)S(1)}, f32[1,768]{1,0:T(1,128)}, u32[]{:S(2)}) copy-start(f32[1,768]{1,0:T(1,128)} %param.15) | copy-start | bytes 9220
  28.2 73.9 %copy-start.38 = (bf16[4,196,768]{2,0,1:T(4,128)(2,1)S(1)}, bf16[4,196,768]{2,0,1:T(4,128)(2,1)}, u32[]{:S(2)}) copy-start(bf16[4,196,768]{2,0,1:T(4,128)(2,1)} %param.9) | copy-start | bytes 3612676
  29.0 142.3 %all-gather.5.cloned.1.call-start = ((), (), s32[]{:S(2)}) async-start(), calls=%async_computation.2 | async-start | bytes 8146944 | tf_op jit(solution)/shard_map/all_gather | solution.py:656
  99.9 299.3 %reduce-scatter.2.cloned.1.call-start = ((), (), s32[]{:S(2)}) async-start(), calls=%async_computation.3 | async-start | bytes 8146944 | tf_op jit(solution)/shard_map/reduce_scatter | solution.py:691
  100.4 3.8 collective-permute-start.2
  104.3 3.2 copy-start.10
  107.5 10.8 %copy-start.11 = (bf16[768,4992]{1,0:T(8,128)(2,1)S(1)}, bf16[768,4992]{1,0:T(8,128)(2,1)}, u32[]{:S(2)}) copy-start(bf16[768,4992]{1,0:T(8,128)(2,1)} %all-gather.3.cloned.1.call-done.refs_0_) | copy-start | bytes 23003140
  118.2 13.2 %copy-start.16 = (bf16[4,6,208,208]{3,2,1,0:T(8,128)(2,1)}, bf16[4,6,208,208]{3,2,1,0:T(8,128)(2,1)S(1)}, u32[]{:S(2)}) copy-start(bf16[4,6,208,208]{3,2,1,0:T(8,128)(2,1)S(1)} %get-tuple-element.78.refs_8_) | copy-start | bytes 6230020
  118.2 13.3 %copy-start.18 = (bf16[832,768]{1,0:T(8,128)(2,1)}, bf16[832,768]{1,0:T(8,128)(2,1)S(1)}, u32[]{:S(2)}) copy-start(bf16[832,768]{1,0:T(8,128)(2,1)S(1)} %get-tuple-element.55.refs_1_.refs_2_.refs_4_) | copy-start | bytes 3833860
  118.2 13.3 %copy-start.21 = (bf16[832,768]{1,0:T(8,128)(2,1)}, bf16[832,768]{1,0:T(8,128)(2,1)S(1)}, u32[]{:S(2)}) copy-start(bf16[832,768]{1,0:T(8,128)(2,1)S(1)} %get-tuple-element.75.refs_5_) | copy-start | bytes 3833860
  118.2 16.2 %copy-start.39 = (bf16[4,196,768]{2,0,1:T(4,128)(2,1)S(1)}, bf16[4,196,768]{2,0,1:T(4,128)(2,1)}, u32[]{:S(2)}) copy-start(bf16[4,196,768]{2,0,1:T(4,128)(2,1)} %param.10) | copy-start | bytes 3612676
  131.5 1.4 copy-start.31
  132.9 2.8 copy-start.29
  132.9 29.1 %collective-permute-start.3 = (bf16[832,768]{1,0:T(8,128)(2,1)S(1)}, bf16[832,768]{1,0:T(8,128)(2,1)S(1)}, u32[]{:S(2)}, u32[]{:S(2)}) collective-permute-start(bf16[832,768]{1,0:T(8,128)(2,1)S(1)} %get-tuple-element.57), channel_id=1, source_target_pairs={{0,16},{16,0},{1,17},{17,1},{2,18},{18,2},{3,19},{19,3},{4,20},{20... | collective-permute-start | bytes 3833864 | tf_op jit(solution)/shard_map/ppermute | solution.py:601
  171.3 3.2 copy-start.14
  174.5 8.9 %copy-start.15 = (bf16[768,4992]{1,0:T(8,128)(2,1)S(1)}, bf16[768,4992]{1,0:T(8,128)(2,1)}, u32[]{:S(2)}) copy-start(bf16[768,4992]{1,0:T(8,128)(2,1)} %all-gather.5.cloned.1.call-done.refs_0_) | copy-start | bytes 23003140
  183.4 14.4 %copy-start.3 = (bf16[4,208,768]{2,1,0:T(8,128)(2,1)S(1)}, bf16[4,208,768]{2,1,0:T(8,128)(2,1)}, u32[]{:S(2)}) copy-start(bf16[4,208,768]{2,1,0:T(8,128)(2,1)} %pad.8.clone) | copy-start | bytes 3833860
  210.9 2.1 copy-start.6
  227.4 1.6 copy-start.7
  229.0 30.6 %collective-permute-start.5 = (bf16[832,768]{1,0:T(8,128)(2,1)}, bf16[832,768]{1,0:T(8,128)(2,1)}, u32[]{:S(2)}, u32[]{:S(2)}) collective-permute-start(bf16[832,768]{1,0:T(8,128)(2,1)} %get-tuple-element.70.mine_ref), channel_id=1, source_target_pairs={{0,16},{16,0},{1,17},{17,1},{2,18},{18,2},{3,19},{19,3},{4,20},{20... | collective-permute-start | bytes 3833864 | tf_op jit(solution)/shard_map/ppermute | solution.py:601
  259.5 1.3 copy-start.4
  260.8 4.4 %copy-start.19 = (bf16[832,768]{1,0:T(8,128)(2,1)S(1)}, bf16[832,768]{1,0:T(8,128)(2,1)}, u32[]{:S(2)}) copy-start(bf16[832,768]{1,0:T(8,128)(2,1)} %copy-done.18) | copy-start | bytes 3833860
  260.8 4.4 %copy-start.30 = (bf16[832,1536]{1,0:T(8,128)(2,1)S(1)}, bf16[832,1536]{1,0:T(8,128)(2,1)}, u32[]{:S(2)}) copy-start(bf16[832,1536]{1,0:T(8,128)(2,1)} %copy-done.29) | copy-start | bytes 7667716
  260.9 4.4 %copy-start.32 = (bf16[832,1536]{1,0:T(8,128)(2,1)S(1)}, bf16[832,1536]{1,0:T(8,128)(2,1)}, u32[]{:S(2)}) copy-start(bf16[832,1536]{1,0:T(8,128)(2,1)} %copy-done.31) | copy-start | bytes 7667716
  265.3 17.3 %copy-start = (bf16[832,768]{1,0:T(8,128)(2,1)}, bf16[832,768]{1,0:T(8,128)(2,1)S(1)}, u32[]{:S(2)}) copy-start(bf16[832,768]{1,0:T(8,128)(2,1)S(1)} %norm_backward.2.refs_1_.g_ref) | copy-start | bytes 3833860
  265.3 4.0 copy-start.12
  283.7 2.8 copy-start.5
  286.5 4.9 %collective-permute-start.6 = (bf16[4,2,48,3072]{3,2,1,0:T(8,128)(2,1)}, bf16[4,2,48,3072]{3,2,1,0:T(8,128)(2,1)}, u32[]{:S(2)}, u32[]{:S(2)}) collective-permute-start(bf16[4,2,48,3072]{3,2,1,0:T(8,128)(2,1)} %dynamic-slice_bitcast_fusion), channel_id=1, source_target_pairs={{0,1},{1,0},{2,3},{3,2},{4,5},{5,4},{6,7},{7,6},{8,9},{9,8},{10,11... | collective-permute-start | bytes 7077896 | tf_op jit(solution)/shard_map/ppermute | solution.py:520
  294.7 1.4 copy-start.33
  297.3 33.5 %collective-permute-start.7 = (bf16[4,48,3072]{2,1,0:T(8,128)(2,1)}, bf16[4,48,3072]{2,1,0:T(8,128)(2,1)}, u32[]{:S(2)}, u32[]{:S(2)}) collective-permute-start(bf16[4,48,3072]{2,1,0:T(8,128)(2,1)} %dynamic-slice_bitcast_fusion.3), channel_id=1, source_target_pairs={{0,2},{1,3},{2,0},{3,1},{4,6},{5,7},{6,4},{7,5},{8,10},{9,11},{10,... | collective-permute-start | bytes 3538952 | tf_op jit(solution)/shard_map/ppermute | solution.py:520
  298.4 1.3 copy-start.1
  299.7 3.2 copy-start.13
  303.0 1.7 copy-start.17
  304.7 1.3 copy-start.20
  307.3 1.3 copy-start.24
  309.7 1.3 copy-start.28
  311.0 19.8 %copy-start.34 = (bf16[4,2,48,3072]{3,2,1,0:T(8,128)(2,1)S(1)}, bf16[4,2,48,3072]{3,2,1,0:T(8,128)(2,1)}, u32[]{:S(2)}) copy-start(bf16[4,2,48,3072]{3,2,1,0:T(8,128)(2,1)} %copy-done.33) | copy-start | bytes 7077892
  335.3 3.6 collective-permute-start.9
  335.5 3.1 collective-permute-start.8
  342.1 20.8 %collective-permute-start.12 = (bf16[4,48,1920]{2,1,0:T(8,128)(2,1)}, bf16[4,48,1920]{2,1,0:T(8,128)(2,1)}, u32[]{:S(2)}, u32[]{:S(2)}) collective-permute-start(bf16[4,48,1920]{2,1,0:T(8,128)(2,1)} %get-tuple-element.114), channel_id=1, source_target_pairs={{0,2},{1,3},{2,0},{3,1},{4,6},{5,7},{6,4},{7,5},{8,10},{9,11},{10,... | collective-permute-start | bytes 2211848 | tf_op jit(solution)/shard_map/ppermute | solution.py:520
  343.3 57.2 %collective-permute-start.4 = (bf16[832,768]{1,0:T(8,128)(2,1)}, bf16[832,768]{1,0:T(8,128)(2,1)}, u32[]{:S(2)}, u32[]{:S(2)}) collective-permute-start(bf16[832,768]{1,0:T(8,128)(2,1)} %copy-done.8), channel_id=1, source_target_pairs={{0,16},{1,17},{2,18},{3,19},{4,20},{5,21},{6,22},{7,23},{8,24},{9,... | collective-permute-start | bytes 3833864 | tf_op jit(solution)/shard_map/ppermute | solution.py:604
  347.9 13.4 %collective-permute-start.11 = (f32[6,768]{1,0:T(8,128)S(1)}, f32[6,768]{1,0:T(8,128)S(1)}, u32[]{:S(2)}, u32[]{:S(2)}) collective-permute-start(f32[6,768]{1,0:T(8,128)S(1)} %add.143), channel_id=1, source_target_pairs={{0,2},{1,3},{2,0},{3,1},{4,6},{5,7},{6,4},{7,5},{8,10},{9,11},{10,... | collective-permute-start | bytes 55304 | tf_op jit(solution)/shard_map/ppermute | solution.py:520
  350.4 15.1 %collective-permute-start.15 = (bf16[48,3072]{1,0:T(8,128)(2,1)S(1)}, bf16[48,3072]{1,0:T(8,128)(2,1)S(1)}, u32[]{:S(2)}, u32[]{:S(2)}) collective-permute-start(bf16[48,3072]{1,0:T(8,128)(2,1)S(1)} %get-tuple-element.116), channel_id=1, source_target_pairs={{0,12},{1,13},{2,14},{3,15},{4,8},{5,9},{6,10},{7,11},{8,4},{9,5},... | collective-permute-start | bytes 884744 | tf_op jit(solution)/shard_map/ppermute | solution.py:520
  352.5 26.6 %collective-permute-start.14 = (bf16[48,3072]{1,0:T(8,128)(2,1)S(1)}, bf16[48,3072]{1,0:T(8,128)(2,1)S(1)}, u32[]{:S(2)}, u32[]{:S(2)}) collective-permute-start(bf16[48,3072]{1,0:T(8,128)(2,1)S(1)} %get-tuple-element.117), channel_id=1, source_target_pairs={{0,8},{1,9},{2,10},{3,11},{4,12},{5,13},{6,14},{7,15},{8,0},{9,1},... | collective-permute-start | bytes 884744 | tf_op jit(solution)/shard_map/ppermute | solution.py:520
  361.4 17.8 %collective-permute-start.13 = (bf16[48,3072]{1,0:T(8,128)(2,1)S(1)}, bf16[48,3072]{1,0:T(8,128)(2,1)S(1)}, u32[]{:S(2)}, u32[]{:S(2)}) collective-permute-start(bf16[48,3072]{1,0:T(8,128)(2,1)S(1)} %get-tuple-element.118), channel_id=1, source_target_pairs={{0,4},{1,5},{2,6},{3,7},{4,0},{5,1},{6,2},{7,3},{8,12},{9,13},{10,... | collective-permute-start | bytes 884744 | tf_op jit(solution)/shard_map/ppermute | solution.py:520
  362.9 41.1 %collective-permute-start.10 = (bf16[832,768]{1,0:T(8,128)(2,1)}, bf16[832,768]{1,0:T(8,128)(2,1)}, u32[]{:S(2)}, u32[]{:S(2)}) collective-permute-start(bf16[832,768]{1,0:T(8,128)(2,1)} %get-tuple-element.88.mine_ref), channel_id=1, source_target_pairs={{16,0},{17,1},{18,2},{19,3},{20,4},{21,5},{22,6},{23,7},{24,8},{25... | collective-permute-start | bytes 3833864 | tf_op jit(solution)/shard_map/ppermute | solution.py:604
  365.5 16.6 %collective-permute-start.18 = (f32[6,768]{1,0:T(8,128)S(1)}, f32[6,768]{1,0:T(8,128)S(1)}, u32[]{:S(2)}, u32[]{:S(2)}) collective-permute-start(f32[6,768]{1,0:T(8,128)S(1)} %add.145), channel_id=1, source_target_pairs={{0,12},{1,13},{2,14},{3,15},{4,8},{5,9},{6,10},{7,11},{8,4},{9,5},... | collective-permute-start | bytes 55304 | tf_op jit(solution)/shard_map/ppermute | solution.py:520
  379.1 5.0 %collective-permute-start.17 = (f32[6,768]{1,0:T(8,128)S(1)}, f32[6,768]{1,0:T(8,128)S(1)}, u32[]{:S(2)}, u32[]{:S(2)}) collective-permute-start(f32[6,768]{1,0:T(8,128)S(1)} %add.145), channel_id=1, source_target_pairs={{0,8},{1,9},{2,10},{3,11},{4,12},{5,13},{6,14},{7,15},{8,0},{9,1},... | collective-permute-start | bytes 55304 | tf_op jit(solution)/shard_map/ppermute | solution.py:520
  379.1 5.0 %collective-permute-start.16 = (f32[6,768]{1,0:T(8,128)S(1)}, f32[6,768]{1,0:T(8,128)S(1)}, u32[]{:S(2)}, u32[]{:S(2)}) collective-permute-start(f32[6,768]{1,0:T(8,128)S(1)} %add.145), channel_id=1, source_target_pairs={{0,4},{1,5},{2,6},{3,7},{4,0},{5,1},{6,2},{7,3},{8,12},{9,13},{10,... | collective-permute-start | bytes 55304 | tf_op jit(solution)/shard_map/ppermute | solution.py:520
  382.1 9.4 %collective-permute-start.21 = (bf16[48,1920]{1,0:T(8,128)(2,1)S(1)}, bf16[48,1920]{1,0:T(8,128)(2,1)S(1)}, u32[]{:S(2)}, u32[]{:S(2)}) collective-permute-start(bf16[48,1920]{1,0:T(8,128)(2,1)S(1)} %get-tuple-element.130), channel_id=1, source_target_pairs={{0,12},{1,13},{2,14},{3,15},{4,8},{5,9},{6,10},{7,11},{8,4},{9,5},... | collective-permute-start | bytes 552968 | tf_op jit(solution)/shard_map/ppermute | solution.py:520
  384.1 14.9 %collective-permute-start.20 = (bf16[48,1920]{1,0:T(8,128)(2,1)S(1)}, bf16[48,1920]{1,0:T(8,128)(2,1)S(1)}, u32[]{:S(2)}, u32[]{:S(2)}) collective-permute-start(bf16[48,1920]{1,0:T(8,128)(2,1)S(1)} %get-tuple-element.131), channel_id=1, source_target_pairs={{0,8},{1,9},{2,10},{3,11},{4,12},{5,13},{6,14},{7,15},{8,0},{9,1},... | collective-permute-start | bytes 552968 | tf_op jit(solution)/shard_map/ppermute | solution.py:520
  384.1 14.9 %collective-permute-start.19 = (bf16[48,1920]{1,0:T(8,128)(2,1)S(1)}, bf16[48,1920]{1,0:T(8,128)(2,1)S(1)}, u32[]{:S(2)}, u32[]{:S(2)}) collective-permute-start(bf16[48,1920]{1,0:T(8,128)(2,1)S(1)} %get-tuple-element.132), channel_id=1, source_target_pairs={{0,4},{1,5},{2,6},{3,7},{4,0},{5,1},{6,2},{7,3},{8,12},{9,13},{10,... | collective-permute-start | bytes 552968 | tf_op jit(solution)/shard_map/ppermute | solution.py:520
  399.1 1.4 copy-start.9
  400.4 11.3 %collective-permute-start.22 = (bf16[48,4992]{1,0:T(8,128)(2,1)S(1)}, bf16[48,4992]{1,0:T(8,128)(2,1)S(1)}, u32[]{:S(2)}, u32[]{:S(2)}) collective-permute-start(bf16[48,4992]{1,0:T(8,128)(2,1)S(1)} %fusion.3), channel_id=1, source_target_pairs={{0,16},{16,0},{1,17},{17,1},{2,18},{18,2},{3,19},{19,3},{4,20},{20... | collective-permute-start | bytes 1437704 | tf_op jit(solution)/shard_map/ppermute | solution.py:601
  402.5 1.5 copy-start.2
  408.1 3.6 copy-start.37
  414.1 2.5 copy-start.36
  417.3 8.1 %collective-permute-start.23 = (f32[6,768]{1,0:T(8,128)S(1)}, f32[6,768]{1,0:T(8,128)S(1)}, u32[]{:S(2)}, u32[]{:S(2)}) collective-permute-start(f32[6,768]{1,0:T(8,128)S(1)} %add_add_fusion), channel_id=1, source_target_pairs={{0,16},{16,0},{1,17},{17,1},{2,18},{18,2},{3,19},{19,3},{4,20},{20... | collective-permute-start | bytes 55304 | tf_op jit(solution)/shard_map/ppermute | solution.py:601
  (11 other events, 11.0 us)
Sparse Core Ops, SparseCore 0:
  29.1 70.6 all-gather.2
  102.6 68.7 all-gather.4
  237.5 97.3 reduce-scatter.1

commit v3 on v2

--- a/solution.py
+++ b/solution.py
@@ -50,9 +50,9 @@
     return lax.broadcasted_iota(jnp.int32, (rows, 128), 1) // HEAD == h
 
 
-def params(steps):
+def params(steps, megabytes=20):
     return pltpu.CompilerParams(
-        dimension_semantics=("arbitrary",) * steps, vmem_limit_bytes=20 * 1024 * 1024
+        dimension_semantics=("arbitrary",) * steps, vmem_limit_bytes=megabytes * 1024 * 1024
     )
 
 
@@ -482,6 +482,705 @@
     )(place, *pieces, grad, qk_gain, 1.0 / qk_gain, normed, qk, v, r, pt, mixed, ff)
 
 
+def copy_all(pairs, sems, wait):
+    for at, (source, target) in enumerate(pairs):
+        copy = pltpu.make_async_copy(source, target, sems.at[at])
+        if wait:
+            copy.wait()
+        else:
+            copy.start()
+
+
+def weight_pairs(w_ref, units, attention_ref, up_ref, down_ref):
+    pairs = [
+        (w_ref.at[:, pl.ds(0, SPLIT)], attention_ref),
+        (w_ref.at[:, pl.ds(SPLIT, units)], up_ref),
+    ]
+    for part in range(units // D):
+        pairs.append((w_ref.at[:, pl.ds(SPLIT + units + part * D, D)], down_ref.at[part]))
+    return pairs
+
+
+def gelu(up):
+    square = up * up
+    tanh = jnp.tanh(up * (C0 + (C0 * C1) * square))
+    share = 0.5 + 0.5 * tanh
+    slope = share + up * (share * (1.0 - share)) * (2.0 * C0 + (6.0 * C0 * C1) * square)
+    return (up * share).astype(BF), slope
+
+
+def attend(tokens, qk_ref, v_ref, pt_ref, mixed_ref, rows):
+    pad = v_ref.shape[0]
+    valid = lax.broadcasted_iota(jnp.int32, (pad, pad), 0) < tokens
+    for pair in range(PAIRS):
+        lanes = slice(pair * 128, (pair + 1) * 128)
+        query = qk_ref[:, lanes]
+        key = qk_ref[:, HALF + pair * 128 : HALF + (pair + 1) * 128]
+        value = v_ref[:, lanes]
+        mixed = jnp.zeros((pad, 128), F32)
+        for h in range(2):
+            mask = half_mask(pad, h)
+            scores = dot_nt(jnp.where(mask, key, 0), query) * HEAD ** (-0.5)
+            scores = jnp.where(valid, scores, -1e30)
+            top = jnp.max(scores, axis=0, keepdims=True)
+            powers = jnp.exp(scores - top)
+            probs = (powers * (1.0 / jnp.sum(powers, axis=0, keepdims=True))).astype(BF)
+            pt_ref[2 * pair + h] = probs
+            mixed += dot_tn(probs, jnp.where(mask, value, 0))
+        mixed_ref[rows, lanes] = mixed.astype(BF)
+
+
+def attend_back(query_of, key_of, value_of, probs_of, d_mixed, d_qk_ref, d_qkv_ref, rows):
+    pad = d_mixed.shape[0]
+    for pair in range(PAIRS):
+        lanes = slice(pair * 128, (pair + 1) * 128)
+        query, key, value = query_of(pair), key_of(pair), value_of(pair)
+        d_mix = d_mixed[:, lanes]
+        d_query = jnp.zeros((pad, 128), F32)
+        d_key = jnp.zeros((pad, 128), F32)
+        d_value = jnp.zeros((pad, 128), F32)
+        for h in range(2):
+            mask = half_mask(pad, h)
+            d_mix_head = jnp.where(mask, d_mix, 0)
+            probs_low = probs_of(2 * pair + h)
+            probs = probs_low.astype(F32)
+            d_probs = dot_nt(value, d_mix_head)
+            weighted = jnp.sum(probs * d_probs, axis=0, keepdims=True)
+            d_scores = (probs * (d_probs - weighted)).astype(BF)
+            d_value += dot(probs_low, d_mix_head)
+            d_key += dot(d_scores, jnp.where(mask, query, 0))
+            d_query += dot_tn(d_scores, jnp.where(mask, key, 0))
+        d_qk_ref[:, lanes] = d_query * HEAD ** (-0.5)
+        d_qk_ref[:, HALF + pair * 128 : HALF + (pair + 1) * 128] = d_key * HEAD ** (-0.5)
+        d_qkv_ref[rows, D + pair * 128 : D + (pair + 1) * 128] = d_value.astype(BF)
+
+
+def head_norm_back(d_heads, shaped, rstd, gain):
+    scaled = d_heads * gain
+    return (rstd * (scaled - head_means(scaled) - shaped * head_means(scaled * shaped))).astype(BF)
+
+
+def whole_block_kernel(
+    tokens,
+    images,
+    units,
+    place,
+    w_ref,
+    x_ref,
+    g_ref,
+    ln_ref,
+    gain_ref,
+    part_ref,
+    out_ref,
+    sums_ref,
+    normed_hbm,
+    mixed_hbm,
+    hidden_hbm,
+    d_up_hbm,
+    d_qkv_hbm,
+    attention_ref,
+    up_ref,
+    down_ref,
+    normed_ref,
+    mixed_ref,
+    hidden_ref,
+    d_up_ref,
+    d_qkv_ref,
+    qk_ref,
+    v_ref,
+    shaped_ref,
+    rstd_ref,
+    pt_ref,
+    slope_ref,
+    d_qk_ref,
+    sems,
+    out_sems,
+):
+    section = place[0]
+    pairs = weight_pairs(w_ref, units, attention_ref, up_ref, down_ref)
+    copy_all(pairs, sems, False)
+    sums_ref[...] = jnp.zeros_like(sums_ref)
+    pad = x_ref.shape[0] // images
+    here = pl.ds(pl.multiple_of(section * HALF, HALF), HALF)
+
+    def leaving(image):
+        rows = pl.ds(pl.multiple_of(image * pad, pad), pad)
+        made = []
+        for source, target in (
+            (normed_ref, normed_hbm),
+            (mixed_ref, mixed_hbm),
+            (hidden_ref, hidden_hbm),
+            (d_up_ref, d_up_hbm),
+            (d_qkv_ref, d_qkv_hbm),
+        ):
+            made.append((source.at[rows, :], target.at[rows, :]))
+        return made
+
+    copy_all(pairs, sems, True)
+
+    def image_step(image, carry):
+        rows = pl.ds(pl.multiple_of(image * pad, pad), pad)
+        x = x_ref[rows, :].astype(F32)
+        centred = x - jnp.mean(x, axis=-1, keepdims=True)
+        spread = jnp.mean(centred * centred, axis=-1, keepdims=True)
+        normed = (centred * lax.rsqrt(spread + EPSILON) * ln_ref[...]).astype(BF)
+        normed_ref[rows, :] = normed
+        qkv = dot(normed, attention_ref[:, D:])
+        qk = qkv[:, :D]
+        centred = qk - head_means(qk)
+        rstd = lax.rsqrt(head_means(centred * centred) + EPSILON)
+        rstd_ref[...] = rstd
+        shaped = centred * rstd
+        shaped_ref[...] = shaped
+        qk_ref[...] = (shaped * gain_ref[...]).astype(BF)
+        v_ref[...] = qkv[:, D:].astype(BF)
+        attend(tokens, qk_ref, v_ref, pt_ref, mixed_ref, rows)
+        part = dot(mixed_ref[rows, :], attention_ref[here, :D])
+        grad = g_ref[rows, :]
+        hidden, slope = gelu(dot(normed, up_ref[...]))
+        hidden_ref[rows, :] = hidden
+        slope_ref[...] = slope
+        for at in range(units // D):
+            columns = slice(at * D, (at + 1) * D)
+            part += dot(hidden[:, columns], down_ref[at])
+            d_up_ref[rows, columns] = (slope_ref[:, columns] * dot_nt(grad, down_ref[at])).astype(BF)
+        part_ref[rows, :] = part.astype(BF)
+        d_normed = dot_nt(d_up_ref[rows, :], up_ref[...])
+        d_mixed = dot_nt(grad, attention_ref[here, :D]).astype(BF)
+        attend_back(
+            lambda pair: qk_ref[:, pair * 128 : (pair + 1) * 128],
+            lambda pair: qk_ref[:, HALF + pair * 128 : HALF + (pair + 1) * 128],
+            lambda pair: v_ref[:, pair * 128 : (pair + 1) * 128],
+            lambda head: pt_ref[head],
+            d_mixed,
+            d_qk_ref,
+            d_qkv_ref,
+            rows,
+        )
+        d_heads = d_qk_ref[...]
+        shaped = shaped_ref[...]
+        sums_ref[1:2, :] += jnp.sum(d_heads * shaped, axis=0, keepdims=True)
+        d_qkv_ref[rows, :D] = head_norm_back(d_heads, shaped, rstd_ref[...], gain_ref[...])
+        d_normed += dot_nt(d_qkv_ref[rows, :], attention_ref[:, D:])
+        out_ref[rows, :] = d_normed.astype(BF)
+        sums_ref[0:1, :] += jnp.sum(d_normed * normed_ref[rows, :].astype(F32), axis=0, keepdims=True)
+        copy_all(leaving(image), out_sems.at[image], False)
+        return carry
+
+    lax.fori_loop(0, images, image_step, 0)
+    for image in range(images):
+        copy_all(leaving(image), out_sems.at[image], True)
+
+
+def weight_grads_kernel(units, halves, place, *refs):
+    sources = [refs[6 * half : 6 * half + 6] for half in range(halves)]
+    grad_ref, hidden_ref, g_ref, normed_ref, d_up_ref, mixed_ref, d_qkv_ref, stage_ref, sems, out_sems = refs[6 * halves :]
+    targets = (hidden_ref, g_ref, normed_ref, d_up_ref, mixed_ref, d_qkv_ref)
+    pairs = []
+    for half in range(halves):
+        rows = sources[half][0].shape[0]
+        at = pl.ds(half * rows, rows)
+        pairs.append([(source, target.at[at, :]) for source, target in zip(sources[half], targets)])
+    for half in range(halves):
+        copy_all(pairs[half], sems.at[half], False)
+    for half in range(halves):
+        copy_all(pairs[half], sems.at[half], True)
+    section = place[0]
+    made = []
+    for at, columns in enumerate((pl.ds(SPLIT, 2 * units), pl.ds(0, SPLIT))):
+        if at == 0:
+            feed_grads(units, g_ref, normed_ref, hidden_ref, d_up_ref, stage_ref, SPLIT)
+        else:
+            attention_grads(section, g_ref, normed_ref, mixed_ref, d_qkv_ref, stage_ref)
+        made.append(
+            pltpu.make_async_copy(stage_ref.at[:, columns], grad_ref.at[:, columns], out_sems.at[at])
+        )
+        made[-1].start()
+    for copy in made:
+        copy.wait()
+
+
+def weight_grads(place, units, halves):
+    rows = sum(half[0].shape[0] for half in halves)
+    return pl.pallas_call(
+        partial(weight_grads_kernel, units, len(halves)),
+        grid_spec=pltpu.PrefetchScalarGridSpec(
+            num_scalar_prefetch=1,
+            grid=(1,),
+            in_specs=[ANYWHERE] * (6 * len(halves)),
+            out_specs=ANYWHERE,
+            scratch_shapes=[
+                pltpu.VMEM((rows, units), BF),
+                pltpu.VMEM((rows, D), BF),
+                pltpu.VMEM((rows, D), BF),
+                pltpu.VMEM((rows, units), BF),
+                pltpu.VMEM((rows, HALF), BF),
+                pltpu.VMEM((rows, 3 * HALF), BF),
+                pltpu.VMEM((D, SPLIT + 2 * units), BF),
+                pltpu.SemaphoreType.DMA((len(halves), 6)),
+                pltpu.SemaphoreType.DMA((2,)),
+            ],
+        ),
+        out_shape=jax.ShapeDtypeStruct((D, SPLIT + 2 * units), BF),
+        compiler_params=params(1, 36),
+        cost_estimate=pl.CostEstimate(
+            flops=2 * rows * D * (4 * HALF + 2 * units),
+            bytes_accessed=rows * (2 * units + 6 * HALF + 2 * D) * 2 + D * (SPLIT + 2 * units) * 2,
+            transcendentals=0,
+        ),
+        name="weight_grads",
+    )(place, *[value for half in halves for value in half])
+
+
+def copy_all_from(pairs, first, sems):
+    for at in range(first, len(pairs)):
+        pltpu.make_async_copy(pairs[at][0], pairs[at][1], sems.at[at]).wait()
+
+
+def feed_grads(units, g_ref, normed_ref, hidden_ref, d_up_ref, stage_ref, base):
+    for at in range(0, units, 512):
+        stage_ref[:, base + at : base + at + 512] = dot_tn(normed_ref[...], d_up_ref[:, at : at + 512]).astype(BF)
+    for at in range(0, units, 384):
+        rows = slice(at % D, at % D + 384)
+        columns = slice(base + units + at // D * D, base + units + at // D * D + D)
+        stage_ref[rows, columns] = dot_tn(hidden_ref[:, at : at + 384], g_ref[...]).astype(BF)
+
+
+def attention_grads(section, g_ref, normed_ref, mixed_ref, d_qkv_ref, stage_ref):
+    here = pl.ds(pl.multiple_of(section * HALF, HALF), HALF)
+    there = pl.ds(pl.multiple_of((1 - section) * HALF, HALF), HALF)
+    stage_ref[here, :D] = dot_tn(mixed_ref[...], g_ref[...]).astype(BF)
+    stage_ref[there, :D] = jnp.zeros((HALF, D), BF)
+    for at in range(0, 3 * HALF, 384):
+        stage_ref[:, D + at : D + at + 384] = dot_tn(normed_ref[...], d_qkv_ref[:, at : at + 384]).astype(BF)
+
+
+def whole_block(tokens, units, place, x, grad, weights, ln_gain, qk_gain, half, halves):
+    rows = x.shape[0] // halves
+    pad = pad_of(tokens)
+    images = rows // pad
+    full = lambda shape: pl.BlockSpec(shape, lambda i, s: (0, 0))
+    own = pl.BlockSpec((rows, D), lambda i, s: (half, 0))
+    widths = (D, HALF, units, units, 3 * HALF)
+    return pl.pallas_call(
+        partial(whole_block_kernel, tokens, images, units),
+        grid_spec=pltpu.PrefetchScalarGridSpec(
+            num_scalar_prefetch=1,
+            grid=(1,),
+            in_specs=[ANYWHERE, own, own, full((1, D)), full((1, D))],
+            out_specs=[full((rows, D)), full((rows, D)), full((8, D))] + [ANYWHERE] * 5,
+            scratch_shapes=[
+                pltpu.VMEM((D, SPLIT), BF),
+                pltpu.VMEM((D, units), BF),
+                pltpu.VMEM((units // D, D, D), BF),
+            ]
+            + [pltpu.VMEM((rows, width), BF) for width in widths]
+            + [
+                pltpu.VMEM((pad, D), BF),
+                pltpu.VMEM((pad, HALF), BF),
+                pltpu.VMEM((pad, D), F32),
+                pltpu.VMEM((pad, D), F32),
+                pltpu.VMEM((2 * PAIRS, pad, pad), BF),
+                pltpu.VMEM((pad, units), F32),
+                pltpu.VMEM((pad, D), F32),
+                pltpu.SemaphoreType.DMA((2 + units // D,)),
+                pltpu.SemaphoreType.DMA((images, 5)),
+            ],
+        ),
+        out_shape=[
+            jax.ShapeDtypeStruct((rows, D), BF),
+            jax.ShapeDtypeStruct((rows, D), BF),
+            jax.ShapeDtypeStruct((8, D), F32),
+        ]
+        + [jax.ShapeDtypeStruct((rows, width), BF) for width in widths],
+        compiler_params=params(1, 36),
+        cost_estimate=pl.CostEstimate(
+            flops=4 * rows * D * (4 * HALF + 2 * units),
+            bytes_accessed=rows * D * 20 + D * (SPLIT + 2 * units) * 2,
+            transcendentals=rows * units,
+        ),
+        name="whole_block",
+    )(place, weights, x, grad, ln_gain, qk_gain)
+
+
+def spread(place, count, stage_ref, columns, mine_ref, sent_ref, sems):
+    core, near, far = place[1], place[2], place[3]
+    rows = stage_ref.shape[0] // count
+    made = []
+    for which, target in enumerate((sent_ref, mine_ref)):
+        for at in range(count // 2):
+            other, step = at // (count // 4), at % (count // 4)
+            device = (far ^ step) * 4 + (near ^ other) * 2 + (core if which else 1 - core)
+            source = stage_ref.at[pl.ds(pl.multiple_of(device * rows, rows), rows), columns]
+            made.append(
+                pltpu.make_async_copy(
+                    source, target.at[pl.ds(at * rows, rows), columns], sems.at[which * (count // 2) + at]
+                )
+            )
+    return made
+
+
+def feed_back_kernel(
+    images,
+    units,
+    count,
+    place,
+    w_ref,
+    g_hbm,
+    normed_hbm,
+    hidden_hbm,
+    slope_hbm,
+    out_ref,
+    mine_ref,
+    sent_ref,
+    up_ref,
+    down_ref,
+    g_ref,
+    normed_ref,
+    hidden_ref,
+    slope_ref,
+    d_up_ref,
+    stage_ref,
+    sems,
+    out_sems,
+):
+    pairs = []
+    for part in range(units // D):
+        pairs.append((w_ref.at[:, pl.ds(SPLIT + units + part * D, D)], down_ref.at[part]))
+    pairs += [
+        (g_hbm, g_ref),
+        (slope_hbm, slope_ref),
+        (w_ref.at[:, pl.ds(SPLIT, units)], up_ref),
+        (hidden_hbm, hidden_ref),
+        (normed_hbm, normed_ref),
+    ]
+    ready = len(pairs) - 2
+    copy_all(pairs, sems, False)
+    copy_all(pairs[:ready], sems, True)
+    pad = g_ref.shape[0] // images
+
+    def image_step(image, carry):
+        rows = pl.ds(pl.multiple_of(image * pad, pad), pad)
+        grad = g_ref[rows, :]
+        for at in range(units // D):
+            columns = slice(at * D, (at + 1) * D)
+            d_up_ref[rows, columns] = (
+                slope_ref[rows, columns].astype(F32) * dot_nt(grad, down_ref[at])
+            ).astype(BF)
+        out_ref[rows, :] = dot_nt(d_up_ref[rows, :], up_ref[...]).astype(BF)
+        return carry
+
+    lax.fori_loop(0, images, image_step, 0)
+    copy_all_from(pairs, ready, sems)
+    for at in range(0, units, 384):
+        rows = slice(at % D, at % D + 384)
+        columns = slice(units + at // D * D, units + at // D * D + D)
+        stage_ref[rows, columns] = dot_tn(hidden_ref[:, at : at + 384], g_ref[...]).astype(BF)
+    downs = spread(place, count, stage_ref, pl.ds(units, units), mine_ref, sent_ref, out_sems.at[0])
+    for copy in downs:
+        copy.start()
+    for at in range(0, units, 512):
+        stage_ref[:, at : at + 512] = dot_tn(normed_ref[...], d_up_ref[:, at : at + 512]).astype(BF)
+    ups = spread(place, count, stage_ref, pl.ds(0, units), mine_ref, sent_ref, out_sems.at[1])
+    for copy in ups:
+        copy.start()
+    for copy in downs + ups:
+        copy.wait()
+
+
+def feed_back(place, units, count, grad, weights, normed, hidden, slope):
+    rows = normed.shape[0]
+    images = 4 if rows % 64 == 0 else 1
+    sends = D // 2
+    return pl.pallas_call(
+        partial(feed_back_kernel, images, units, count),
+        grid_spec=pltpu.PrefetchScalarGridSpec(
+            num_scalar_prefetch=1,
+            grid=(1,),
+            in_specs=[ANYWHERE] * 5,
+            out_specs=[pl.BlockSpec((rows, D), lambda i, s: (0, 0)), ANYWHERE, ANYWHERE],
+            scratch_shapes=[
+                pltpu.VMEM((D, units), BF),
+                pltpu.VMEM((units // D, D, D), BF),
+                pltpu.VMEM((rows, D), BF),
+                pltpu.VMEM((rows, D), BF),
+                pltpu.VMEM((rows, units), BF),
+                pltpu.VMEM((rows, units), BF),
+                pltpu.VMEM((rows, units), BF),
+                pltpu.VMEM((D, 2 * units), BF),
+                pltpu.SemaphoreType.DMA((5 + units // D,)),
+                pltpu.SemaphoreType.DMA((2, count)),
+            ],
+        ),
+        out_shape=[
+            jax.ShapeDtypeStruct((rows, D), BF),
+            jax.ShapeDtypeStruct((sends, 2 * units), BF),
+            jax.ShapeDtypeStruct((sends, 2 * units), BF),
+        ],
+        compiler_params=params(1, 36),
+        cost_estimate=pl.CostEstimate(
+            flops=8 * rows * D * units,
+            bytes_accessed=rows * D * 6 + rows * units * 4 + D * units * 8,
+            transcendentals=0,
+        ),
+        name="feed_back",
+    )(place, weights, grad, normed, hidden, slope)
+
+
+def attention_back_kernel(
+    images,
+    count,
+    place,
+    w_hbm,
+    g_hbm,
+    qk_hbm,
+    v_hbm,
+    r_hbm,
+    pt_hbm,
+    ff_hbm,
+    normed_hbm,
+    mixed_hbm,
+    gain_ref,
+    inverse_ref,
+    ln_inverse_ref,
+    sums_ref,
+    out_ref,
+    mine_ref,
+    sent_ref,
+    w_ref,
+    g_ref,
+    qk_ref,
+    v_ref,
+    r_ref,
+    pt_ref,
+    ff_ref,
+    normed_ref,
+    mixed_ref,
+    d_qk_ref,
+    d_qkv_ref,
+    stage_ref,
+    total_ref,
+    gains_ref,
+    low_ref,
+    sems,
+    mixed_sem,
+    out_sems,
+):
+    section = place[0]
+    pad = g_ref.shape[0] // images
+    here = pl.ds(pl.multiple_of(section * HALF, HALF), HALF)
+
+    def pairs_of(image):
+        rows = pl.ds(pl.multiple_of(image * pad, pad), pad)
+        pairs = [(pt_hbm.at[image], pt_ref.at[image])]
+        for source, target in (
+            (g_hbm, g_ref),
+            (v_hbm, v_ref),
+            (qk_hbm, qk_ref),
+            (r_hbm, r_ref),
+            (ff_hbm, ff_ref),
+            (normed_hbm, normed_ref),
+        ):
+            pairs.append((source.at[rows, :], target.at[rows, :]))
+        return pairs
+
+    once = [(w_hbm.at[:, pl.ds(0, SPLIT)], w_ref), (mixed_hbm, mixed_ref)]
+    copy_all(once[:1], mixed_sem, False)
+    for image in range(images):
+        copy_all(pairs_of(image), sems.at[image], False)
+    pltpu.make_async_copy(once[1][0], once[1][1], mixed_sem.at[1]).start()
+    total_ref[...] = jnp.zeros_like(total_ref)
+    copy_all(once[:1], mixed_sem, True)
+
+    def image_step(image, carry):
+        rows = pl.ds(pl.multiple_of(image * pad, pad), pad)
+        copy_all(pairs_of(image), sems.at[image], True)
+        d_mixed = dot_nt(g_ref[rows, :], w_ref[here, :D]).astype(BF)
+        attend_back(
+            lambda pair: qk_ref[rows, pair * 128 : (pair + 1) * 128],
+            lambda pair: qk_ref[rows, HALF + pair * 128 : HALF + (pair + 1) * 128],
+            lambda pair: v_ref[rows, pair * 128 : (pair + 1) * 128],
+            lambda head: pt_ref[image, head],
+            d_mixed,
+            d_qk_ref,
+            d_qkv_ref,
+            rows,
+        )
+        d_heads = d_qk_ref[...]
+        shaped = qk_ref[rows, :].astype(F32) * inverse_ref[...]
+        total_ref[1:2, :] += jnp.sum(d_heads * shaped, axis=0, keepdims=True)
+        d_qkv_ref[rows, :D] = head_norm_back(d_heads, shaped, r_ref[rows, :].astype(F32), gain_ref[...])
+        d_normed = dot_nt(d_qkv_ref[rows, :], w_ref[:, D:]) + ff_ref[rows, :].astype(F32)
+        out_ref[rows, :] = d_normed.astype(BF)
+        total_ref[0:1, :] += jnp.sum(d_normed * normed_ref[rows, :].astype(F32), axis=0, keepdims=True)
+        return carry
+
+    lax.fori_loop(0, images, image_step, 0)
+    pltpu.make_async_copy(once[1][0], once[1][1], mixed_sem.at[1]).wait()
+    gains_ref[...] = jnp.zeros_like(gains_ref)
+    for block, source in enumerate((total_ref, sums_ref)):
+        at = 3 * block
+        gains_ref[at : at + 1, :D] = source[0:1, :] * ln_inverse_ref[block : block + 1, :]
+        gains_ref[at + 1 : at + 2, here] = source[1:2, :HALF]
+        gains_ref[at + 2 : at + 3, here] = source[1:2, HALF:]
+    low_ref[...] = gains_ref[...].astype(BF)
+    sends = D // 2
+    made = []
+    for which, target in enumerate((sent_ref, mine_ref)):
+        made.append(
+            pltpu.make_async_copy(low_ref, target.at[pl.ds(sends, 16), :], out_sems.at[count + which])
+        )
+    attention_grads(section, g_ref, normed_ref, mixed_ref, d_qkv_ref, stage_ref)
+    made += spread(place, count, stage_ref, pl.ds(0, SPLIT), mine_ref, sent_ref, out_sems)
+    for copy in made:
+        copy.start()
+    for copy in made:
+        copy.wait()
+
+
+def attention_back(tokens, place, count, grad, weights, qk_gain, ln_inverse, sums, normed, qk, v, r, pt, mixed, ff):
+    rows = normed.shape[0]
+    pad = pad_of(tokens)
+    images = rows // pad
+    sends = D // 2
+    full = lambda shape: pl.BlockSpec(shape, lambda i, s: (0, 0))
+    return pl.pallas_call(
+        partial(attention_back_kernel, images, count),
+        grid_spec=pltpu.PrefetchScalarGridSpec(
+            num_scalar_prefetch=1,
+            grid=(1,),
+            in_specs=[ANYWHERE] * 9 + [full((1, D)), full((1, D)), full((2, D)), full((8, D))],
+            out_specs=[full((rows, D)), ANYWHERE, ANYWHERE],
+            scratch_shapes=[
+                pltpu.VMEM((D, SPLIT), BF),
+                pltpu.VMEM((rows, D), BF),
+                pltpu.VMEM((rows, D), BF),
+                pltpu.VMEM((rows, HALF), BF),
+                pltpu.VMEM((rows, D), BF),
+                pltpu.VMEM((images, 2 * PAIRS, pad, pad), BF),
+                pltpu.VMEM((rows, D), BF),
+                pltpu.VMEM((rows, D), BF),
+                pltpu.VMEM((rows, HALF), BF),
+                pltpu.VMEM((pad, D), F32),
+                pltpu.VMEM((rows, 3 * HALF), BF),
+                pltpu.VMEM((D, SPLIT), BF),
+                pltpu.VMEM((8, D), F32),
+                pltpu.VMEM((16, SPLIT), F32),
+                pltpu.VMEM((16, SPLIT), BF),
+                pltpu.SemaphoreType.DMA((images, 7)),
+                pltpu.SemaphoreType.DMA((2,)),
+                pltpu.SemaphoreType.DMA((count + 2,)),
+            ],
+        ),
+        out_shape=[
+            jax.ShapeDtypeStruct((rows, D), BF),
+            jax.ShapeDtypeStruct((sends + 16, SPLIT), BF),
+            jax.ShapeDtypeStruct((sends + 16, SPLIT), BF),
+        ],
+        compiler_params=params(1, 36),
+        cost_estimate=pl.CostEstimate(
+            flops=4 * rows * D * 4 * HALF + 16 * images * 6 * pad * pad * 64,
+            bytes_accessed=rows * D * 16 + D * SPLIT * 4,
+            transcendentals=0,
+        ),
+        name="attention_back",
+    )(place, weights, grad, qk, v, r, pt, ff, normed, mixed, qk_gain, 1.0 / qk_gain, ln_inverse, sums)
+
+
+def pack_kernel(count, place, qkv_ref, up_ref, proj_ref, down_ref, mine_ref, theirs_ref):
+    rows = qkv_ref.shape[0]
+    group = up_ref.shape[1] // (4 * count)
+    section = place[0]
+    up = up_ref[...].astype(F32)
+    ups = []
+    for part in range(4):
+        pieces = [up[:, (4 * at + part) * group : (4 * at + part + 1) * group] for at in range(count)]
+        ups.append(jnp.concatenate(pieces, axis=1).astype(BF))
+    for half, target in ((section, mine_ref), (1 - section, theirs_ref)):
+        target[:, :D] = proj_ref[...]
+        for pair in range(3):
+            source = pl.ds(pl.multiple_of(pair * D + half * HALF, HALF), HALF)
+            target[:, D + pair * HALF : D + (pair + 1) * HALF] = qkv_ref[:, source]
+        for part in range(2):
+            at = SPLIT + part * D
+            target[:, at : at + D] = jnp.where(half == 0, ups[part], ups[2 + part])
+            at = SPLIT + (2 + part) * D
+            source = pl.ds(pl.multiple_of((2 * half + part) * rows, rows), rows)
+            target[:, at : at + D] = down_ref[source, :]
+
+
+def pack(place, count, w_qkv, w_up, w_proj, w_down):
+    rows = w_qkv.shape[0]
+    width = SPLIT + w_up.shape[1]
+    full = lambda value: pl.BlockSpec(value.shape, lambda i, s: (0, 0))
+    shape = jax.ShapeDtypeStruct((rows, width), BF)
+    return pl.pallas_call(
+        partial(pack_kernel, count),
+        grid_spec=pltpu.PrefetchScalarGridSpec(
+            num_scalar_prefetch=1,
+            grid=(1,),
+            in_specs=[full(value) for value in (w_qkv, w_up, w_proj, w_down)],
+            out_specs=[full(shape)] * 2,
+        ),
+        out_shape=[shape] * 2,
+        compiler_params=params(1),
+        name="pack",
+    )(place, w_qkv, w_up, w_proj, w_down)
+
+
+def finish_feed_kernel(count, place, sum_ref, arrived_ref, second_ref, second_arrived_ref, up_ref, down_ref):
+    rows = sum_ref.shape[0]
+    units = sum_ref.shape[1] // 2
+    group = units // (2 * count)
+    first = place[0] == 0
+    low = jnp.where(first, sum_ref[...], second_arrived_ref[:, SPLIT:]).astype(F32)
+    high = jnp.where(first, arrived_ref[...], second_ref[:, SPLIT:]).astype(F32)
+    sources = (low, low, high, high)
+    pieces = []
+    for at in range(count):
+        for part, source in enumerate(sources):
+            column = part % 2 * D + at * group
+            pieces.append(source[:, column : column + group])
+    up_ref[...] = jnp.concatenate(pieces, axis=1)
+    for part, source in enumerate(sources):
+        column = units + part % 2 * D
+        down_ref[part * rows : (part + 1) * rows, :] = source[:, column : column + D]
+
+
+def finish_attention_kernel(
+    place, sum_ref, arrived_ref, second_ref, second_arrived_ref, qkv_ref, proj_ref, ln_ref, query_ref, key_ref
+):
+    rows = qkv_ref.shape[0]
+    first = place[0] == 0
+    low = jnp.where(first, sum_ref[:rows, :], second_arrived_ref[:, :SPLIT]).astype(F32)
+    high = jnp.where(first, arrived_ref[:rows, :], second_ref[:, :SPLIT]).astype(F32)
+    proj_ref[...] = low[:, :D] + high[:, :D]
+    for pair in range(3):
+        at = D + pair * HALF
+        qkv_ref[:, pair * D : pair * D + HALF] = low[:, at : at + HALF]
+        qkv_ref[:, pair * D + HALF : (pair + 1) * D] = high[:, at : at + HALF]
+    gains = sum_ref[rows:, :D].astype(F32) + arrived_ref[rows:, :D].astype(F32)
+    for at, target in enumerate((ln_ref, query_ref, key_ref)):
+        target[...] = jnp.where(first, gains[at : at + 1, :], gains[3 + at : 4 + at, :])
+
+
+def finish(kernel, name, place, values, shapes):
+    full = lambda value: pl.BlockSpec(value.shape, lambda i, s: (0, 0))
+    shapes = [jax.ShapeDtypeStruct(shape, F32) for shape in shapes]
+    return pl.pallas_call(
+        kernel,
+        grid_spec=pltpu.PrefetchScalarGridSpec(
+            num_scalar_prefetch=1,
+            grid=(1,),
+            in_specs=[full(value) for value in values],
+            out_specs=[full(shape) for shape in shapes],
+        ),
+        out_shape=shapes,
+        compiler_params=params(1),
+        name=name,
+    )(place, *values)
+
+
 def norm_backward_kernel(g_ref, x_ref, mine_ref, theirs_ref, ln_ref, out_ref):
     x = x_ref[...].astype(F32)
     centred = x - jnp.mean(x, axis=-1, keepdims=True)
@@ -524,59 +1223,8 @@
     return lax.optimization_barrier((value,) + others)[0]
 
 
-def gather_far(shard):
-    count = lax.axis_size("dp")
-    return [shard] + [relative(shard, 4 * far) for far in range(1, count // 4)]
-
-
-def gather_near(quads):
-    nears = [relative(piece, 2) for piece in quads]
-    pieces = []
-    for left, right in zip(quads, nears):
-        pieces += [left, relative(left, 1), right, relative(right, 1)]
-    rows, width = pieces[0].shape
-    if rows % 16 == 0:
-        return pieces
-    me = lax.axis_index("dp")
-    whole = jnp.zeros((len(pieces), rows, width), BF)
-    for step, piece in enumerate(pieces):
-        whole = lax.dynamic_update_slice(whole, piece[None], (me ^ step, 0, 0))
-    return [whole.reshape(len(pieces) * rows, width)]
-
-
 def add_low(left, right):
     return (left.astype(F32) + right.astype(F32)).astype(BF)
-
-
-def pick(value, at, axis):
-    return lax.dynamic_index_in_dim(value, at, axis, keepdims=False)
-
-
-def coordinates():
-    me = lax.axis_index("dp")
-    return me % 2, (me // 2) % 2, me // 4
-
-
-def scatter_core(terms):
-    count = lax.axis_size("dp")
-    core, _, _ = coordinates()
-    rows, width = terms.shape
-    shaped = terms.reshape(count // 4, 2, 2, rows // count, width)
-    return pick(shaped, core, 2), pick(shaped, 1 - core, 2)
-
-
-def scatter_near(total):
-    _, near, _ = coordinates()
-    return pick(total, near, 1), pick(total, 1 - near, 1)
-
-
-def scatter_far(total):
-    count = lax.axis_size("dp")
-    _, _, far = coordinates()
-    terms = [pick(total, far, 0)]
-    for step in range(1, count // 4):
-        terms.append(relative(pick(total, far ^ step, 0), 4 * step))
-    return terms
 
 
 def add_all(terms):
@@ -584,6 +1232,13 @@
     for term in terms[1:]:
         result = result + term.astype(F32)
     return result
+
+
+def spread_rows(terms, count, place):
+    at = jnp.arange(count // 2)
+    device = (place[3] ^ (at % (count // 4))) * 4 + (place[2] ^ (at // (count // 4))) * 2
+    shaped = terms.reshape(count, terms.shape[0] // count, terms.shape[1])
+    return [shaped[device + core].reshape(-1, terms.shape[1]) for core in (place[1], 1 - place[1])]
 
 
 def on_device(images, cotangent, w_qkv, w_up, w_proj, w_down, ln_gain, q_gain, k_gain):
@@ -603,7 +1258,8 @@
     def give(value, source):
         return lax.ppermute(value, "section", [(source, 1 - source)])
 
-    place = jnp.stack([section, 0 * me]).astype(jnp.int32)
+    place = jnp.stack([section, me % 2, (me // 2) % 2, me // 4]).astype(jnp.int32)
+    aligned = rows % 16 == 0
 
     def attention_half(half):
         parts = [w_proj[0]]
@@ -621,20 +1277,16 @@
             parts.append(w_down[0, part * group : (part + 1) * group])
         return jnp.concatenate(parts, axis=1)
 
-    shards = [[None, None], [None, None]]
-    held = None
-    for kind, half_of in enumerate((attention_half, feed_half)):
-        halves = (half_of(0), half_of(1))
-        mine = jnp.where(first, halves[0], halves[1])
-        theirs = jnp.where(first, halves[1], halves[0])
-        other = swap(theirs if held is None else after(theirs, held))
-        held = other
-        shards[0][kind] = jnp.where(first, mine, other)
-        shards[1][kind] = jnp.where(first, other, mine)
-
+    if aligned:
+        mine, theirs = pack(place, count, w_qkv[0], w_up[0], w_proj[0], w_down[0])
+    else:
+        low, high = (jnp.concatenate([attention_half(half), feed_half(half)], axis=1) for half in range(2))
+        mine, theirs = jnp.where(first, low, high), jnp.where(first, high, low)
+    other = swap(theirs)
     own_gains = jnp.concatenate([ln_gain, q_gain, k_gain], axis=0)
-    their_gains = swap(after(own_gains, *shards[0]))
+    their_gains = swap(own_gains)
     gains = (jnp.where(first, own_gains, their_gains), jnp.where(first, their_gains, own_gains))
+    shards = (jnp.where(first, mine, after(other, their_gains)), jnp.where(first, other, mine))
 
     at_half = lambda gain: lax.dynamic_slice_in_dim(gain, section * HALF, HALF, 0)
     ln_gains = [gains[block][:1] for block in range(2)]
@@ -650,98 +1302,146 @@
 
     weights = []
     for block in range(2):
-        shard = jnp.concatenate(shards[block], axis=1)
+        shard = shards[block]
         if block == 1:
             shard = after(shard, weights[0][0])
         weights.append([lax.all_gather(shard, "dp", axis=0, tiled=True)])
 
-    inputs, kept, parts = [padded(images)], [], []
-    for block in range(2):
-        saved = attention_forward(
-            tokens, place, inputs[block], weights[block], ln_gains[block], qk_gains[block]
+    first_in = padded(images)
+    none = jnp.stack([section, 0 * section]).astype(jnp.int32)
+    saved = attention_forward(tokens, none, first_in, weights[0], ln_gains[0], qk_gains[0])
+    hidden, slope, part = feed_forward(none, units, saved[0], weights[0], saved[6])
+    kept = tuple(saved[:6]) + (hidden, slope)
+    middle = (first_in.astype(F32) + part.astype(F32) + swap(part).astype(F32)).astype(BF)
+
+    grad = padded(cotangent)
+    halves, last_parts, parts, theirs, sums_1 = [], [], [], [], 0
+    for half in range(2):
+        last_half, part, sums, normed, mixed, hidden, d_up, d_qkv = whole_block(
+            tokens, units, place, middle, grad, weights[1][0], ln_gains[1], qk_gains[1], half, 2
         )
-        hidden, slope, part = feed_forward(place, units, saved[0], weights[block], saved[6])
-        kept.append(tuple(saved[:6]) + (hidden, slope))
+        own = slice(half * (number // 2) * pad, (half + 1) * (number // 2) * pad)
+        halves.append((hidden, grad[own], normed, d_up, mixed, d_qkv))
+        last_parts.append(last_half)
         parts.append(part)
-        if block == 0:
-            inputs.append((inputs[0].astype(F32) + part.astype(F32) + swap(part).astype(F32)).astype(BF))
-
-    def feed_step(block, grad):
-        normed, hidden, slope = kept[block][0], kept[block][6], kept[block][7]
-        return feed_backward(place, units, grad, normed, weights[block], hidden, slope)
-
-    def attention_step(block, grad, feed_part):
-        return attention_backward(
-            tokens, place, grad, weights[block], qk_gains[block], *kept[block][:6], feed_part
+        theirs.append(swap(part))
+        sums_1 = sums_1 + sums
+    halves[1] = (after(halves[1][0], theirs[0]),) + halves[1][1:]
+    terms = weight_grads(place, units, halves)
+    second_sum = lax.psum_scatter(terms, "dp", scatter_dimension=0, tiled=True)
+    middle_grad = norm_backward(
+        after(grad, terms), middle, jnp.concatenate(parts), jnp.concatenate(theirs), ln_gains[1]
+    )
+    last_part = jnp.concatenate(last_parts)
+
+    quarter = count // 4 * rows
+    if aligned:
+        feed_part, mine, sent = feed_back(place, units, count, middle_grad, weights[0][0], kept[0], *kept[6:])
+    else:
+        terms, feed_part = feed_backward(none, units, middle_grad, kept[0], weights[0], *kept[6:])
+        mine, sent = spread_rows(terms, count, place)
+    total = add_low(mine, relative(sent, 1))
+    sent = total[quarter:]
+    arrived = relative(sent, 2)
+    ln_inverse = 1.0 / jnp.concatenate(ln_gains, axis=0)
+    attention_in = after(middle_grad, sent)
+    if aligned:
+        part, mine, sent = attention_back(
+            tokens, place, count, attention_in, weights[0][0], qk_gains[0], ln_inverse, sums_1, *kept[:6], feed_part
         )
-
-    def core_stage(terms):
-        mine, sent = scatter_core(terms)
-        return mine, relative(sent, 1)
-
-    def near_stage(mine, arrived):
-        mine, sent = scatter_near(add_low(mine, arrived))
-        return mine, sent, relative(sent, 2)
-
-    grad = padded(cotangent)
-    feed_grads, feed_part = feed_step(1, grad)
-    attention_grads, part, sums_1 = attention_step(1, grad, feed_part)
-    theirs = swap(part)
-    terms = jnp.concatenate([attention_grads, feed_grads], axis=1)
-    second_sum = lax.psum_scatter(terms, "dp", scatter_dimension=0, tiled=True).astype(F32)
-    middle_grad = norm_backward(grad, inputs[1], part, theirs, ln_gains[1])
-    feed_grads, feed_part = feed_step(0, middle_grad)
-
-    feed_near = near_stage(*core_stage(feed_grads))
-    attention_grads, part, sums_0 = attention_step(0, after(middle_grad, feed_near[1]), feed_part)
-    feed_far = add_low(feed_near[0], feed_near[2])
-    feed_terms = scatter_far(feed_far)
-
-    gain_rows = []
-    for block, sums in enumerate((sums_0, sums_1)):
-        zero = jnp.zeros((D,), F32)
-        put = lambda value: lax.dynamic_update_slice_in_dim(zero, value, section * HALF, 0)
-        gain_rows += [sums[0] / gains[block][0], put(sums[1, :HALF]), put(sums[1, HALF:])]
-    totals = jnp.stack(gain_rows)
-
-    kept_rows, arrived = core_stage(after(attention_grads, feed_far))
-    totals = totals + relative(after(totals, feed_far), 1)
-    kept_rows, sent_rows, arrived = near_stage(after(kept_rows, totals), arrived)
-    totals = totals + relative(after(totals, sent_rows), 2)
-    attention_far = add_low(after(kept_rows, totals), arrived)
-    attention_terms = scatter_far(attention_far)
-    after_far = after(totals, attention_far)
-    totals = add_all([totals] + [relative(after_far, 4 * far) for far in range(1, count // 4)])
-    feed_sum = add_all([after(feed_terms[0], attention_far)] + feed_terms[1:])
-    attention_sum = add_all([after(attention_terms[0], feed_sum, totals)] + attention_terms[1:])
-    theirs = give(after(part, sent_rows), 1)
-    summed = [jnp.concatenate([attention_sum, feed_sum], axis=1), second_sum]
-    first_grad = norm_backward(middle_grad, inputs[0], part, theirs, ln_gains[0])
+    else:
+        terms, part, sums_0 = attention_backward(
+            tokens, none, attention_in, weights[0], qk_gains[0], *kept[:6], feed_part
+        )
+        mine, sent = spread_rows(terms, count, place)
+        gain_rows = jnp.zeros((16, SPLIT), F32)
+        for block, sums in enumerate((sums_0, sums_1)):
+            gain_rows = gain_rows.at[3 * block, :D].set(sums[0] * ln_inverse[block])
+            for kind in range(2):
+                value = sums[1:2, kind * HALF : (kind + 1) * HALF]
+                gain_rows = lax.dynamic_update_slice(gain_rows, value, (3 * block + 1 + kind, section * HALF))
+        mine, sent = (jnp.concatenate([value, gain_rows.astype(BF)], axis=0) for value in (mine, sent))
+    far_total = add_low(total[:quarter], arrived)
+    far = range(1, count // 4)
+    feed_terms = [far_total[:rows]]
+    for step in far:
+        feed_terms.append(relative(far_total[step * rows : (step + 1) * rows], 4 * step))
+
+    total = add_low(mine, relative(after(sent, far_total), 1))
+    sent = total[quarter:]
+    arrived = relative(sent, 2)
+    theirs = give(part, 1)
+    last_theirs = give(after(last_part, part), 0)
+    far_total = add_low(total[:quarter], arrived[:quarter])
+    gain_total = add_low(total[2 * quarter :], arrived[quarter:])
+    attention_terms = [jnp.concatenate([far_total[:rows], gain_total], axis=0)]
+    for step in far:
+        message = jnp.concatenate([far_total[step * rows : (step + 1) * rows], gain_total], axis=0)
+        attention_terms.append(relative(message, 4 * step))
+    second_theirs = give(second_sum, 0)
+    feed_sum = add_all([after(feed_terms[0], far_total)] + feed_terms[1:]).astype(BF)
+    feed_theirs = give(feed_sum, 1)
+    attention_sum = add_all([after(attention_terms[0], feed_sum, second_theirs, theirs)] + attention_terms[1:]).astype(BF)
+    attention_theirs = swap(attention_sum)
+
+    first_grad = norm_backward(middle_grad, first_in, after(part, attention_sum), theirs, ln_gains[0])
     input_grads = trimmed(jnp.where(first, first_grad, middle_grad))
-    last = (inputs[1].astype(F32) + parts[1].astype(F32)) + give(parts[1], 0).astype(F32)
-    outputs = trimmed(jnp.where(first, inputs[1], last.astype(BF)))
-
-    own = jnp.where(first, summed[0], summed[1])
-    theirs = swap(jnp.where(first, summed[1], summed[0]).astype(BF)).astype(F32)
-    low_half = jnp.where(first, own, theirs)
-    high_half = jnp.where(first, theirs, own)
-    grad_proj = own[:, :D] + theirs[:, :D]
+    last_theirs = after(last_theirs, feed_sum)
+    last = middle.astype(F32) + last_part.astype(F32) + last_theirs.astype(F32)
+    outputs = trimmed(jnp.where(first, middle, last.astype(BF)))
+
+    if aligned:
+        grad_up, grad_down = finish(
+            partial(finish_feed_kernel, count),
+            "finish_feed",
+            place,
+            (feed_sum, feed_theirs, second_sum, second_theirs),
+            ((rows, 2 * units), (4 * rows, D)),
+        )
+        grad_qkv, grad_proj, grad_ln, grad_q, grad_k = finish(
+            finish_attention_kernel,
+            "finish_attention",
+            place,
+            (attention_sum, attention_theirs, second_sum, second_theirs),
+            ((rows, 3 * D), (rows, D), (1, D), (1, D), (1, D)),
+        )
+        return (
+            outputs[None],
+            input_grads[None],
+            grad_qkv[None],
+            grad_up[None],
+            grad_proj[None],
+            grad_down[None],
+            grad_ln,
+            grad_q,
+            grad_k,
+        )
+
+    def halves_of(own, theirs):
+        own, theirs = own.astype(F32), theirs.astype(F32)
+        return jnp.where(first, own, theirs), jnp.where(first, theirs, own)
+
+    own = jnp.where(first, feed_sum, second_sum[:, SPLIT:])
+    other = jnp.where(first, feed_theirs, second_theirs[:, SPLIT:])
+    ups, downs = [], []
+    for source in halves_of(own, other):
+        for part in range(2):
+            at = part * D
+            ups.append(source[:, at : at + D].reshape(rows, count, 1, group))
+            downs.append(source[:, units + at : units + at + D])
+    grad_up = jnp.concatenate(ups, axis=2).reshape(rows, 2 * units)
+    grad_down = jnp.concatenate(downs, axis=0)
+
+    own = jnp.where(first, attention_sum[:rows], second_sum[:, :SPLIT])
+    other = jnp.where(first, attention_theirs[:rows], second_theirs[:, :SPLIT])
+    low_half, high_half = halves_of(own, other)
+    grad_proj = low_half[:, :D] + high_half[:, :D]
     pieces = []
     for pair in range(3):
         at = slice(D + pair * HALF, D + (pair + 1) * HALF)
         pieces += [low_half[:, at], high_half[:, at]]
     grad_qkv = jnp.concatenate(pieces, axis=1)
-    ups, downs = [], []
-    for source in (low_half, high_half):
-        for part in range(2):
-            at = SPLIT + part * D
-            ups.append(source[:, at : at + D].reshape(rows, count, 1, group))
-            at = SPLIT + units + part * D
-            downs.append(source[:, at : at + D])
-    grad_up = jnp.concatenate(ups, axis=2).reshape(rows, 2 * units)
-    grad_down = jnp.concatenate(downs, axis=0)
-
-    totals = totals + swap(after(totals, own))
+    totals = attention_sum[rows : rows + 6, :D].astype(F32) + attention_theirs[rows : rows + 6, :D].astype(F32)
     totals = jnp.where(first, totals[:3], totals[3:])
     return (
         outputs[None],

time: 439 us -> 412 us (0.938)
  local copies, waits for them, and re-layouts: 68.1 us -> 35.1 us
  other arithmetic: 25.5 us -> 10.2 us
  Pallas kernels: 107 us -> 122 us
  waiting for transfers between devices: 183 us -> 192 us
    pallas_call x4 -> x8, Pallas kernels: 55 us -> 93.7 us  [the longest x2 36.6 us: whole_block(): pl.pallas_call(partial(whole_block_kernel, tokens, images, units), grid_s...]
    ppermute x2 -> x4, waiting for transfers between devices: 0.01 us -> 14.8 us  [give(): return lax.ppermute(value, 'section', [(source, 1 - source)])]
    pallas_call x2 -> x1, Pallas kernels: 26.6 us -> 13.2 us  [feed_forward(): pl.pallas_call(partial(feed_forward_kernel, steps, len(pieces)), grid_spe...]
    unnamed x105 -> x97, local copies, waits for them, and re-layouts: 41.3 us -> 32.1 us
    squeeze x8 -> x0, local copies, waits for them, and re-layouts: 9.09 us -> none  [the longest x6 7.15 us: pick(): return lax.dynamic_index_in_dim(value, at, axis, keepdims=False)]
    pallas_call x2 -> x1, Pallas kernels: 17.7 us -> 8.9 us  [attention_forward(): pl.pallas_call(partial(attention_forward_kernel, tokens, len(pieces)), gr...]
    ppermute x15 -> x10, starting transfers between devices: 19 us -> 10.6 us  [relative(): lax.ppermute(value, 'dp', [(source, source ^ step) for source in range(co...]
    ppermute x7 -> x6, waiting for transfers between devices: 60.8 us -> 52.5 us  [swap(): return lax.ppermute(value, 'section', [(0, 1), (1, 0)])]
  transfers between devices with their start and end apart: 27 -> 23, of which waited for: 16 -> 12; matrix products, arithmetic and copies ran while one was open for 11% -> 4% of each run, Pallas kernels for 13% -> 22%
where the time goes in v3:
time: 412 us; the launch traced here: 405 us
  waiting for transfers between devices  192 us (47%)
  Pallas kernels  122 us (30%)
  local copies, waits for them, and re-layouts  35.1 us (9%)
  starting transfers between devices  30.9 us (8%)
  between operations  14.9 us (4%)
  other arithmetic  10.2 us (2%)
    all_gather x2, waiting for transfers between devices, on_device(): weights.append([lax.all_gather(shard, 'dp', axis=0, tiled=True)])  80.4 us
    ppermute x6, waiting for transfers between devices, swap(): return lax.ppermute(value, 'section', [(0, 1), (1, 0)])  52.5 us
    ppermute x10, waiting for transfers between devices, relative(): lax.ppermute(value, 'dp', [(source, source ^ step) for source in range(co...  44.8 us
    pallas_call x2, Pallas kernels, whole_block(): pl.pallas_call(partial(whole_block_kernel, tokens, images, units), grid_s...  36.6 us
    unnamed x97, local copies, waits for them, and re-layouts  32.1 us
    pallas_call x1, Pallas kernels, attention_back(): pl.pallas_call(partial(attention_back_kernel, images, count), grid_spec=p...  23.8 us
    pallas_call x1, Pallas kernels, feed_back(): pl.pallas_call(partial(feed_back_kernel, images, units, count), grid_spec...  16.5 us
    ppermute x4, waiting for transfers between devices, give(): return lax.ppermute(value, 'section', [(source, 1 - source)])  14.8 us
  transfers between devices with their start and end apart: 23, of which 12 were waited for; matrix products, arithmetic and copies ran while one was open for 4% of the time, Pallas kernels for 22%

profile of v3, /device:TPU:0, one launch (start us, length us, event | category | flops | bytes accessed | tf_op | source)
XLA Modules:
  0.0 405.4 jit_solution(3240832356540952702)
XLA Ops:
  7.3 1.0 copy-done.11
  8.3 1.0 copy-done.12
  9.3 0.9 copy-done.13
  10.2 0.9 copy-done.14
  11.1 0.9 pack.1
  11.9 3.0 collective-permute-start
  15.8 10.4 %collective-permute-done.1 = f32[3,768]{1,0:T(4,128)S(1)} collective-permute-done((f32[3,768]{1,0:T(4,128)S(1)}, f32[3,768]{1,0:T(4,128)S(1)}, u32[]{:S(2)}, u32[]{:S(2)}) %collective-permute-start.1) | collective-permute-done | bytes 9248 | tf_op jit(solution)/shard_map/ppermute | solution.py:1256
  26.2 1.0 broadcast_select_fusion.1
  27.3 71.9 %all-gather.3.cloned.1.call-done.refs_0_.w_ref.w_hbm = bf16[768,4992]{1,0:T(8,128)(2,1)} async-done(((bf16[48,4992]{1,0:T(8,128)(2,1)}), bf16[768,4992]{1,0:T(8,128)(2,1)}) %all-gather.3.cloned.1.call-update) | async-done | bytes 7667728 | tf_op jit(solution)/shard_map/all_gather | solution.py:1308
  99.3 1.4 copy.26
  101.5 3.2 copy-done.15
  104.7 8.9 %attention_forward.1 = (bf16[832,768]{1,0:T(8,128)(2,1)S(1)}, bf16[832,768]{1,0:T(8,128)(2,1)S(1)}, bf16[832,384]{1,0:T(8,128)(2,1)S(1)}, bf16[832,768]{1,0:T(8,...) custom-call(s32[2]{0:T(128)S(1)} %pad_add_fusion.place, ...), custom_call_target="tpu_custom_call" | custom-call | flops 2494562304 | bytes 10616832 | tf_op jit(solution)/shard_map/attention_forward/pallas_call | solution.py:141
  113.6 1.1 copy-done.22
  114.8 1.0 copy-done.24
  115.8 0.8 copy-done.26
  116.7 13.2 %feed_forward.1 = (bf16[832,1536]{1,0:T(8,128)(2,1)S(1)}, bf16[832,1536]{1,0:T(8,128)(2,1)S(1)}, bf16[832,768]{1,0:T(8,128)(2,1)S(1)}) custom-call(s32[2]{0:T(128)S(1)} %pad_add_fusion.place, bf16[768,4992]{1,0:T(8,128)(2,1)S(1)} %copy-done.16, bf16[832,768]{1,0:T(8,128)(2,1)S(1)} %get-tuple-element.64.refs_1_.normed_hbm, ...), custom_call_target="tpu_custom_call" | custom-call | flops 3925868544 | bytes 13664256 | tf_op jit(solution)/shard_map/feed_forward/pallas_call | solution.py:246
  130.0 1.5 copy-done.32
  131.4 1.5 collective-permute-start.2
  133.0 1.2 pad.8.clone
  134.3 27.3 %collective-permute-done.2 = bf16[832,768]{1,0:T(8,128)(2,1)S(1)} collective-permute-done((bf16[832,768]{1,0:T(8,128)(2,1)S(1)}, bf16[832,768]{1,0:T(8,128)(2,1)S(1)}, u32[]{:S(2)}, u32[]{:S(2)}) %collective-permute-start.2) | collective-permute-done | bytes 1277984 | tf_op jit(solution)/shard_map/ppermute | solution.py:1256
  162.3 8.4 %all-gather.5.cloned.1.call-done.w_ref = bf16[768,4992]{1,0:T(8,128)(2,1)} async-done(((bf16[48,4992]{1,0:T(8,128)(2,1)}), bf16[768,4992]{1,0:T(8,128)(2,1)}) %all-gather.5.cloned.1.call-update) | async-done | bytes 7667728 | tf_op jit(solution)/shard_map/all_gather | solution.py:1308
  170.7 1.3 copy-done.3
  172.0 3.2 copy-done.17
  175.2 18.5 %whole_block.2 = (bf16[416,768]{1,0:T(8,128)(2,1)S(1)}, bf16[416,768]{1,0:T(8,128)(2,1)S(1)}, f32[8,768]{1,0:T(8,128)S(1)}, bf16[416,768]{1,0:T(8,128)(2,1)S(1)}...) custom-call(s32[4]{0:T(128)S(1)} %pad_add_fusion.1.place, ...), custom_call_target="tpu_custom_call" | custom-call | flops 5888802816 | bytes 14057472 | tf_op jit(solution)/shard_map/whole_block/pallas_call | solution.py:765
  193.7 1.5 collective-permute-start.3
  195.2 1.0 pad_slice_fusion
  196.4 18.2 %whole_block.3 = (bf16[416,768]{1,0:T(8,128)(2,1)S(1)}, bf16[416,768]{1,0:T(8,128)(2,1)S(1)}, f32[8,768]{1,0:T(8,128)S(1)}, bf16[416,768]{1,0:T(8,128)(2,1)S(1)}...) custom-call(s32[4]{0:T(128)S(1)} %pad_add_fusion.1.place, ...), custom_call_target="tpu_custom_call" | custom-call | flops 5888802816 | bytes 14057472 | tf_op jit(solution)/shard_map/whole_block/pallas_call | solution.py:765
  215.4 0.8 copy-done.9
  216.2 0.9 copy-done.40
  217.1 12.7 %weight_grads.1 = bf16[768,4992]{1,0:T(8,128)(2,1)S(1)} custom-call(s32[4]{0:T(128)S(1)} %pad_add_fusion.1.place, bf16[416,1536]{1,0:T(8,128)(2,1)S(1)} %get-tuple-element.70.refs_0_, bf16[416,768]{1,0:T(8,128)(2,1)S(1)} %bitcast.30, bf16[416,768]{1,0:T(8,128)(2,1)S(1)} %get-tuple-element.71.refs_2_, bf16[416,1536]{1,0:T(8,128)(2,1)S(1)} %get-tuple-element.72.refs_3_, ...), custom_call_target="tpu_custom_call" | custom-call | flops 5888802816 | bytes 19169280 | tf_op jit(solution)/shard_map/weight_grads/pallas_call | solution.py:705
  229.8 3.0 copy-done.2
  233.5 1.2 pad_maximum_fusion.mine_ref
  234.7 14.7 %collective-permute-done.4 = bf16[416,768]{1,0:T(8,128)(2,1)S(1)} collective-permute-done((bf16[416,768]{1,0:T(8,128)(2,1)}, bf16[416,768]{1,0:T(8,128)(2,1)S(1)}, u32[]{:S(2)}, u32[]{:S(2)}) %collective-permute-start.4) | collective-permute-done | bytes 639008 | tf_op jit(solution)/shard_map/ppermute | solution.py:1256
  249.5 2.1 norm_backward.2.g_hbm.g_ref
  252.0 1.3 copy-done.33
  253.3 16.5 %feed_back.1 = (bf16[832,768]{1,0:T(8,128)(2,1)S(1)}, bf16[384,3072]{1,0:T(8,128)(2,1)S(1)}, bf16[384,3072]{1,0:T(8,128)(2,1)S(1)}) custom-call(s32[4]{0:T(128)S(1)} %pad_add_fusion.1.place, bf16[768,4992]{1,0:T(8,128)(2,1)} %all-gather.3.cloned.1.call-done.refs_0_.w_ref.w_hbm, bf16[832,768]{1,0:T(8,128)(2,1)S(1)} %norm_backward.2.g_hbm.g_ref, ...), custom_call_target="tpu_custom_call" | custom-call | flops 7851737088 | bytes 18382848 | tf_op jit(solution)/shard_map/feed_back/pallas_call | solution.py:895
  269.9 4.5 %collective-permute-done.5 = bf16[384,3072]{1,0:T(8,128)(2,1)S(1)} collective-permute-done((bf16[384,3072]{1,0:T(8,128)(2,1)S(1)}, bf16[384,3072]{1,0:T(8,128)(2,1)S(1)}, u32[]{:S(2)}, u32[]{:S(2)}) %collective-permute-start.5) | collective-permute-done | bytes 2359328 | tf_op jit(solution)/shard_map/ppermute | solution.py:1219
  274.4 0.9 add_convert_fusion
  277.4 23.8 %attention_back.1 = (bf16[832,768]{1,0:T(8,128)(2,1)}, bf16[400,1920]{1,0:T(8,128)(2,1)S(1)}, bf16[400,1920]{1,0:T(8,128)(2,1)S(1)}) custom-call(s32[4]{0:T(128)S(1)} %pad_add_fusion.1.place, bf16[768,4992]{1,0:T(8,128)(2,1)} %all-gather.3.cloned.1.call-done.refs_0_.w_ref.w_hbm, bf16[832,768]{1,0:T(8,128)(2,1)S(1)} %norm_backward.2.g_hbm.g_ref, ...), custom_call_target="tpu_custom_call" | custom-call | flops 4989124608 | bytes 16121856 | tf_op jit(solution)/shard_map/attention_back/pallas_call | solution.py:1047
  301.3 7.9 %collective-permute-done.7 = bf16[192,3072]{1,0:T(8,128)(2,1)S(1)} collective-permute-done((bf16[192,3072]{1,0:T(8,128)(2,1)S(1)}, bf16[192,3072]{1,0:T(8,128)(2,1)S(1)}, u32[]{:S(2)}, u32[]{:S(2)}) %collective-permute-start.7) | collective-permute-done | bytes 1179680 | tf_op jit(solution)/shard_map/ppermute | solution.py:1219
  309.7 3.3 collective-permute-done.8
  314.7 1.3 collective-permute-start.14
  316.0 5.7 %collective-permute-start.6 = (bf16[832,768]{1,0:T(8,128)(2,1)S(1)}, bf16[832,768]{1,0:T(8,128)(2,1)S(1)}, u32[]{:S(2)}, u32[]{:S(2)}) collective-permute-start(bf16[832,768]{1,0:T(8,128)(2,1)S(1)} %constant_dynamic-update-slice_fusion), channel_id=1, source_target_pairs={{0,16},{1,17},{2,18},{3,19},{4,20},{5,21},{6,22},{7,23},{8,24},{9,... | collective-permute-start | bytes 3833864 | tf_op jit(solution)/shard_map/ppermute | solution.py:1259
  321.8 3.2 collective-permute-start.12
  325.0 13.4 %collective-permute-done.9 = bf16[208,1920]{1,0:T(8,128)(2,1)S(1)} collective-permute-done((bf16[208,1920]{1,0:T(8,128)(2,1)S(1)}, bf16[208,1920]{1,0:T(8,128)(2,1)S(1)}, u32[]{:S(2)}, u32[]{:S(2)}) %collective-permute-start.9) | collective-permute-done | bytes 798752 | tf_op jit(solution)/shard_map/ppermute | solution.py:1219
  338.4 1.5 collective-permute-start.10
  340.2 0.9 pad_maximum_fusion.5
  341.1 7.8 %collective-permute-done.6 = bf16[832,768]{1,0:T(8,128)(2,1)S(1)} collective-permute-done((bf16[832,768]{1,0:T(8,128)(2,1)S(1)}, bf16[832,768]{1,0:T(8,128)(2,1)S(1)}, u32[]{:S(2)}, u32[]{:S(2)}) %collective-permute-start.6) | collective-permute-done | bytes 1277984 | tf_op jit(solution)/shard_map/ppermute | solution.py:1259
  348.9 1.1 copy-done.38
  350.0 3.2 collective-permute-start.17
  353.2 1.4 collective-permute-start.16
  354.6 15.6 %collective-permute-done.11 = bf16[48,3072]{1,0:T(8,128)(2,1)S(1)} collective-permute-done((bf16[48,3072]{1,0:T(8,128)(2,1)S(1)}, bf16[48,3072]{1,0:T(8,128)(2,1)S(1)}, u32[]{:S(2)}, u32[]{:S(2)}) %collective-permute-start.11) | collective-permute-done | bytes 294944 | tf_op jit(solution)/shard_map/ppermute | solution.py:1219
  371.0 2.9 collective-permute-start.13
  373.8 1.3 add_convert_fusion.6.sum_ref
  375.1 1.3 collective-permute-start.19
  376.4 7.0 %collective-permute-done.13.second_arrived_ref = bf16[48,4992]{1,0:T(8,128)(2,1)S(1)} collective-permute-done((bf16[48,4992]{1,0:T(8,128)(2,1)}, bf16[48,4992]{1,0:T(8,128)(2,1)S(1)}, u32[]{:S(2)}, u32[]{:S(2)}) %collective-permute-start.13) | collective-permute-done | bytes 479264 | tf_op jit(solution)/shard_map/ppermute | solution.py:1259
  383.4 1.3 add_convert_fusion.7.sum_ref
  384.8 2.4 collective-permute-start.18
  387.2 3.8 norm_backward.3
  391.0 1.0 fusion
  392.1 1.5 copy.31
  393.7 1.5 copy.30
  395.1 1.9 finish_feed.1
  397.0 1.4 finish_attention.1
  (136 shorter events, 10.3 us)
Async XLA Ops:
  7.2 92.0 %all-gather.3.cloned.1.call-start = ((), (), s32[]{:S(2)}) async-start(), calls=%async_computation.1 | async-start | bytes 8146944 | tf_op jit(solution)/shard_map/all_gather | solution.py:1308
  7.3 1.0 copy-start.11
  8.3 1.0 copy-start.12
  9.3 0.9 copy-start.13
  10.2 0.9 copy-start.14
  11.9 14.2 %collective-permute-start = (bf16[48,4992]{1,0:T(8,128)(2,1)S(1)}, bf16[48,4992]{1,0:T(8,128)(2,1)S(1)}, u32[]{:S(2)}, u32[]{:S(2)}) collective-permute-start(bf16[48,4992]{1,0:T(8,128)(2,1)S(1)} %get-tuple-element.62), channel_id=1, source_target_pairs={{0,16},{16,0},{1,17},{17,1},{2,18},{18,2},{3,19},{19,3},{4,20},{20... | collective-permute-start | bytes 1437704 | tf_op jit(solution)/shard_map/ppermute | solution.py:1256
  15.7 10.5 %collective-permute-start.1 = (f32[3,768]{1,0:T(4,128)S(1)}, f32[3,768]{1,0:T(4,128)S(1)}, u32[]{:S(2)}, u32[]{:S(2)}) collective-permute-start(f32[3,768]{1,0:T(4,128)S(1)} %pad_maximum_fusion.6), channel_id=1, source_target_pairs={{0,16},{16,0},{1,17},{17,1},{2,18},{18,2},{3,19},{19,3},{4,20},{20... | collective-permute-start | bytes 27656 | tf_op jit(solution)/shard_map/ppermute | solution.py:1256
  27.2 143.5 %all-gather.5.cloned.1.call-start = ((), (), s32[]{:S(2)}) async-start(), calls=%async_computation.2 | async-start | bytes 8146944 | tf_op jit(solution)/shard_map/all_gather | solution.py:1308
  99.2 271.7 %reduce-scatter.2.cloned.1.call-start = ((), (), s32[]{:S(2)}) async-start(), calls=%async_computation.3 | async-start | bytes 8146944 | tf_op jit(solution)/shard_map/reduce_scatter | solution.py:1331
  101.5 3.2 copy-start.15
  104.7 12.0 %copy-start.16 = (bf16[768,4992]{1,0:T(8,128)(2,1)S(1)}, bf16[768,4992]{1,0:T(8,128)(2,1)}, u32[]{:S(2)}) copy-start(bf16[768,4992]{1,0:T(8,128)(2,1)} %all-gather.3.cloned.1.call-done.refs_0_.w_ref.w_hbm) | copy-start | bytes 23003140
  113.6 1.2 copy-start.22
  114.8 1.0 copy-start.24
  115.8 0.9 copy-start.26
  116.7 13.3 %copy-start.18 = (bf16[4,6,208,208]{3,2,1,0:T(8,128)(2,1)}, bf16[4,6,208,208]{3,2,1,0:T(8,128)(2,1)S(1)}, u32[]{:S(2)}) copy-start(bf16[4,6,208,208]{3,2,1,0:T(8,128)(2,1)S(1)} %get-tuple-element.92.pt_hbm) | copy-start | bytes 6230020
  116.7 13.3 %copy-start.20 = (bf16[832,768]{1,0:T(8,128)(2,1)}, bf16[832,768]{1,0:T(8,128)(2,1)S(1)}, u32[]{:S(2)}) copy-start(bf16[832,768]{1,0:T(8,128)(2,1)S(1)} %get-tuple-element.64.refs_1_.normed_hbm) | copy-start | bytes 3833860
  116.7 13.3 %copy-start.28 = (bf16[832,384]{1,0:T(8,128)(2,1)}, bf16[832,384]{1,0:T(8,128)(2,1)S(1)}, u32[]{:S(2)}) copy-start(bf16[832,384]{1,0:T(8,128)(2,1)S(1)} %get-tuple-element.94.mixed_hbm) | copy-start | bytes 1916932
  116.7 16.2 %copy-start.34 = (bf16[4,196,768]{2,0,1:T(4,128)(2,1)S(1)}, bf16[4,196,768]{2,0,1:T(4,128)(2,1)}, u32[]{:S(2)}) copy-start(bf16[4,196,768]{2,0,1:T(4,128)(2,1)} %param.10) | copy-start | bytes 3612676
  130.0 1.5 copy-start.32
  131.4 2.8 copy-start.30
  131.4 30.2 %collective-permute-start.2 = (bf16[832,768]{1,0:T(8,128)(2,1)S(1)}, bf16[832,768]{1,0:T(8,128)(2,1)S(1)}, u32[]{:S(2)}, u32[]{:S(2)}) collective-permute-start(bf16[832,768]{1,0:T(8,128)(2,1)S(1)} %get-tuple-element.66), channel_id=1, source_target_pairs={{0,16},{16,0},{1,17},{17,1},{2,18},{18,2},{3,19},{19,3},{4,20},{20... | collective-permute-start | bytes 3833864 | tf_op jit(solution)/shard_map/ppermute | solution.py:1256
  170.7 1.3 copy-start.3
  172.0 3.2 copy-start.17
  175.2 20.0 %copy-start.35 = (bf16[4,196,768]{2,0,1:T(4,128)(2,1)S(1)}, bf16[4,196,768]{2,0,1:T(4,128)(2,1)}, u32[]{:S(2)}) copy-start(bf16[4,196,768]{2,0,1:T(4,128)(2,1)} %param.10) | copy-start | bytes 3612676
  193.7 2.6 copy-start.7
  193.7 22.5 %collective-permute-start.3 = (bf16[416,768]{1,0:T(8,128)(2,1)S(1)}, bf16[416,768]{1,0:T(8,128)(2,1)S(1)}, u32[]{:S(2)}, u32[]{:S(2)}) collective-permute-start(bf16[416,768]{1,0:T(8,128)(2,1)S(1)} %get-tuple-element.76), channel_id=1, source_target_pairs={{0,16},{16,0},{1,17},{17,1},{2,18},{18,2},{3,19},{19,3},{4,20},{20... | collective-permute-start | bytes 1916936 | tf_op jit(solution)/shard_map/ppermute | solution.py:1256
  214.6 0.8 copy-start.6
  216.2 0.9 copy-start.40
  229.8 3.0 copy-start.2
  232.8 16.6 %copy-start.41 = (bf16[416,768]{1,0:T(8,128)(2,1)S(1)}, bf16[416,768]{1,0:T(8,128)(2,1)}, u32[]{:S(2)}) copy-start(bf16[416,768]{1,0:T(8,128)(2,1)} %copy-done.40) | copy-start | bytes 1916932
  232.9 16.5 %collective-permute-start.4 = (bf16[416,768]{1,0:T(8,128)(2,1)}, bf16[416,768]{1,0:T(8,128)(2,1)S(1)}, u32[]{:S(2)}, u32[]{:S(2)}) collective-permute-start(bf16[416,768]{1,0:T(8,128)(2,1)} %copy-done.6), channel_id=1, source_target_pairs={{0,16},{16,0},{1,17},{17,1},{2,18},{18,2},{3,19},{19,3},{4,20},{20... | collective-permute-start | bytes 1916936 | tf_op jit(solution)/shard_map/ppermute | solution.py:1256
  234.7 14.8 %copy-start.4 = (bf16[4,208,768]{2,1,0:T(8,128)(2,1)S(1)}, bf16[4,208,768]{2,1,0:T(8,128)(2,1)}, u32[]{:S(2)}) copy-start(bf16[4,208,768]{2,1,0:T(8,128)(2,1)} %pad.8.clone) | copy-start | bytes 3833860
  249.5 2.2 copy-start.21
  249.5 2.5 copy-start.31
  249.5 3.8 copy-start.33
  251.7 24.5 %copy-start = (bf16[832,768]{1,0:T(8,128)(2,1)}, bf16[832,768]{1,0:T(8,128)(2,1)S(1)}, u32[]{:S(2)}) copy-start(bf16[832,768]{1,0:T(8,128)(2,1)S(1)} %norm_backward.2.g_hbm.g_ref) | copy-start | bytes 3833860
  269.8 4.6 %collective-permute-start.5 = (bf16[384,3072]{1,0:T(8,128)(2,1)S(1)}, bf16[384,3072]{1,0:T(8,128)(2,1)S(1)}, u32[]{:S(2)}, u32[]{:S(2)}) collective-permute-start(bf16[384,3072]{1,0:T(8,128)(2,1)S(1)} %get-tuple-element.87), channel_id=1, source_target_pairs={{0,1},{1,0},{2,3},{3,2},{4,5},{5,4},{6,7},{7,6},{8,9},{9,8},{10,11... | collective-permute-start | bytes 7077896 | tf_op jit(solution)/shard_map/ppermute | solution.py:1219
  274.4 1.8 copy-start.19
  274.4 2.1 copy-start.25
  274.4 2.2 copy-start.29
  275.3 2.0 copy-start.23
  275.3 2.1 copy-start.27
  275.4 33.8 %collective-permute-start.7 = (bf16[192,3072]{1,0:T(8,128)(2,1)S(1)}, bf16[192,3072]{1,0:T(8,128)(2,1)S(1)}, u32[]{:S(2)}, u32[]{:S(2)}) collective-permute-start(bf16[192,3072]{1,0:T(8,128)(2,1)S(1)} %slice.114), channel_id=1, source_target_pairs={{0,2},{1,3},{2,0},{3,1},{4,6},{5,7},{6,4},{7,5},{8,10},{9,11},{10,... | collective-permute-start | bytes 3538952 | tf_op jit(solution)/shard_map/ppermute | solution.py:1219
  301.3 8.4 %copy-start.8 = (bf16[416,768]{1,0:T(8,128)(2,1)S(1)}, bf16[416,768]{1,0:T(8,128)(2,1)}, u32[]{:S(2)}) copy-start(bf16[416,768]{1,0:T(8,128)(2,1)} %copy-done.7) | copy-start | bytes 1916932
  309.6 3.4 collective-permute-start.8
  313.4 1.3 copy-start.10
  313.5 24.9 %collective-permute-start.9 = (bf16[208,1920]{1,0:T(8,128)(2,1)S(1)}, bf16[208,1920]{1,0:T(8,128)(2,1)S(1)}, u32[]{:S(2)}, u32[]{:S(2)}) collective-permute-start(bf16[208,1920]{1,0:T(8,128)(2,1)S(1)} %slice.118), channel_id=1, source_target_pairs={{0,2},{1,3},{2,0},{3,1},{4,6},{5,7},{6,4},{7,5},{8,10},{9,11},{10,... | collective-permute-start | bytes 2396168 | tf_op jit(solution)/shard_map/ppermute | solution.py:1219
  314.7 25.4 %copy-start.36 = (bf16[832,768]{1,0:T(8,128)(2,1)}, bf16[832,768]{1,0:T(8,128)(2,1)S(1)}, u32[]{:S(2)}) copy-start(bf16[832,768]{1,0:T(8,128)(2,1)S(1)} %constant_dynamic-update-slice_fusion) | copy-start | bytes 3833860
  314.7 60.4 %collective-permute-start.14 = (bf16[832,768]{1,0:T(8,128)(2,1)}, bf16[832,768]{1,0:T(8,128)(2,1)}, u32[]{:S(2)}, u32[]{:S(2)}) collective-permute-start(bf16[832,768]{1,0:T(8,128)(2,1)} %get-tuple-element.105.mine_ref), channel_id=1, source_target_pairs={{16,0},{17,1},{18,2},{19,3},{20,4},{21,5},{22,6},{23,7},{24,8},{25... | collective-permute-start | bytes 3833864 | tf_op jit(solution)/shard_map/ppermute | solution.py:1259
  316.0 32.9 %collective-permute-start.6 = (bf16[832,768]{1,0:T(8,128)(2,1)S(1)}, bf16[832,768]{1,0:T(8,128)(2,1)S(1)}, u32[]{:S(2)}, u32[]{:S(2)}) collective-permute-start(bf16[832,768]{1,0:T(8,128)(2,1)S(1)} %constant_dynamic-update-slice_fusion), channel_id=1, source_target_pairs={{0,16},{1,17},{2,18},{3,19},{4,20},{5,21},{6,22},{7,23},{8,24},{9,... | collective-permute-start | bytes 3833864 | tf_op jit(solution)/shard_map/ppermute | solution.py:1259
  321.8 31.4 %collective-permute-start.12 = (bf16[48,3072]{1,0:T(8,128)(2,1)S(1)}, bf16[48,3072]{1,0:T(8,128)(2,1)S(1)}, u32[]{:S(2)}, u32[]{:S(2)}) collective-permute-start(bf16[48,3072]{1,0:T(8,128)(2,1)S(1)} %get-tuple-element.120), channel_id=1, source_target_pairs={{0,12},{1,13},{2,14},{3,15},{4,8},{5,9},{6,10},{7,11},{8,4},{9,5},... | collective-permute-start | bytes 884744 | tf_op jit(solution)/shard_map/ppermute | solution.py:1219
  325.0 45.2 %collective-permute-start.11 = (bf16[48,3072]{1,0:T(8,128)(2,1)S(1)}, bf16[48,3072]{1,0:T(8,128)(2,1)S(1)}, u32[]{:S(2)}, u32[]{:S(2)}) collective-permute-start(bf16[48,3072]{1,0:T(8,128)(2,1)S(1)} %get-tuple-element.121), channel_id=1, source_target_pairs={{0,8},{1,9},{2,10},{3,11},{4,12},{5,13},{6,14},{7,15},{8,0},{9,1},... | collective-permute-start | bytes 884744 | tf_op jit(solution)/shard_map/ppermute | solution.py:1219
  338.4 32.6 %collective-permute-start.10 = (bf16[48,3072]{1,0:T(8,128)(2,1)S(1)}, bf16[48,3072]{1,0:T(8,128)(2,1)}, u32[]{:S(2)}, u32[]{:S(2)}) collective-permute-start(bf16[48,3072]{1,0:T(8,128)(2,1)S(1)} %get-tuple-element.122), channel_id=1, source_target_pairs={{0,4},{1,5},{2,6},{3,7},{4,0},{5,1},{6,2},{7,3},{8,12},{9,13},{10,... | collective-permute-start | bytes 884744 | tf_op jit(solution)/shard_map/ppermute | solution.py:1219
  348.9 1.1 copy-start.38
  350.0 33.5 %collective-permute-start.17 = (bf16[64,1920]{1,0:T(8,128)(2,1)}, bf16[64,1920]{1,0:T(8,128)(2,1)}, u32[]{:S(2)}, u32[]{:S(2)}) collective-permute-start(bf16[64,1920]{1,0:T(8,128)(2,1)} %get-tuple-element.132), channel_id=1, source_target_pairs={{0,12},{1,13},{2,14},{3,15},{4,8},{5,9},{6,10},{7,11},{8,4},{9,5},... | collective-permute-start | bytes 737288 | tf_op jit(solution)/shard_map/ppermute | solution.py:1219
  353.2 30.2 %collective-permute-start.16 = (bf16[64,1920]{1,0:T(8,128)(2,1)}, bf16[64,1920]{1,0:T(8,128)(2,1)}, u32[]{:S(2)}, u32[]{:S(2)}) collective-permute-start(bf16[64,1920]{1,0:T(8,128)(2,1)} %get-tuple-element.131), channel_id=1, source_target_pairs={{0,8},{1,9},{2,10},{3,11},{4,12},{5,13},{6,14},{7,15},{8,0},{9,1},... | collective-permute-start | bytes 737288 | tf_op jit(solution)/shard_map/ppermute | solution.py:1219
  371.0 12.5 %collective-permute-start.15 = (bf16[64,1920]{1,0:T(8,128)(2,1)}, bf16[64,1920]{1,0:T(8,128)(2,1)}, u32[]{:S(2)}, u32[]{:S(2)}) collective-permute-start(bf16[64,1920]{1,0:T(8,128)(2,1)} %get-tuple-element.130), channel_id=1, source_target_pairs={{0,4},{1,5},{2,6},{3,7},{4,0},{5,1},{6,2},{7,3},{8,12},{9,13},{10,... | collective-permute-start | bytes 737288 | tf_op jit(solution)/shard_map/ppermute | solution.py:1219
  371.0 16.3 %copy-start.1 = (bf16[832,768]{1,0:T(8,128)(2,1)S(1)}, bf16[832,768]{1,0:T(8,128)(2,1)}, u32[]{:S(2)}) copy-start(bf16[832,768]{1,0:T(8,128)(2,1)} %copy-done) | copy-start | bytes 3833860
  371.0 12.4 %collective-permute-start.13 = (bf16[48,4992]{1,0:T(8,128)(2,1)}, bf16[48,4992]{1,0:T(8,128)(2,1)S(1)}, u32[]{:S(2)}, u32[]{:S(2)}) collective-permute-start(bf16[48,4992]{1,0:T(8,128)(2,1)} %reduce-scatter.2.cloned.1.call-done.second_ref), channel_id=1, source_target_pairs={{0,16},{1,17},{2,18},{3,19},{4,20},{5,21},{6,22},{7,23},{8,24},{9,... | collective-permute-start | bytes 1437704 | tf_op jit(solution)/shard_map/ppermute | solution.py:1259
  375.1 20.0 %collective-permute-start.19 = (bf16[48,3072]{1,0:T(8,128)(2,1)S(1)}, bf16[48,3072]{1,0:T(8,128)(2,1)S(1)}, u32[]{:S(2)}, u32[]{:S(2)}) collective-permute-start(bf16[48,3072]{1,0:T(8,128)(2,1)S(1)} %add_convert_fusion.6.sum_ref), channel_id=1, source_target_pairs={{16,0},{17,1},{18,2},{19,3},{20,4},{21,5},{22,6},{23,7},{24,8},{25... | collective-permute-start | bytes 884744 | tf_op jit(solution)/shard_map/ppermute | solution.py:1259
  384.8 6.2 %copy-start.37 = (bf16[832,768]{1,0:T(8,128)(2,1)S(1)}, bf16[832,768]{1,0:T(8,128)(2,1)}, u32[]{:S(2)}) copy-start(bf16[832,768]{1,0:T(8,128)(2,1)} %copy-done.36) | copy-start | bytes 3833860
  384.8 6.2 %copy-start.39 = (bf16[832,768]{1,0:T(8,128)(2,1)S(1)}, bf16[832,768]{1,0:T(8,128)(2,1)}, u32[]{:S(2)}) copy-start(bf16[832,768]{1,0:T(8,128)(2,1)} %copy-done.38) | copy-start | bytes 3833860
  384.8 12.2 %collective-permute-start.18 = (bf16[64,1920]{1,0:T(8,128)(2,1)S(1)}, bf16[64,1920]{1,0:T(8,128)(2,1)S(1)}, u32[]{:S(2)}, u32[]{:S(2)}) collective-permute-start(bf16[64,1920]{1,0:T(8,128)(2,1)S(1)} %add_convert_fusion.7.sum_ref), channel_id=1, source_target_pairs={{0,16},{16,0},{1,17},{17,1},{2,18},{18,2},{3,19},{19,3},{4,20},{20... | collective-permute-start | bytes 737288 | tf_op jit(solution)/shard_map/ppermute | solution.py:1256
  393.6 1.5 copy-start.5
  (5 other events, 3.6 us)
Sparse Core Ops, SparseCore 0:
  27.3 71.8 all-gather.2
  102.0 68.7 all-gather.4
  233.0 119.4 reduce-scatter.1
